TPU v7x, 32 devices: a whole 2x2x4 slice. The times are simulated.
32 devices in a mesh: seq: 4 (over x, core), clip: 8 (over z, y).
Axes of the slice: x: 2, y: 2, z: 4, core: 2. Of those that a mesh axis runs over, the one named last changes fastest.
Arguments:
- patches: bfloat16 [64, 8, 64, 768], P('clip', None, 'seq'), may hold values from -6 to 6
- mask_index: int32 [64, 450], P('clip'), may hold values from 0 to 511, as said below
- mask_count: int32 [64], P('clip'), may hold values from 100 to 450, as said below
- cotangent: bfloat16 [64, 8, 64, 768], P('clip', None, 'seq'), may hold values from -6 to 6
- w_qkv: bfloat16 [768, 2304], P(('seq', 'clip')), may hold values from -0.3125 to 0.3125
- w_out: bfloat16 [768, 768], P(('seq', 'clip')), may hold values from -0.4375 to 0.4375
- mask_embed: bfloat16 [768], P(('seq', 'clip')), may hold values from -5 to 5
- gains: bfloat16 [2, 768], P(None, ('seq', 'clip')), may hold values from 0.5 to 1.5
- biases: bfloat16 [6, 768], P(None, ('seq', 'clip')), may hold values from -0.5 to 0.5
- w_up: bfloat16 [768, 3072], P(('seq', 'clip')), may hold values from -0.21875 to 0.21875
- w_down: bfloat16 [3072, 768], P(('seq', 'clip')), may hold values from -0.109375 to 0.109375
- up_bias: bfloat16 [3072], P(('seq', 'clip')), may hold values from -2.5 to 2.5
- avg_qkv: float32 [768, 2304], P(('seq', 'clip')), may hold values from -0.3125 to 0.3125
- avg_out: float32 [768, 768], P(('seq', 'clip')), may hold values from -0.4375 to 0.4375
- avg_mask: float32 [768], P(('seq', 'clip')), may hold values from -5 to 5
- avg_gains: float32 [2, 768], P(None, ('seq', 'clip')), may hold values from -1 to 1
- avg_biases: float32 [6, 768], P(None, ('seq', 'clip')), may hold values from -0.5 to 0.5
- avg_up: float32 [768, 3072], P(('seq', 'clip')), may hold values from -0.21875 to 0.21875
- avg_down: float32 [3072, 768], P(('seq', 'clip')), may hold values from -0.109375 to 0.109375
- avg_up_bias: float32 [3072], P(('seq', 'clip')), may hold values from -2.5 to 2.5
Outputs:
- activations: bfloat16 [64, 8, 64, 768], P('clip', None, 'seq')
- input_grad: bfloat16 [64, 8, 64, 768], P('clip', None, 'seq')
- grad_qkv: float32 [768, 2304], P(('seq', 'clip'))
- grad_out: float32 [768, 768], P(('seq', 'clip'))
- grad_mask: float32 [768], P(('seq', 'clip'))
- grad_gains: float32 [2, 768], P(None, ('seq', 'clip'))
- grad_biases: float32 [6, 768], P(None, ('seq', 'clip'))
- grad_up: float32 [768, 3072], P(('seq', 'clip'))
- grad_down: float32 [3072, 768], P(('seq', 'clip'))
- grad_up_bias: float32 [3072], P(('seq', 'clip'))
- new_qkv: float32 [768, 2304], P(('seq', 'clip'))
- new_out: float32 [768, 768], P(('seq', 'clip'))
- new_mask: float32 [768], P(('seq', 'clip'))
- new_gains: float32 [2, 768], P(None, ('seq', 'clip'))
- new_biases: float32 [6, 768], P(None, ('seq', 'clip'))
- new_up: float32 [768, 3072], P(('seq', 'clip'))
- new_down: float32 [3072, 768], P(('seq', 'clip'))
- new_up_bias: float32 [3072], P(('seq', 'clip'))
Inputs may be any that keep to these rules, and one draw needn't show every extreme that they name: `mask_index`: each row holds 450 different patch numbers of its clip; only its first mask_count entries are masked, the others are to be ignored. `mask_count`: some clip has exactly 450 masked patches in every draw.
All inputs are finite; a program needn't handle non-finite values.
Results may differ from a plain program's by a relative error of at most 0.015.
Values may be sent and summed in bfloat16 or wider, within the bound.
No kernel may reach another device: no remote copies, remote signals or barrier semaphores. Data moves between devices by JAX's collectives and lax.ppermute only.
A program may use at most 192 MiB of HBM per device.

v0:
```python
from functools import partial
import math

import jax
import jax.numpy as jnp
from jax import lax
from jax.sharding import PartitionSpec as P

H = 12


norm_eps = 1e-06


def layer_norm(hidden, gain_row, shift_row):
    center = hidden - jnp.mean(hidden, axis=-1, keepdims=True)
    spread = jnp.mean(center * center, axis=-1, keepdims=True)
    return center * lax.rsqrt(spread + norm_eps) * gain_row + shift_row


def exact_gelu(upper_rows):
    return jax.nn.gelu(upper_rows, approximate=False)


def row_product(left_side, right_side):
    return lax.dot_general(
        left_side, right_side, (((0,), (0,)), ((), ())), preferred_element_type=jnp.float32
    )


def back_product(left_side, right_side):
    return lax.dot_general(
        left_side, right_side, (((1,), (1,)), ((), ())), preferred_element_type=jnp.float32
    )


def split_heads(array_rows, head_count):
    clip_count, row_count, model_width = array_rows.shape
    return array_rows.reshape(clip_count, row_count, head_count, model_width // head_count)


def make_groups(array_rows, group_size):
    return array_rows.reshape(
        (array_rows.shape[0] // group_size, group_size) + array_rows.shape[1:]
    )


def attend_forward(operands, head_count, score_scale):
    queries, keys_all, values_all = operands
    clip_count, query_rows, model_width = queries.shape
    query_h = split_heads(queries, head_count)
    key_h = split_heads(keys_all, head_count)
    value_h = split_heads(values_all, head_count)
    scores = (
        jnp.einsum("cqhd,ckhd->chqk", query_h, key_h, preferred_element_type=jnp.float32)
        * score_scale
    )
    row_max = jnp.max(scores, axis=-1, keepdims=True)
    shifted = jnp.exp(scores - row_max)
    row_sum = jnp.sum(shifted, axis=-1, keepdims=True)
    attn_prob = shifted / row_sum
    mixed_rows = jnp.einsum(
        "chqk,ckhd->cqhd",
        attn_prob.astype(jnp.bfloat16),
        value_h,
        preferred_element_type=jnp.float32,
    )
    log_total = (row_max + jnp.log(row_sum))[..., 0]
    return (mixed_rows.reshape(clip_count, query_rows, model_width).astype(jnp.bfloat16), log_total)


def attend_backward(operands, head_count, score_scale):
    queries, keys_all, values_all, grad_mixed, log_total = operands
    clip_count, query_rows, model_width = queries.shape
    key_rows = keys_all.shape[1]
    query_h = split_heads(queries, head_count)
    key_h = split_heads(keys_all, head_count)
    value_h = split_heads(values_all, head_count)
    grad_heads = split_heads(grad_mixed, head_count)
    scores = (
        jnp.einsum("cqhd,ckhd->chqk", query_h, key_h, preferred_element_type=jnp.float32)
        * score_scale
    )
    attn_prob = jnp.exp(scores - log_total[..., None])
    grad_prob = jnp.einsum(
        "cqhd,ckhd->chqk", grad_heads, value_h, preferred_element_type=jnp.float32
    )
    inner_sum = jnp.sum(grad_prob * attn_prob, axis=-1, keepdims=True)
    grad_scores = (attn_prob * (grad_prob - inner_sum)).astype(jnp.bfloat16)
    grad_query = (
        jnp.einsum("chqk,ckhd->cqhd", grad_scores, key_h, preferred_element_type=jnp.float32)
        * score_scale
    )
    grad_key = (
        jnp.einsum("chqk,cqhd->ckhd", grad_scores, query_h, preferred_element_type=jnp.float32)
        * score_scale
    )
    grad_value = jnp.einsum(
        "chqk,cqhd->ckhd",
        attn_prob.astype(jnp.bfloat16),
        grad_heads,
        preferred_element_type=jnp.float32,
    )
    grad_query = grad_query.reshape(clip_count, query_rows, model_width).astype(jnp.bfloat16)
    grad_key = grad_key.reshape(clip_count, key_rows, model_width)
    grad_value = grad_value.reshape(clip_count, key_rows, model_width)
    return (grad_query, grad_key, grad_value)


def body(
    patches,
    mask_index,
    mask_count,
    cotangent,
    w_qkv,
    w_out,
    mask_embed,
    gains,
    biases,
    w_up,
    w_down,
    up_bias,
    avg_qkv,
    avg_out,
    avg_mask,
    avg_gains,
    avg_biases,
    avg_up,
    avg_down,
    avg_up_bias,
):
    clip_count, freq_rows, time_local, model_width = patches.shape
    seq_size = lax.axis_size("seq")
    time_total = time_local * seq_size
    length = freq_rows * time_total
    local_len = freq_rows * time_local
    row_total = clip_count * local_len
    head_count = H
    score_scale = 1.0 / math.sqrt(model_width // head_count)
    forward_fn = partial(attend_forward, head_count=head_count, score_scale=score_scale)
    backward_fn = partial(attend_backward, head_count=head_count, score_scale=score_scale)
    gathered = (
        lax.all_gather(w_qkv, ("seq", "clip"), axis=0, tiled=True),
        lax.all_gather(w_out, ("seq", "clip"), axis=0, tiled=True),
        lax.all_gather(mask_embed, ("seq", "clip"), axis=0, tiled=True),
        lax.all_gather(gains, ("seq", "clip"), axis=1, tiled=True),
        lax.all_gather(biases, ("seq", "clip"), axis=1, tiled=True),
        lax.all_gather(w_up, ("seq", "clip"), axis=0, tiled=True),
        lax.all_gather(w_down, ("seq", "clip"), axis=0, tiled=True),
        lax.all_gather(up_bias, ("seq", "clip"), axis=0, tiled=True),
    )
    full_qkv, full_out, full_mask, full_gains, full_biases, full_up, full_down, full_up_bias = (
        gathered
    )
    gain_rows = full_gains.astype(jnp.float32)
    bias_rows = full_biases.astype(jnp.float32)
    mask_vector = full_mask.astype(jnp.float32)
    up_shift = full_up_bias.astype(jnp.float32)
    freq_ids = lax.broadcasted_iota(jnp.int32, (freq_rows, time_local), 0)
    time_ids = (
        lax.broadcasted_iota(jnp.int32, (freq_rows, time_local), 1)
        + lax.axis_index("seq") * time_local
    )
    positions = (freq_ids * time_total + time_ids).reshape(local_len)
    slot_ids = lax.broadcasted_iota(jnp.int32, mask_index.shape, 1)
    slot_live = slot_ids < mask_count[:, None]
    slot_hits = (mask_index[:, :, None] == positions[None, None, :]) & slot_live[:, :, None]
    masked = jnp.any(slot_hits, axis=1).reshape(row_total, 1)
    fresh_rows = patches.reshape(row_total, model_width).astype(jnp.float32)
    start_rows = jnp.where(masked, mask_vector, fresh_rows)
    normed_one, norm_pull_one = jax.vjp(layer_norm, start_rows, gain_rows[0], bias_rows[0])
    normed_low = normed_one.astype(jnp.bfloat16)
    joined = jnp.dot(normed_low, full_qkv, preferred_element_type=jnp.float32)
    queries = (joined[:, :model_width] + bias_rows[1]).astype(jnp.bfloat16)
    keys_loc = joined[:, model_width : 2 * model_width].astype(jnp.bfloat16)
    values_loc = (joined[:, 2 * model_width :] + bias_rows[2]).astype(jnp.bfloat16)
    grid_shape = (clip_count, freq_rows, time_local, model_width)
    key_grid = keys_loc.reshape(grid_shape)
    value_grid = values_loc.reshape(grid_shape)
    key_all, value_all = (
        lax.all_gather(key_grid, "seq", axis=2, tiled=True),
        lax.all_gather(value_grid, "seq", axis=2, tiled=True),
    )
    group_size = math.gcd(clip_count, max(1, 512 // local_len))
    query_groups = make_groups(queries.reshape(clip_count, local_len, model_width), group_size)
    key_groups = make_groups(key_all.reshape(clip_count, length, model_width), group_size)
    value_groups = make_groups(value_all.reshape(clip_count, length, model_width), group_size)
    mixed_groups, log_groups = lax.map(forward_fn, (query_groups, key_groups, value_groups))
    mixed_flat = mixed_groups.reshape(row_total, model_width)
    middle = start_rows + (
        jnp.dot(mixed_flat, full_out, preferred_element_type=jnp.float32) + bias_rows[3]
    )
    normed_two, norm_pull_two = jax.vjp(layer_norm, middle, gain_rows[1], bias_rows[4])
    second_low = normed_two.astype(jnp.bfloat16)
    upper_rows = jnp.dot(second_low, full_up, preferred_element_type=jnp.float32) + up_shift
    active, gelu_pull = jax.vjp(exact_gelu, upper_rows)
    active_low = active.astype(jnp.bfloat16)
    final_rows = middle + (
        jnp.dot(active_low, full_down, preferred_element_type=jnp.float32) + bias_rows[5]
    )
    activations = final_rows.astype(jnp.bfloat16).reshape(patches.shape)
    grad_final = cotangent.reshape(row_total, model_width)
    grad_down_part = row_product(active_low, grad_final)
    grad_down_bias = jnp.sum(grad_final.astype(jnp.float32), axis=0)
    grad_active = back_product(grad_final, full_down)
    (grad_upper,) = gelu_pull(grad_active)
    grad_upper_low = grad_upper.astype(jnp.bfloat16)
    grad_up_part = row_product(second_low, grad_upper_low)
    grad_up_shift = jnp.sum(grad_upper_low.astype(jnp.float32), axis=0)
    grad_second = back_product(grad_upper_low, full_up)
    grad_mid_norm, grad_gain_two, grad_bias_two = norm_pull_two(grad_second)
    grad_middle = grad_final.astype(jnp.float32) + grad_mid_norm
    grad_branch = grad_middle.astype(jnp.bfloat16)
    grad_out_part = row_product(mixed_flat, grad_branch)
    grad_out_bias = jnp.sum(grad_branch.astype(jnp.float32), axis=0)
    grad_mixed = back_product(grad_branch, full_out).astype(jnp.bfloat16)
    grad_mixed_groups = make_groups(
        grad_mixed.reshape(clip_count, local_len, model_width), group_size
    )
    grad_query_groups, grad_key_groups, grad_value_groups = lax.map(
        backward_fn, (query_groups, key_groups, value_groups, grad_mixed_groups, log_groups)
    )
    grad_key_own, grad_value_own = (
        lax.psum_scatter(
            grad_key_groups.reshape(clip_count, freq_rows, time_total, model_width).astype(
                jnp.bfloat16
            ),
            "seq",
            scatter_dimension=2,
            tiled=True,
        ).astype(jnp.float32),
        lax.psum_scatter(
            grad_value_groups.reshape(clip_count, freq_rows, time_total, model_width).astype(
                jnp.bfloat16
            ),
            "seq",
            scatter_dimension=2,
            tiled=True,
        ).astype(jnp.float32),
    )
    grad_query_loc = grad_query_groups.reshape(row_total, model_width)
    grad_key_loc = grad_key_own.reshape(row_total, model_width).astype(jnp.bfloat16)
    grad_value_loc = grad_value_own.reshape(row_total, model_width).astype(jnp.bfloat16)
    grad_joined = jnp.concatenate([grad_query_loc, grad_key_loc, grad_value_loc], axis=1)
    grad_qkv_part = row_product(normed_low, grad_joined)
    grad_query_bias = jnp.sum(grad_query_loc.astype(jnp.float32), axis=0)
    grad_value_bias = jnp.sum(grad_value_loc.astype(jnp.float32), axis=0)
    grad_first = back_product(grad_joined, full_qkv)
    grad_start_norm, grad_gain_one, grad_bias_one = norm_pull_one(grad_first)
    grad_start = grad_middle + grad_start_norm
    input_grad = jnp.where(masked, 0.0, grad_start).astype(jnp.bfloat16).reshape(patches.shape)
    grad_mask_part = jnp.sum(jnp.where(masked, grad_start, 0.0), axis=0)
    grad_gain_part = jnp.stack([grad_gain_one, grad_gain_two])
    grad_bias_part = jnp.stack(
        [
            grad_bias_one,
            grad_query_bias,
            grad_value_bias,
            grad_out_bias,
            grad_bias_two,
            grad_down_bias,
        ]
    )
    summed = (
        lax.psum_scatter(grad_qkv_part, ("seq", "clip"), scatter_dimension=0, tiled=True),
        lax.psum_scatter(grad_out_part, ("seq", "clip"), scatter_dimension=0, tiled=True),
        lax.psum_scatter(grad_mask_part, ("seq", "clip"), scatter_dimension=0, tiled=True),
        lax.psum_scatter(grad_gain_part, ("seq", "clip"), scatter_dimension=1, tiled=True),
        lax.psum_scatter(grad_bias_part, ("seq", "clip"), scatter_dimension=1, tiled=True),
        lax.psum_scatter(grad_up_part, ("seq", "clip"), scatter_dimension=0, tiled=True),
        lax.psum_scatter(grad_down_part, ("seq", "clip"), scatter_dimension=0, tiled=True),
        lax.psum_scatter(grad_up_shift, ("seq", "clip"), scatter_dimension=0, tiled=True),
    )
    new_qkv = 0.9 * avg_qkv + 0.1 * w_qkv.astype(jnp.float32)
    new_out = 0.9 * avg_out + 0.1 * w_out.astype(jnp.float32)
    new_mask = 0.9 * avg_mask + 0.1 * mask_embed.astype(jnp.float32)
    new_gains = 0.9 * avg_gains + 0.1 * gains.astype(jnp.float32)
    new_biases = 0.9 * avg_biases + 0.1 * biases.astype(jnp.float32)
    new_up = 0.9 * avg_up + 0.1 * w_up.astype(jnp.float32)
    new_down = 0.9 * avg_down + 0.1 * w_down.astype(jnp.float32)
    new_up_bias = 0.9 * avg_up_bias + 0.1 * up_bias.astype(jnp.float32)
    return (
        activations,
        input_grad,
        summed[0],
        summed[1],
        summed[2],
        summed[3],
        summed[4],
        summed[5],
        summed[6],
        summed[7],
        new_qkv,
        new_out,
        new_mask,
        new_gains,
        new_biases,
        new_up,
        new_down,
        new_up_bias,
    )


def solution(mesh):
    placed = (
        P("clip", None, "seq", None),
        P("clip", None),
        P("clip"),
        P("clip", None, "seq", None),
        P(("seq", "clip"), None),
        P(("seq", "clip"), None),
        P(("seq", "clip")),
        P(None, ("seq", "clip")),
        P(None, ("seq", "clip")),
        P(("seq", "clip"), None),
        P(("seq", "clip"), None),
        P(("seq", "clip")),
        P(("seq", "clip"), None),
        P(("seq", "clip"), None),
        P(("seq", "clip")),
        P(None, ("seq", "clip")),
        P(None, ("seq", "clip")),
        P(("seq", "clip"), None),
        P(("seq", "clip"), None),
        P(("seq", "clip")),
    )
    return jax.shard_map(
        body,
        mesh=mesh,
        in_specs=placed,
        out_specs=(
            P("clip", None, "seq", None),
            P("clip", None, "seq", None),
            P(("seq", "clip"), None),
            P(("seq", "clip"), None),
            P(("seq", "clip")),
            P(None, ("seq", "clip")),
            P(None, ("seq", "clip")),
            P(("seq", "clip"), None),
            P(("seq", "clip"), None),
            P(("seq", "clip")),
            P(("seq", "clip"), None),
            P(("seq", "clip"), None),
            P(("seq", "clip")),
            P(None, ("seq", "clip")),
            P(None, ("seq", "clip")),
            P(("seq", "clip"), None),
            P(("seq", "clip"), None),
            P(("seq", "clip")),
        ),
        check_vma=False,
    )
```

profile of v0, /device:TPU:0, one launch (start us, length us, event | category | flops | bytes accessed | tf_op | source)
XLA Modules:
  0.0 1272.0 jit_solution(1368373145277587235)
XLA Ops:
  9.9 42.7 %all-reduce.7 = (bf16[768]{0:T(1024)(128)(2,1)S(1)}, bf16[3072]{0:T(1024)(128)(2,1)S(1)}) all-reduce(bf16[768]{0:T(1024)(128)(2,1)S(1)} %dynamic-update-slice, bf16[3072]{0:T(1024)(128)(2,1)S(1)} %dynamic-update-slice.1), channel_id=1, replica_groups=mesh['seq'=4,'clip'=8] {'seq','clip'}, use_global_device_ids=true, to_apply=%add | all-reduce | flops 3840 | bytes 15360
  52.6 65.9 %all-gather = bf16[32,24,2]{1,2,0:T(2,128)(2,1)S(1)} all-gather(bf16[1,24,2]{1,2,0:T(2,128)(2,1)} %bitcast.197), channel_id=1, replica_groups=mesh['seq'=4,'clip'=8] {'seq','clip'}, dimensions={0}, use_global_device_ids=true | all-gather | bytes 3168 | tf_op jit(solution)/shard_map/all_gather | solution.py:146
  118.8 63.9 %all-gather.1 = bf16[32,24,6]{1,2,0:T(8,128)(2,1)S(1)} all-gather(bf16[1,24,6]{1,2,0:T(8,128)(2,1)} %bitcast.196), channel_id=1, replica_groups=mesh['seq'=4,'clip'=8] {'seq','clip'}, dimensions={0}, use_global_device_ids=true | all-gather | bytes 9504 | tf_op jit(solution)/shard_map/all_gather | solution.py:147
  192.0 6.4 fusion.35
  198.4 3.6 copy-done.16
  203.4 4.5 fusion.16
  212.2 35.7 %all-gather.13.cloned.1.call-done = bf16[8,8,64,768]{3,2,1,0:T(8,128)(2,1)} async-done(((bf16[8,8,16,768]{3,2,1,0:T(8,128)(2,1)}), bf16[8,8,64,768]{3,2,1,0:T(8,128)(2,1)}) %all-gather.13.cloned.1.call-update) | async-done | bytes 6291472 | tf_op jit(solution)/shard_map/all_gather | solution.py:181
  247.9 8.7 copy.90
  256.5 39.8 %all-gather.11.cloned.1.call-done = bf16[8,8,64,768]{3,2,1,0:T(8,128)(2,1)} async-done(((bf16[8,8,16,768]{3,2,1,0:T(8,128)(2,1)}), bf16[8,8,64,768]{3,2,1,0:T(8,128)(2,1)}) %all-gather.11.cloned.1.call-update) | async-done | bytes 6291472 | tf_op jit(solution)/shard_map/all_gather | solution.py:182
  296.4 8.6 copy.88
  305.0 30.4 %while.26 = (s32[]{:T(128)}, bf16[2,4,128,768]{3,2,1,0:T(8,128)(2,1)S(1)}, f32[2,4,12,128]{3,2,1,0:T(8,128)S(1)}, bf16[2,4,512,768]{2,3,1,0:T(8,128)(2,1)}, bf16...) while((s32[]{:T(128)}, bf16[2,4,128,768]{3,2,1,0:T(8,128)(2,1)S(1)}, ...), condition=%wide.region_6.7_spmd, body=%wide.region_3.6_spmd.sunk | while | flops 834004992 | bytes 63135844 | solution.py:188
  314.6 5.2 fusion.91
  329.8 5.2 fusion.91
  335.4 17.9 %all-gather.15.cloned.1.call-done = bf16[768,768]{1,0:T(8,128)(2,1)} async-done(((bf16[24,768]{1,0:T(8,128)(2,1)}), bf16[768,768]{1,0:T(8,128)(2,1)}) %all-gather.15.cloned.1.call-update) | async-done | bytes 1179664 | tf_op jit(solution)/shard_map/all_gather | solution.py:144
  353.3 3.9 fusion.33
  357.8 60.8 %all-gather.17.cloned.1.call-done = bf16[768,3072]{1,0:T(8,128)(2,1)} async-done(((bf16[24,3072]{1,0:T(8,128)(2,1)}), bf16[768,3072]{1,0:T(8,128)(2,1)}) %all-gather.17.cloned.1.call-update) | async-done | bytes 4718608 | tf_op jit(solution)/shard_map/all_gather | solution.py:148
  418.5 35.8 %multiply_convert_fusion.2 = (bf16[1024,3072]{1,0:T(8,128)(2,1)}, f32[1024,3072]{1,0:T(8,128)}, f32[1024,3072]{1,0:T(8,128)}) fusion(f32[3072]{0:T(1024)S(1)} %copy-done.51, bf16[768,3072]{1,0:T(8,128)(2,1)} %all-gather.17.cloned.1.call-done, f32[1024,768]{1,0:T(8,128)S(1)} %get-tuple-element.251, f32[768]{0:T(1024)S(1)} %copy-done.35, ...), kind=kOutput, calls=%fused_computation.34 | convolution fusion | flops 5043388416 | bytes 39348224 | tf_op jit(solution)/shard_map/dot_general | solution.py:195
  454.3 28.8 %all-gather.19.cloned.1.call-done = bf16[3072,768]{1,0:T(8,128)(2,1)} async-done(((bf16[96,768]{1,0:T(8,128)(2,1)}), bf16[3072,768]{1,0:T(8,128)(2,1)}) %all-gather.19.cloned.1.call-update) | async-done | bytes 4718608 | tf_op jit(solution)/shard_map/all_gather | solution.py:149
  483.1 19.3 %convert_reduce_fusion = (f32[3072]{0:T(1024)}, bf16[1024,3072]{1,0:T(8,128)(2,1)}) fusion(f32[1024,3072]{1,0:T(8,128)} %get-tuple-element.237, bf16[1024,768]{1,0:T(8,128)(2,1)} %bitcast.175, bf16[3072,768]{1,0:T(8,128)(2,1)} %all-gather.19.cloned.1.call-done, f32[1024,3072]{1,0:T(8,128)} %get-tuple-element.252, f32[3072]{0:T(1024)S(1)} %copy-done.51), kind=kOutput, calls=%fused_computation.32 | convolution fusion | flops 4885312512 | bytes 37773312 | tf_op jit(solution)/shard_map/dot_general | solution.py:32
  502.5 9.8 multiply_reduce_fusion.2
  518.5 115.8 %while.27 = (s32[]{:T(128)}, bf16[2,4,128,768]{2,3,1,0:T(8,128)(2,1)}, bf16[2,4,512,768]{3,2,1,0:T(8,128)(2,1)}, bf16[2,4,512,768]{3,2,1,0:T(8,128)(2,1)}, bf16[...) while((s32[]{:T(128)}, ...), condition=%wide.region_13.14_spmd, body=%wide.region_11.13_spmd.sunk | while | flops 2054940672 | bytes 306094400 | solution.py:220
  522.2 4.1 constant_dynamic-slice_fusion.20
  529.5 5.2 fusion.103
  534.9 4.7 copy.134
  539.6 12.5 multiply_reduce_fusion.11
  552.1 6.6 multiply_convert_fusion.5
  564.6 4.8 copy.135
  571.5 4.9 constant_dynamic-update-slice_fusion.9
  580.0 4.1 constant_dynamic-slice_fusion.20
  587.3 5.2 fusion.103
  592.7 4.7 copy.134
  597.4 12.5 multiply_reduce_fusion.11
  609.9 6.6 multiply_convert_fusion.5
  622.4 4.8 copy.135
  629.3 5.0 constant_dynamic-update-slice_fusion.9
  635.2 4.9 fusion.36
  640.2 12.3 fusion.27
  652.6 10.7 fusion.37
  666.1 24.6 %reduce-scatter.9.cloned.1.call-done = bf16[8,8,16,768]{3,2,1,0:T(8,128)(2,1)} async-done(((bf16[8,8,64,768]{3,2,1,0:T(8,128)(2,1)}), bf16[8,8,16,768]{3,2,1,0:T(8,128)(2,1)}) %reduce-scatter.9.cloned.1.call-update) | async-done | bytes 1572880 | tf_op jit(solution)/shard_map/reduce_scatter | solution.py:224
  690.7 60.5 %reduce-scatter.11.cloned.1.call-done = bf16[8,8,16,768]{3,2,1,0:T(8,128)(2,1)} async-done(((bf16[8,8,64,768]{3,2,1,0:T(8,128)(2,1)}), bf16[8,8,16,768]{3,2,1,0:T(8,128)(2,1)}) %reduce-scatter.11.cloned.1.call-update) | async-done | bytes 1572880 | tf_op jit(solution)/shard_map/reduce_scatter | solution.py:232
  751.1 9.6 fusion.22
  774.4 9.6 add_convert_fusion.1
  784.5 5.8 multiply_reduce_fusion.3
  796.0 40.3 %all-reduce.6 = (f32[768]{0:T(1024)S(1)}, f32[2,768]{1,0:T(2,128)S(1)}, f32[6,768]{1,0:T(8,128)S(1)}, f32[3072]{0:T(1024)S(1)}) all-reduce(f32[768]{0:T(1024)S(1)} %get-tuple-element.248, f32[2,768]{1,0:T(2,128)S(1)} %pad_maximum_fusion.3, f32[6,768]{1,0:T(8,128)S(1)} %stack.27, ...), channel_id=6, replica_groups=mesh['seq'=4,'clip'=8] {'seq','clip'}, use_global_device_ids=true, to_apply=%region_21.22.clone | all-reduce | flops 9984 | bytes 79872
  838.8 18.1 %reduce-scatter.15.cloned.1.call-done = f32[24,768]{1,0:T(8,128)} async-done(((f32[768,768]{1,0:T(8,128)}), f32[24,768]{1,0:T(8,128)}) %reduce-scatter.15.cloned.1.call-update) | async-done | bytes 73744 | tf_op jit(solution)/shard_map/reduce_scatter | solution.py:266
  856.9 141.5 %reduce-scatter.17.cloned.1.call-done = f32[24,3072]{1,0:T(8,128)} async-done(((f32[768,3072]{1,0:T(8,128)}), f32[24,3072]{1,0:T(8,128)}) %reduce-scatter.17.cloned.1.call-update) | async-done | bytes 294928 | tf_op jit(solution)/shard_map/reduce_scatter | solution.py:270
  998.4 141.7 %reduce-scatter.19.cloned.1.call-done = f32[96,768]{1,0:T(8,128)} async-done(((f32[3072,768]{1,0:T(8,128)}), f32[96,768]{1,0:T(8,128)}) %reduce-scatter.19.cloned.1.call-update) | async-done | bytes 294928 | tf_op jit(solution)/shard_map/reduce_scatter | solution.py:271
  1140.1 124.7 %reduce-scatter.13.cloned.1.call-done = f32[24,2304]{1,0:T(8,128)} async-done(((f32[768,2304]{1,0:T(8,128)}), f32[24,2304]{1,0:T(8,128)}) %reduce-scatter.13.cloned.1.call-update) | async-done | bytes 221200 | tf_op jit(solution)/shard_map/reduce_scatter | solution.py:265
  (269 shorter events, 99.8 us)
Async XLA Ops:
  7.2 181.5 %copy-start.11 = (bf16[8,8,16,768]{3,2,1,0:T(8,128)(2,1)S(1)}, bf16[8,8,16,768]{3,2,1,0:T(8,128)(2,1)}, u32[]{:S(2)}) copy-start(bf16[8,8,16,768]{3,2,1,0:T(8,128)(2,1)} %param.24) | copy-start | bytes 4718596
  7.2 184.8 %all-gather.9.cloned.1.call-start = ((), (), s32[]{:S(2)}) async-start(), calls=%async_computation.6 | async-start | bytes 3649536 | tf_op jit(solution)/shard_map/all_gather | solution.py:143
  7.9 239.9 %all-gather.13.cloned.1.call-start = ((), (), s32[]{:S(2)}) async-start(), calls=%async_computation.8 | async-start | bytes 7864320 | tf_op jit(solution)/shard_map/all_gather | solution.py:181
  52.6 139.4 %copy-start.30 = (f32[768]{0:T(1024)}, f32[768]{0:T(1024)S(1)}, u32[]{:S(2)}) copy-start(f32[768]{0:T(1024)S(1)} %convert_element_type.162) | copy-start | bytes 9220
  188.7 9.7 copy-start.37
  203.4 93.0 %all-gather.11.cloned.1.call-start = ((), (), s32[]{:S(2)}) async-start(), calls=%async_computation.7 | async-start | bytes 7864320 | tf_op jit(solution)/shard_map/all_gather | solution.py:182
  208.0 145.3 %all-gather.15.cloned.1.call-start = ((), (), s32[]{:S(2)}) async-start(), calls=%async_computation.9 | async-start | bytes 1216512 | tf_op jit(solution)/shard_map/all_gather | solution.py:144
  208.5 210.0 %all-gather.17.cloned.1.call-start = ((), (), s32[]{:S(2)}) async-start(), calls=%async_computation.10 | async-start | bytes 4866048 | tf_op jit(solution)/shard_map/all_gather | solution.py:148
  209.1 274.0 %all-gather.19.cloned.1.call-start = ((), (), s32[]{:S(2)}) async-start(), calls=%async_computation.11 | async-start | bytes 4866048 | tf_op jit(solution)/shard_map/all_gather | solution.py:149
  209.7 481.0 %reduce-scatter.9.cloned.1.call-start = ((), (), s32[]{:S(2)}) async-start(), calls=%async_computation.12 | async-start | bytes 7864320 | tf_op jit(solution)/shard_map/reduce_scatter | solution.py:224
  305.0 48.3 %copy-start.31 = (f32[768]{0:T(1024)S(1)}, f32[768]{0:T(1024)}, u32[]{:S(2)}) copy-start(f32[768]{0:T(1024)} %copy-done.30) | copy-start | bytes 9220
  305.0 48.3 %copy-start.48 = (pred[8,128]{1,0:T(8,128)(4,1)S(1)}, pred[8,128]{1,0:T(8,128)(4,1)}, u32[]{:S(2)}) copy-start(pred[8,128]{1,0:T(8,128)(4,1)} %copy-done.47) | copy-start | bytes 3076
  305.0 48.3 %copy-start.57 = (f32[768]{0:T(1024)S(1)}, f32[768]{0:T(1024)}, u32[]{:S(2)}) copy-start(f32[768]{0:T(1024)} %get-tuple-element.188) | copy-start | bytes 9220
  335.4 17.9 %copy-start.60 = (bf16[2,4,128,768]{3,2,1,0:T(8,128)(2,1)}, bf16[2,4,128,768]{3,2,1,0:T(8,128)(2,1)S(1)}, u32[]{:S(2)}) copy-start(bf16[2,4,128,768]{3,2,1,0:T(8,128)(2,1)S(1)} %get-tuple-element.100) | copy-start | bytes 4718596
  357.2 155.1 %copy-start.7 = (f32[1024,768]{1,0:T(8,128)}, f32[1024,768]{1,0:T(8,128)S(1)}, u32[]{:S(2)}) copy-start(f32[1024,768]{1,0:T(8,128)S(1)} %get-tuple-element.251) | copy-start | bytes 9437188
  357.2 61.3 %copy-start.33 = (f32[768]{0:T(1024)S(1)}, f32[768]{0:T(1024)}, u32[]{:S(2)}) copy-start(f32[768]{0:T(1024)} %get-tuple-element.192) | copy-start | bytes 9220
  357.2 61.3 %copy-start.35 = (f32[768]{0:T(1024)S(1)}, f32[768]{0:T(1024)}, u32[]{:S(2)}) copy-start(f32[768]{0:T(1024)} %get-tuple-element.187) | copy-start | bytes 9220
  357.2 61.3 %copy-start.51 = (f32[3072]{0:T(1024)S(1)}, f32[3072]{0:T(1024)}, u32[]{:S(2)}) copy-start(f32[3072]{0:T(1024)} %convert_element_type.172) | copy-start | bytes 36868
  357.2 155.0 %copy-start.25 = (f32[1024]{0:T(1024)}, f32[1024]{0:T(1024)S(1)}, u32[]{:S(2)}) copy-start(f32[1024]{0:T(1024)S(1)} %broadcast_multiply_fusion.2) | copy-start | bytes 12292
  357.7 154.5 %copy-start.28 = (f32[1024]{0:T(1024)}, f32[1024]{0:T(1024)S(1)}, u32[]{:S(2)}) copy-start(f32[1024]{0:T(1024)S(1)} %fusion.24) | copy-start | bytes 12292
  539.6 12.5 copy-start.1
  564.6 6.9 copy-start.2
  597.4 12.5 copy-start.1
  622.4 6.9 copy-start.2
  634.3 116.8 %reduce-scatter.11.cloned.1.call-start = ((), (), s32[]{:S(2)}) async-start(), calls=%async_computation.13 | async-start | bytes 7864320 | tf_op jit(solution)/shard_map/reduce_scatter | solution.py:232
  635.1 221.7 %reduce-scatter.15.cloned.1.call-start = ((), (), s32[]{:S(2)}) async-start(), calls=%async_computation.15 | async-start | bytes 2433024 | tf_op jit(solution)/shard_map/reduce_scatter | solution.py:266
  640.1 358.3 %reduce-scatter.17.cloned.1.call-start = ((), (), s32[]{:S(2)}) async-start(), calls=%async_computation.16 | async-start | bytes 9732096 | tf_op jit(solution)/shard_map/reduce_scatter | solution.py:270
  652.5 487.6 %reduce-scatter.19.cloned.1.call-start = ((), (), s32[]{:S(2)}) async-start(), calls=%async_computation.17 | async-start | bytes 9732096 | tf_op jit(solution)/shard_map/reduce_scatter | solution.py:271
  663.3 601.5 %reduce-scatter.13.cloned.1.call-start = ((), (), s32[]{:S(2)}) async-start(), calls=%async_computation.14 | async-start | bytes 7299072 | tf_op jit(solution)/shard_map/reduce_scatter | solution.py:265
  760.7 9.0 copy-start.22
  760.7 10.8 copy-start.24
  760.8 12.4 copy-start.23
  760.8 13.2 %copy-start.50 = (f32[768]{0:T(1024)S(1)}, f32[768]{0:T(1024)}, u32[]{:S(2)}) copy-start(f32[768]{0:T(1024)} %get-tuple-element.230) | copy-start | bytes 9220
  760.8 12.4 copy-start.27
  760.8 13.1 %copy-start.55 = (f32[768]{0:T(1024)S(1)}, f32[768]{0:T(1024)}, u32[]{:S(2)}) copy-start(f32[768]{0:T(1024)} %get-tuple-element.180) | copy-start | bytes 9220
  760.8 13.1 %copy-start.54 = (f32[768]{0:T(1024)S(1)}, f32[768]{0:T(1024)}, u32[]{:S(2)}) copy-start(f32[768]{0:T(1024)} %get-tuple-element.184) | copy-start | bytes 9220
  760.8 13.2 %copy-start.17 = (bf16[2,4,128,768]{2,3,1,0:T(8,128)(2,1)S(1)}, bf16[2,4,128,768]{2,3,1,0:T(8,128)(2,1)}, u32[]{:S(2)}) copy-start(bf16[2,4,128,768]{2,3,1,0:T(8,128)(2,1)} %get-tuple-element.102) | copy-start | bytes 4718596
  760.8 13.4 %copy-start.56 = (f32[768]{0:T(1024)S(1)}, f32[768]{0:T(1024)}, u32[]{:S(2)}) copy-start(f32[768]{0:T(1024)} %get-tuple-element.186) | copy-start | bytes 9220
  774.3 9.7 copy-start.19
  774.3 10.0 copy-start.12
  774.3 10.0 copy-start.20
  774.3 10.0 copy-start.32
  774.3 10.0 copy-start.38
  774.4 10.0 copy-start.40
  774.4 10.0 copy-start.42
  774.4 10.0 copy-start.49
  774.4 10.0 copy-start.58
  774.4 10.0 copy-start.59
  (33 other events, 125.9 us)
Sparse Core Ops, SparseCore 0:
  10.9 62.7 all-gather.8
  203.5 44.3 all-gather.12
  250.0 46.3 all-gather.10
  299.2 54.0 all-gather.14
  356.1 62.3 all-gather.16
  421.3 61.8 all-gather.18
  634.4 56.1 reduce-scatter.8
  693.2 57.8 reduce-scatter.10
  757.0 99.8 reduce-scatter.14
  863.2 135.1 reduce-scatter.16
  1004.9 135.1 reduce-scatter.18
  1146.2 118.5 reduce-scatter.12
where the time goes:
time: 1280 us; the launch traced here: 1270 us
  waiting for transfers between devices  697 us (54%)
  blocking collectives  213 us (17%)
  matrix products  196 us (15%)
  local copies, waits for them, and re-layouts  96.9 us (8%)
  other arithmetic  52.7 us (4%)
  between operations  15.5 us (1%)
    reduce_scatter x1, waiting for transfers between devices, body(): lax.psum_scatter(grad_down_part, ('seq', 'clip'), scatter_dimension=0, ti...  142 us
    reduce_scatter x1, waiting for transfers between devices, body(): lax.psum_scatter(grad_up_part, ('seq', 'clip'), scatter_dimension=0, tile...  142 us
    reduce_scatter x1, waiting for transfers between devices, body(): lax.psum_scatter(grad_qkv_part, ('seq', 'clip'), scatter_dimension=0, til...  125 us
    unnamed x2, blocking collectives  83 us
    all_gather x1, blocking collectives, body(): lax.all_gather(gains, ('seq', 'clip'), axis=1, tiled=True)  65.9 us
    all_gather x1, blocking collectives, body(): lax.all_gather(biases, ('seq', 'clip'), axis=1, tiled=True)  63.9 us
    all_gather x1, waiting for transfers between devices, body(): lax.all_gather(w_up, ('seq', 'clip'), axis=0, tiled=True)  60.8 us
    reduce_scatter x1, waiting for transfers between devices, body(): lax.psum_scatter(grad_value_groups.reshape(clip_count, freq_rows, time_to...  60.5 us
  transfers between devices with their start and end apart: 12, of which 11 were waited for; matrix products, arithmetic and copies ran while one was open for 14% of the time, Pallas kernels for 0%

commit v1 on v0

v1 whole, which is shorter than its diff:
```python
import math
from functools import partial

import jax
import jax.numpy as jnp
from jax import lax
from jax.experimental import pallas as pl
from jax.experimental.pallas import tpu as pltpu
from jax.sharding import Mesh, PartitionSpec as P

H = 12
norm_eps = 1e-06
F32 = jnp.float32
BF16 = jnp.bfloat16
ALL = ("sx", "core", "clip")


def layer_norm(hidden, gain_row, shift_row):
    center = hidden - jnp.mean(hidden, axis=-1, keepdims=True)
    spread = jnp.mean(center * center, axis=-1, keepdims=True)
    return center * lax.rsqrt(spread + norm_eps) * gain_row + shift_row


def exact_gelu(upper_rows):
    return upper_rows * (0.5 + 0.5 * lax.erf(upper_rows * math.sqrt(0.5)))


def dot(left_side, right_side, left_dim, right_dim):
    return lax.dot_general(
        left_side, right_side, (((left_dim,), (right_dim,)), ((), ())), preferred_element_type=F32
    )


def forward_kernel(q_ref, k_ref, v_ref, o_ref, log_ref, *, head_size, scale):
    length = q_ref.shape[0] * q_ref.shape[2]
    query = q_ref[...].reshape(length, -1) * scale
    key = k_ref[...].reshape(length, -1)
    value = v_ref[...].reshape(length, -1)
    mixed = []
    for i in range(query.shape[1] // head_size):
        cols = slice(i * head_size, (i + 1) * head_size)
        scores = dot(key[:, cols], query[:, cols], 1, 1)
        top = jnp.max(scores, axis=0, keepdims=True)
        shifted = jnp.exp(scores - top)
        total = jnp.sum(shifted, axis=0, keepdims=True)
        mixed.append(dot(value[:, cols], shifted.astype(BF16), 0, 0) / total)
        log_ref[0, 0, i : i + 1, :] = top + jnp.log(total)
    mixed = jnp.concatenate(mixed, axis=0).T.astype(BF16)
    o_ref[...] = mixed.reshape(o_ref.shape)


def backward_kernel(q_ref, k_ref, v_ref, g_ref, log_ref, dq_ref, dk_ref, dv_ref, *, head_size, scale):
    length = q_ref.shape[0] * q_ref.shape[2]
    query = q_ref[...].reshape(length, -1) * scale
    key = k_ref[...].reshape(length, -1)
    value = v_ref[...].reshape(length, -1)
    grad = g_ref[...].reshape(length, -1)
    grad_query, grad_key, grad_value = [], [], []
    for i in range(query.shape[1] // head_size):
        cols = slice(i * head_size, (i + 1) * head_size)
        scores = dot(key[:, cols], query[:, cols], 1, 1)
        prob = jnp.exp(scores - log_ref[0, 0, i : i + 1, :])
        grad_prob = dot(value[:, cols], grad[:, cols], 1, 1)
        inner = jnp.sum(grad_prob * prob, axis=0, keepdims=True)
        grad_scores = (prob * (grad_prob - inner)).astype(BF16)
        grad_query.append(dot(key[:, cols], grad_scores, 0, 0))
        grad_key.append(dot(grad_scores, query[:, cols], 1, 0))
        grad_value.append(dot(prob.astype(BF16), grad[:, cols], 1, 0))
    dq = (jnp.concatenate(grad_query, axis=0) * scale).T.astype(BF16)
    dq_ref[...] = dq.reshape(dq_ref.shape)
    dk_ref[...] = jnp.concatenate(grad_key, axis=1).astype(BF16).reshape(dk_ref.shape)
    dv_ref[...] = jnp.concatenate(grad_value, axis=1).astype(BF16).reshape(dv_ref.shape)


def head_spec(shape, offset):
    slots, _, rows, _ = shape
    return pl.BlockSpec((slots, 1, rows, 128), lambda c, j: (0, c, 0, j + offset))


def attend_forward(queries, keys, values, head_count):
    slots, clips, rows, width = queries.shape
    head_size = width // head_count
    blocks, per_block = width // 128, 128 // head_size
    return pl.pallas_call(
        partial(forward_kernel, head_size=head_size, scale=1.0 / math.sqrt(head_size)),
        grid=(clips, blocks),
        in_specs=[head_spec(queries.shape, 0)] * 3,
        out_specs=[
            head_spec(queries.shape, 0),
            pl.BlockSpec((1, 1, per_block, slots * rows), lambda c, j: (c, j, 0, 0)),
        ],
        out_shape=[
            jax.ShapeDtypeStruct(queries.shape, BF16),
            jax.ShapeDtypeStruct((clips, blocks, per_block, slots * rows), F32),
        ],
        name="attend_forward",
    )(queries, keys, values)


def attend_backward(queries, keys, values, grad_mixed, logs, head_count, first, count):
    slots, clips, rows, width = queries.shape
    head_size = width // head_count
    per_block = 128 // head_size
    spec = head_spec(queries.shape, first)
    out_spec = head_spec(queries.shape, 0)
    out_shape = jax.ShapeDtypeStruct((slots, clips, rows, count * 128), BF16)
    return pl.pallas_call(
        partial(backward_kernel, head_size=head_size, scale=1.0 / math.sqrt(head_size)),
        grid=(clips, count),
        in_specs=[spec] * 4
        + [pl.BlockSpec((1, 1, per_block, slots * rows), lambda c, j: (c, j + first, 0, 0))],
        out_specs=[out_spec] * 3,
        out_shape=[out_shape] * 3,
        name="attend_backward",
    )(queries, keys, values, grad_mixed, logs)


def swap(array, axis_name, bit):
    size = lax.axis_size(axis_name)
    return lax.ppermute(array, axis_name, [(i, i ^ bit) for i in range(size)])


def bit_of(axis_name, bit):
    return (lax.axis_index(axis_name) // bit) % 2


def device_bits():
    bits = []
    for axis_name in ALL:
        bit = lax.axis_size(axis_name) // 2
        while bit:
            bits.append((axis_name, bit))
            bit //= 2
    return bits


def scatter_sum(part, order, send_type=BF16):
    left = device_bits()
    array = part.reshape((2,) * len(left) + part.shape[1:])
    for step in order:
        axis = left.index(step)
        mine = bit_of(*step)
        keep = lax.dynamic_index_in_dim(array, mine, axis, False)
        send = lax.dynamic_index_in_dim(array, 1 - mine, axis, False).astype(send_type)
        array = keep + swap(send, *step).astype(F32)
        left.pop(axis)
    return array


def gather_all(shard, order):
    bits = device_bits()
    array, have = shard, []
    for step in order:
        other = swap(array, *step)
        have = sorted(have + [step], key=bits.index)
        axis = have.index(step)
        mine = bit_of(*step)
        both = jnp.stack([array, other], axis=axis)
        flip = jnp.stack([other, array], axis=axis)
        array = jnp.where(mine == 0, both, flip)
    return array.reshape((-1,) + shard.shape)


def body(
    patches,
    mask_index,
    mask_count,
    cotangent,
    w_qkv,
    w_out,
    mask_embed,
    gains,
    biases,
    w_up,
    w_down,
    up_bias,
    avg_qkv,
    avg_out,
    avg_mask,
    avg_gains,
    avg_biases,
    avg_up,
    avg_down,
    avg_up_bias,
):
    clip_count, freq_rows, time_local, width = patches.shape
    seq_names = ("sx", "core")
    seq_size = lax.axis_size("sx") * lax.axis_size("core")
    seq_here = lax.axis_index(seq_names)
    devices = seq_size * lax.axis_size("clip")
    local_len = freq_rows * time_local
    own_clips = clip_count // seq_size
    row_total = seq_size * own_clips * local_len
    grid_shape = (seq_size, own_clips, local_len, width)

    bits = device_bits()
    clip_bits = [b for b in bits if b[0] == "clip"]
    other_bits = [b for b in bits if b[0] == "sx"]
    core_bits = [b for b in bits if b[0] == "core"]
    low_first = clip_bits[::-1]
    order_a = core_bits + other_bits + low_first
    order_b = core_bits + low_first[:1] + other_bits + low_first[1:]

    def trade(chunks):
        return [chunks[0]] + [
            lax.ppermute(chunks[k], seq_names, [(i, i ^ k) for i in range(seq_size)])
            for k in range(1, seq_size)
        ]

    def rows_in(array):
        array = array.reshape(seq_size, own_clips, local_len, width)
        got = trade(
            [lax.dynamic_index_in_dim(array, seq_here ^ k, 0, False) for k in range(seq_size)]
        )
        return jnp.stack(got).reshape(row_total, width)

    def rows_out(array):
        array = array.reshape(grid_shape)
        got = jnp.stack(trade([array[k] for k in range(seq_size)]))
        order = [lax.dynamic_index_in_dim(got, seq_here ^ k, 0, False) for k in range(seq_size)]
        return jnp.stack(order).reshape(patches.shape)

    share = width // devices
    up_share = up_bias.shape[0]
    small = jnp.concatenate([mask_embed, gains.reshape(-1), biases.reshape(-1), up_bias])
    small_size = small.shape[0]
    small_padded = -(-small_size // 128) * 128
    small = jnp.pad(small, (0, small_padded - small_size))
    small_all = gather_all(small, clip_bits + other_bits + core_bits)

    full_qkv = lax.all_gather(w_qkv, ALL, axis=0, tiled=True)
    patch_rows = rows_in(patches)
    grad_final = rows_in(cotangent)
    full_out = lax.all_gather(w_out, ALL, axis=0, tiled=True)
    full_up = lax.all_gather(w_up, ALL, axis=0, tiled=True)
    full_down = lax.all_gather(w_down, ALL, axis=0, tiled=True)

    small_rows = small_all[:, : 9 * share].astype(F32).reshape(devices, 9, share)
    small_rows = small_rows.transpose(1, 0, 2).reshape(9, width)
    mask_vector, gain_rows, bias_rows = small_rows[0], small_rows[1:3], small_rows[3:9]
    up_shift = small_all[:, 9 * share : small_size].astype(F32).reshape(-1)

    slot_ids = lax.broadcasted_iota(jnp.int32, (seq_size, freq_rows, time_local), 0)
    freq_ids = lax.broadcasted_iota(jnp.int32, (seq_size, freq_rows, time_local), 1)
    time_ids = lax.broadcasted_iota(jnp.int32, (seq_size, freq_rows, time_local), 2)
    time_ids = time_ids + (slot_ids ^ seq_here) * time_local
    positions = (freq_ids * (time_local * seq_size) + time_ids).reshape(-1)
    own_index = lax.dynamic_slice_in_dim(mask_index, seq_here * own_clips, own_clips, 0)
    own_count = lax.dynamic_slice_in_dim(mask_count, seq_here * own_clips, own_clips, 0)
    live = lax.broadcasted_iota(jnp.int32, own_index.shape, 1) < own_count[:, None]
    live_index = jnp.where(live, own_index, -1)
    hits = live_index[:, :, None] == positions[None, None, :]
    masked = jnp.any(hits, axis=1).reshape(own_clips, seq_size, local_len)
    masked = masked.transpose(1, 0, 2).reshape(row_total, 1)

    start_rows = jnp.where(masked, mask_vector, patch_rows.astype(F32))
    normed_one, norm_pull_one = jax.vjp(layer_norm, start_rows, gain_rows[0], bias_rows[0])
    normed_low = normed_one.astype(BF16)
    joined = jnp.dot(normed_low, full_qkv, preferred_element_type=F32)
    queries = (joined[:, :width] + bias_rows[1]).astype(BF16).reshape(grid_shape)
    keys = joined[:, width : 2 * width].astype(BF16).reshape(grid_shape)
    values = (joined[:, 2 * width :] + bias_rows[2]).astype(BF16).reshape(grid_shape)
    mixed, logs = attend_forward(queries, keys, values, H)
    mixed_flat = mixed.reshape(row_total, width)
    middle = start_rows + (jnp.dot(mixed_flat, full_out, preferred_element_type=F32) + bias_rows[3])
    normed_two, norm_pull_two = jax.vjp(layer_norm, middle, gain_rows[1], bias_rows[4])
    second_low = normed_two.astype(BF16)
    upper_rows = jnp.dot(second_low, full_up, preferred_element_type=F32) + up_shift
    active, gelu_pull = jax.vjp(exact_gelu, upper_rows)
    active_low = active.astype(BF16)
    final_rows = middle + (jnp.dot(active_low, full_down, preferred_element_type=F32) + bias_rows[5])
    activations = rows_out(final_rows.astype(BF16))

    def by_owner(part):
        return part.reshape(devices, -1, part.shape[1])

    def send_grad(part):
        half = part.shape[1] // 2
        part = by_owner(part)
        return jnp.concatenate(
            [scatter_sum(part[..., :half], order_a), scatter_sum(part[..., half:], order_b)], axis=1
        )

    grad_down = send_grad(dot(active_low, grad_final, 0, 0))
    grad_down_bias = jnp.sum(grad_final.astype(F32), axis=0)
    grad_active = dot(grad_final, full_down, 1, 1)
    (grad_upper,) = gelu_pull(grad_active)
    grad_upper_low = grad_upper.astype(BF16)
    grad_up = send_grad(dot(second_low, grad_upper_low, 0, 0))
    grad_up_shift = jnp.sum(grad_upper_low.astype(F32), axis=0)
    grad_second = dot(grad_upper_low, full_up, 1, 1)
    grad_mid_norm, grad_gain_two, grad_bias_two = norm_pull_two(grad_second)
    grad_middle = grad_final.astype(F32) + grad_mid_norm
    grad_branch = grad_middle.astype(BF16)
    grad_out = send_grad(dot(mixed_flat, grad_branch, 0, 0))
    grad_out_bias = jnp.sum(grad_branch.astype(F32), axis=0)
    grad_mixed = dot(grad_branch, full_out, 1, 1).astype(BF16).reshape(grid_shape)
    groups = 3
    per_group = width // 128 // groups
    pieces = [
        attend_backward(queries, keys, values, grad_mixed, logs, H, g * per_group, per_group)
        for g in range(groups)
    ]
    grad_joined = jnp.concatenate(
        [p[i].reshape(row_total, -1) for i in range(3) for p in pieces], axis=1
    )
    grad_qkv = send_grad(dot(normed_low, grad_joined, 0, 0))
    grad_query_bias = jnp.sum(grad_joined[:, :width].astype(F32), axis=0)
    grad_value_bias = jnp.sum(grad_joined[:, 2 * width :].astype(F32), axis=0)
    grad_first = dot(grad_joined, full_qkv, 1, 1)
    grad_start_norm, grad_gain_one, grad_bias_one = norm_pull_one(grad_first)
    grad_start = grad_middle + grad_start_norm
    input_grad = rows_out(jnp.where(masked, 0.0, grad_start).astype(BF16))
    grad_mask_part = jnp.sum(jnp.where(masked, grad_start, 0.0), axis=0)
    small_grads = jnp.stack(
        [
            grad_mask_part,
            grad_gain_one,
            grad_gain_two,
            grad_bias_one,
            grad_query_bias,
            grad_value_bias,
            grad_out_bias,
            grad_bias_two,
            grad_down_bias,
        ]
    )
    small_grads = small_grads.reshape(9, devices, share).transpose(1, 0, 2).reshape(devices, -1)
    small_grads = jnp.concatenate([small_grads, grad_up_shift.reshape(devices, up_share)], axis=1)
    small_grads = jnp.pad(small_grads, ((0, 0), (0, small_padded - small_size)))
    small_sum = scatter_sum(small_grads, order_a, F32)
    own_rows = small_sum[: 9 * share].reshape(9, share)

    def moved(average, param):
        return 0.9 * average + 0.1 * param.astype(F32)

    return (
        activations,
        input_grad,
        grad_qkv,
        grad_out,
        own_rows[0],
        own_rows[1:3],
        own_rows[3:9],
        grad_up,
        grad_down,
        small_sum[9 * share : small_size],
        moved(avg_qkv, w_qkv),
        moved(avg_out, w_out),
        moved(avg_mask, mask_embed),
        moved(avg_gains, gains),
        moved(avg_biases, biases),
        moved(avg_up, w_up),
        moved(avg_down, w_down),
        moved(avg_up_bias, up_bias),
    )


def solution(mesh):
    seq_size, clip_size = mesh.shape["seq"], mesh.shape["clip"]
    fine = Mesh(mesh.devices.reshape(seq_size // 2, 2, clip_size), ALL)
    rows = P("clip", None, ("sx", "core"), None)
    first, second, only = P(ALL, None), P(None, ALL), P(ALL)
    params = (first, first, only, second, second, first, first, only)
    return jax.shard_map(
        body,
        mesh=fine,
        in_specs=(rows, P("clip", None), P("clip"), rows) + params + params,
        out_specs=(rows, rows) + params + params,
        check_vma=False,
    )
```

time: 1280 us -> 625 us (0.49)
  waiting for transfers between devices: 697 us -> 274 us
  blocking collectives: 213 us -> 0 us
  matrix products: 196 us -> 85.1 us
  starting transfers between devices: 0.7 us -> 62.2 us
  Pallas kernels: 0 us -> 49.7 us
    reduce_scatter x6 -> x0, waiting for transfers between devices: 511 us -> none  [the longest x1 142 us: body(): lax.psum_scatter(grad_down_part, ('seq', 'clip'), scatter_dimension=0, ti...]
    all_gather x2 -> x0, blocking collectives: 130 us -> none  [the longest x1 65.9 us: body(): lax.all_gather(gains, ('seq', 'clip'), axis=1, tiled=True)]
    ppermute x0 -> x62, waiting for transfers between devices: none -> 124 us  [the longest x50 108 us: swap(): return lax.ppermute(array, axis_name, [(i, i ^ bit) for i in range(size)])]
    dot_general x26 -> x12, matrix products: 196 us -> 85.1 us  [the longest x8 52.6 us: dot(): lax.dot_general(left_side, right_side, (((left_dim,), (right_dim,)), ((),...]
    unnamed x2 -> x0, blocking collectives: 83 us -> none
    ppermute x0 -> x62, starting transfers between devices: none -> 62.1 us  [the longest x50 54.7 us: swap(): return lax.ppermute(array, axis_name, [(i, i ^ bit) for i in range(size)])]
    pallas_call x0 -> x4, Pallas kernels: none -> 49.7 us  [the longest x3 31.9 us: attend_backward(): pl.pallas_call(partial(backward_kernel, head_size=head_size, scale=1.0 /...]
    all_gather x6 -> x4, waiting for transfers between devices: 183 us -> 148 us  [the longest x1 61 us: body(): full_up = lax.all_gather(w_up, ALL, axis=0, tiled=True)]
  transfers between devices with their start and end apart: 12 -> 66, of which waited for: 11 -> 41; matrix products, arithmetic and copies ran while one was open for 14% -> 26% of each run, Pallas kernels for 0% -> 3%
where the time goes in v1:
time: 625 us; the launch traced here: 620 us
  waiting for transfers between devices  274 us (44%)
  local copies, waits for them, and re-layouts  92.1 us (15%)
  matrix products  85.1 us (14%)
  starting transfers between devices  62.2 us (10%)
  Pallas kernels  49.7 us (8%)
  other arithmetic  41.2 us (7%)
  between operations  15.6 us (2%)
    ppermute x50, waiting for transfers between devices, swap(): return lax.ppermute(array, axis_name, [(i, i ^ bit) for i in range(size)])  108 us
    all_gather x1, waiting for transfers between devices, body(): full_up = lax.all_gather(w_up, ALL, axis=0, tiled=True)  61 us
    ppermute x50, starting transfers between devices, swap(): return lax.ppermute(array, axis_name, [(i, i ^ bit) for i in range(size)])  54.7 us
    dot_general x8, matrix products, dot(): lax.dot_general(left_side, right_side, (((left_dim,), (right_dim,)), ((),...  52.6 us
    all_gather x1, waiting for transfers between devices, body(): full_down = lax.all_gather(w_down, ALL, axis=0, tiled=True)  52.2 us
    pallas_call x3, Pallas kernels, attend_backward(): pl.pallas_call(partial(backward_kernel, head_size=head_size, scale=1.0 /...  31.9 us
    all_gather x1, waiting for transfers between devices, body(): full_out = lax.all_gather(w_out, ALL, axis=0, tiled=True)  27 us
    unnamed x145, local copies, waits for them, and re-layouts  18.5 us
  transfers between devices with their start and end apart: 66, of which 41 were waited for; matrix products, arithmetic and copies ran while one was open for 26% of the time, Pallas kernels for 3%

profile of v1, /device:TPU:0, one launch (start us, length us, event | category | flops | bytes accessed | tf_op | source)
XLA Modules:
  0.0 620.0 jit_solution(15831946501138315876)
XLA Ops:
  11.7 4.1 collective-permute-start
  15.9 2.5 constant_dynamic-slice_fusion.33
  40.0 11.1 %collective-permute-done.3 = bf16[2,2,2,384]{3,0,2,1:T(2,128)(2,1)S(1)} collective-permute-done((bf16[2,2,2,384]{3,0,2,1:T(2,128)(2,1)S(1)}, bf16[2,2,2,384]{3,0,2,1:T(2,128)(2,1)S(1)}, u32[]{:S(2)}, u32[]{:S(2)}) %collective-permute-start.3) | collective-permute-done | bytes 6176 | tf_op jit(solution)/shard_map/ppermute | solution.py:120
  55.4 2.4 fusion.12
  61.6 5.6 collective-permute-done.12
  67.3 2.6 convert_reduce_fusion.1
  69.9 7.6 %all-gather.5.cloned.1.call-done = bf16[768,2304]{1,0:T(8,128)(2,1)} async-done(((bf16[24,2304]{1,0:T(8,128)(2,1)}), bf16[768,2304]{1,0:T(8,128)(2,1)}) %all-gather.5.cloned.1.call-update) | async-done | bytes 3538960 | tf_op jit(solution)/shard_map/all_gather | solution.py:231
  77.5 5.8 fusion.85
  84.6 2.3 fusion.8
  86.9 17.9 %attend_forward.1 = (bf16[4,2,128,768]{3,2,1,0:T(8,128)(2,1)}, f32[2,6,2,512]{3,2,1,0:T(2,128)}) custom-call(bf16[4,2,128,768]{3,2,1,0:T(8,128)(2,1)} %bitcast.346, bf16[4,2,128,768]{3,2,1,0:T(8,128)(2,1)} %bitcast.338, bf16[4,2,128,768]{3,2,1,0:T(8,128)(2,1)} %bitcast.342), custom_call_target="tpu_custom_call" | custom-call | tf_op jit(solution)/shard_map/attend_forward/pallas_call | solution.py:84
  104.8 2.6 copy.190
  107.4 27.0 %all-gather.7.cloned.1.call-done = bf16[768,768]{1,0:T(8,128)(2,1)} async-done(((bf16[24,768]{1,0:T(8,128)(2,1)}), bf16[768,768]{1,0:T(8,128)(2,1)}) %all-gather.7.cloned.1.call-update) | async-done | bytes 1179664 | tf_op jit(solution)/shard_map/all_gather | solution.py:234
  134.4 3.9 fusion.84
  138.8 61.0 %all-gather.9.cloned.1.call-done = bf16[768,3072]{1,0:T(8,128)(2,1)} async-done(((bf16[24,3072]{1,0:T(8,128)(2,1)}), bf16[768,3072]{1,0:T(8,128)(2,1)}) %all-gather.9.cloned.1.call-update) | async-done | bytes 4718608 | tf_op jit(solution)/shard_map/all_gather | solution.py:235
  199.8 12.4 %fusion.3 = (bf16[3072,1024]{0,1:T(8,128)(2,1)}, f32[1024,3072]{1,0:T(8,128)}) fusion(f32[3072]{0:T(1024)S(1)} %reshape.852, bf16[768,3072]{1,0:T(8,128)(2,1)} %all-gather.9.cloned.1.call-done, f32[1024,768]{1,0:T(8,128)S(1)} %get-tuple-element.108, f32[768]{0:T(1024)S(1)} %add.575, f32[768]{0:T(1024)S(1)} %mul.279, f32[1024]{0:T(1024)S(1)} %fusion.62, ...), kind=kOutput, calls=%fused_computation.9 | convolution fusion | flops 4854644736 | bytes 26765312 | tf_op jit(solution)/shard_map/dot_general | solution.py:268
  212.2 52.2 %all-gather.11.cloned.1.call-done = bf16[3072,768]{1,0:T(8,128)(2,1)} async-done(((bf16[96,768]{1,0:T(8,128)(2,1)}), bf16[3072,768]{1,0:T(8,128)(2,1)}) %all-gather.11.cloned.1.call-update) | async-done | bytes 4718608 | tf_op jit(solution)/shard_map/all_gather | solution.py:236
  264.4 12.8 %convert_reduce_fusion = (f32[3072]{0:T(1024)}, bf16[1024,3072]{1,0:T(8,128)(2,1)S(1)}) fusion(f32[1024,3072]{1,0:T(8,128)} %get-tuple-element.114, f32[3072]{0:T(1024)S(1)} %reshape.852, bf16[1024,768]{1,0:T(8,128)(2,1)} %bitcast.370, bf16[3072,768]{1,0:T(8,128)(2,1)} %all-gather.11.cloned.1.call-done), kind=kOutput, calls=%fused_computation.5 | convolution fusion | flops 4879021056 | bytes 25190400 | tf_op jit(solution)/shard_map/dot_general | solution.py:29
  277.2 6.1 multiply_reduce_fusion
  287.0 2.6 convolution_convert_fusion
  289.6 10.5 %attend_backward.3 = (bf16[4,2,128,256]{3,2,1,0:T(8,128)(2,1)}, bf16[4,2,128,256]{3,2,1,0:T(8,128)(2,1)}, bf16[4,2,128,256]{3,2,1,0:T(8,128)(2,1)}) custom-call(bf16[4,2,128,768]{3,2,1,0:T(8,128)(2,1)} %bitcast.347, bf16[4,2,128,768]{3,2,1,0:T(8,128)(2,1)} %bitcast.339, bf16[4,2,128,768]{3,2,1,0:T(8,128)(2,1)} %bitcast.343, ...), custom_call_target="tpu_custom_call" | custom-call | tf_op jit(solution)/shard_map/attend_backward/pallas_call | solution.py:107
  300.1 10.7 %attend_backward.4 = (bf16[4,2,128,256]{3,2,1,0:T(8,128)(2,1)}, bf16[4,2,128,256]{3,2,1,0:T(8,128)(2,1)}, bf16[4,2,128,256]{3,2,1,0:T(8,128)(2,1)}) custom-call(bf16[4,2,128,768]{3,2,1,0:T(8,128)(2,1)} %bitcast.348, bf16[4,2,128,768]{3,2,1,0:T(8,128)(2,1)} %bitcast.340, bf16[4,2,128,768]{3,2,1,0:T(8,128)(2,1)} %bitcast.344, ...), custom_call_target="tpu_custom_call" | custom-call | tf_op jit(solution)/shard_map/attend_backward/pallas_call | solution.py:107
  310.8 10.6 %attend_backward.5 = (bf16[4,2,128,256]{3,2,1,0:T(8,128)(2,1)}, bf16[4,2,128,256]{3,2,1,0:T(8,128)(2,1)}, bf16[4,2,128,256]{3,2,1,0:T(8,128)(2,1)}) custom-call(bf16[4,2,128,768]{3,2,1,0:T(8,128)(2,1)} %bitcast.349, bf16[4,2,128,768]{3,2,1,0:T(8,128)(2,1)} %bitcast.341, bf16[4,2,128,768]{3,2,1,0:T(8,128)(2,1)} %bitcast.345, ...), custom_call_target="tpu_custom_call" | custom-call | tf_op jit(solution)/shard_map/attend_backward/pallas_call | solution.py:107
  321.4 10.7 %fusion.72 = f32[768,3072]{1,0:T(8,128)} fusion(bf16[1024,3072]{1,0:T(8,128)(2,1)} %copy-done.12, f32[1024,768]{1,0:T(8,128)S(1)} %get-tuple-element.108, f32[768]{0:T(1024)S(1)} %add.575, f32[768]{0:T(1024)S(1)} %mul.279, f32[1024]{0:T(1024)S(1)} %fusion.62, f32[1024]{0:T(1024)S(1)} %broadcast_multiply_fusion), kind=kOutput, calls=%fused_computation.294 | convolution fusion | flops 4835770368 | bytes 18888704 | tf_op jit(solution)/shard_map/dot_general | solution.py:29
  332.1 10.5 %add_convert_fusion.1 = bf16[1024,768]{1,0:T(8,128)(2,1)S(1)} fusion(f32[1024,768]{1,0:T(8,128)S(1)} %get-tuple-element.108, bf16[3072,768]{1,0:T(8,128)(2,1)} %all-gather.11.cloned.1.call-done, f32[1024,3072]{1,0:T(8,128)} %get-tuple-element.114, f32[3072]{0:T(1024)S(1)} %reshape.852, f32[768]{0:T(1024)S(1)} %add.583), kind=kOutput, calls=%fused_computation.34 | convolution fusion | flops 4853071872 | bytes 22035456 | tf_op jit(solution)/shard_map/dot_general | solution.py:271
  349.3 5.0 multiply_reduce_fusion.1
  360.5 3.9 fusion.6
  404.0 8.3 %fusion.78 = (f32[32,24,1536]{2,1,0:T(8,128)}, f32[32,24,1536]{2,1,0:T(8,128)}) fusion(f32[32,24,3072]{2,1,0:T(8,128)} %bitcast.350), kind=kLoop, calls=%fused_computation.299 | loop fusion | bytes 18874368 | tf_op jit(solution)/shard_map/slice | solution.py:281
  412.2 8.6 %copy.201 = bf16[3072,1024]{1,0:T(8,128)(2,1)} copy(bf16[3072,1024]{0,1:T(8,128)(2,1)} %get-tuple-element.113) | data formatting | bytes 12582912 | tf_op jit(solution)/shard_map/convert_element_type | solution.py:270
  420.9 10.1 %fusion.86 = f32[32,96,768]{2,1,0:T(8,128)} fusion(bf16[32,96,1024]{2,1,0:T(8,128)(2,1)} %bitcast.376, bf16[1024,768,1]{1,0,2:T(8,128)(2,1)S(1)} %bitcast.371), kind=kOutput, calls=%fused_computation.307 | convolution fusion | flops 4831838208 | bytes 17301504 | tf_op jit(solution)/shard_map/dot_general | solution.py:29
  431.0 4.4 fusion.77
  435.4 4.6 fusion.17
  442.3 2.8 fusion.16
  465.8 3.0 collective-permute-done.16
  468.9 7.1 %collective-permute-done.15 = bf16[2,128,768]{2,1,0:T(8,128)(2,1)S(1)} collective-permute-done((bf16[2,128,768]{2,1,0:T(8,128)(2,1)}, bf16[2,128,768]{2,1,0:T(8,128)(2,1)S(1)}, u32[]{:S(2)}, u32[]{:S(2)}) %collective-permute-start.15) | collective-permute-done | bytes 393248 | tf_op jit(solution)/shard_map/ppermute | solution.py:206
  483.8 3.7 collective-permute-done.28
  489.1 2.8 collective-permute-done.34
  493.5 2.8 collective-permute-done.29
  497.7 2.5 collective-permute-done.35
  501.7 2.5 collective-permute-done.30
  505.8 3.0 collective-permute-done.36
  510.5 3.0 collective-permute-done.31
  522.8 5.3 collective-permute-done.23
  530.5 28.3 %collective-permute-done.24 = bf16[2,2,24,1152]{3,2,0,1:T(8,128)(2,1)S(1)} collective-permute-done((bf16[2,2,24,1152]{3,2,0,1:T(8,128)(2,1)S(1)}, bf16[2,2,24,1152]{3,2,0,1:T(8,128)(2,1)S(1)}, u32[]{:S(2)}, u32[]{:S(2)}) %collective-permute-start.24) | collective-permute-done | bytes 221216 | tf_op jit(solution)/shard_map/ppermute | solution.py:120
  559.3 5.7 collective-permute-done.19
  566.5 3.8 collective-permute-done.25
  571.7 3.9 collective-permute-done.20
  577.3 4.1 collective-permute-done.26
  582.3 4.7 collective-permute-done.21
  (472 shorter events, 175.1 us)
Async XLA Ops:
  7.2 70.3 %all-gather.5.cloned.1.call-start = ((), (), s32[]{:S(2)}) async-start(), calls=%async_computation | async-start | bytes 3649536 | tf_op jit(solution)/shard_map/all_gather | solution.py:231
  7.9 126.5 %all-gather.7.cloned.1.call-start = ((), (), s32[]{:S(2)}) async-start(), calls=%async_computation.1 | async-start | bytes 1216512 | tf_op jit(solution)/shard_map/all_gather | solution.py:234
  8.7 191.1 %all-gather.9.cloned.1.call-start = ((), (), s32[]{:S(2)}) async-start(), calls=%async_computation.2 | async-start | bytes 4866048 | tf_op jit(solution)/shard_map/all_gather | solution.py:235
  9.4 255.0 %all-gather.11.cloned.1.call-start = ((), (), s32[]{:S(2)}) async-start(), calls=%async_computation.3 | async-start | bytes 4866048 | tf_op jit(solution)/shard_map/all_gather | solution.py:236
  11.7 20.0 %collective-permute-start = (bf16[384]{0:T(512)(128)(2,1)S(1)}, bf16[384]{0:T(512)(128)(2,1)S(1)}, u32[]{:S(2)}, u32[]{:S(2)}) collective-permute-start(bf16[384]{0:T(512)(128)(2,1)S(1)} %fusion.71), channel_id=1, source_target_pairs={{0,4},{1,5},{2,6},{3,7},{4,0},{5,1},{6,2},{7,3},{8,12},{9,13},{10,... | collective-permute-start | bytes 2312 | tf_op jit(solution)/shard_map/ppermute | solution.py:120
  18.5 36.8 %collective-permute-start.7 = (bf16[2,128,768]{2,1,0:T(8,128)(2,1)}, bf16[2,128,768]{2,1,0:T(8,128)(2,1)}, u32[]{:S(2)}, u32[]{:S(2)}) collective-permute-start(bf16[2,128,768]{2,1,0:T(8,128)(2,1)} %get-tuple-element.91), channel_id=1, source_target_pairs={{0,24},{8,16},{16,8},{24,0},{1,25},{9,17},{17,9},{25,1},{2,26},{10... | collective-permute-start | bytes 1179656 | tf_op jit(solution)/shard_map/ppermute | solution.py:206
  19.1 36.3 %collective-permute-start.6 = (bf16[2,128,768]{2,1,0:T(8,128)(2,1)}, bf16[2,128,768]{2,1,0:T(8,128)(2,1)}, u32[]{:S(2)}, u32[]{:S(2)}) collective-permute-start(bf16[2,128,768]{2,1,0:T(8,128)(2,1)} %get-tuple-element.92), channel_id=1, source_target_pairs={{0,16},{8,24},{16,0},{24,8},{1,17},{9,25},{17,1},{25,9},{2,18},{10... | collective-permute-start | bytes 1179656 | tf_op jit(solution)/shard_map/ppermute | solution.py:206
  20.0 35.4 %collective-permute-start.5 = (bf16[2,128,768]{2,1,0:T(8,128)(2,1)}, bf16[2,128,768]{2,1,0:T(8,128)(2,1)}, u32[]{:S(2)}, u32[]{:S(2)}) collective-permute-start(bf16[2,128,768]{2,1,0:T(8,128)(2,1)} %get-tuple-element.93), channel_id=1, source_target_pairs={{0,8},{8,0},{16,24},{24,16},{1,9},{9,1},{17,25},{25,17},{2,10},{10... | collective-permute-start | bytes 1179656 | tf_op jit(solution)/shard_map/ppermute | solution.py:206
  21.4 40.3 %collective-permute-start.13 = (bf16[2,128,768]{2,1,0:T(8,128)(2,1)}, bf16[2,128,768]{2,1,0:T(8,128)(2,1)S(1)}, u32[]{:S(2)}, u32[]{:S(2)}) collective-permute-start(bf16[2,128,768]{2,1,0:T(8,128)(2,1)} %get-tuple-element.79), channel_id=1, source_target_pairs={{0,24},{8,16},{16,8},{24,0},{1,25},{9,17},{17,9},{25,1},{2,26},{10... | collective-permute-start | bytes 1179656 | tf_op jit(solution)/shard_map/ppermute | solution.py:206
  39.1 11.9 %collective-permute-start.3 = (bf16[2,2,2,384]{3,0,2,1:T(2,128)(2,1)S(1)}, bf16[2,2,2,384]{3,0,2,1:T(2,128)(2,1)S(1)}, u32[]{:S(2)}, u32[]{:S(2)}) collective-permute-start(bf16[2,2,2,384]{3,0,2,1:T(2,128)(2,1)S(1)} %broadcast_select_fusion.3), channel_id=1, source_target_pairs={{0,16},{16,0},{1,17},{17,1},{2,18},{18,2},{3,19},{19,3},{4,20},{20... | collective-permute-start | bytes 18440 | tf_op jit(solution)/shard_map/ppermute | solution.py:120
  52.3 15.0 %collective-permute-start.12 = (bf16[2,128,768]{2,1,0:T(8,128)(2,1)}, bf16[2,128,768]{2,1,0:T(8,128)(2,1)S(1)}, u32[]{:S(2)}, u32[]{:S(2)}) collective-permute-start(bf16[2,128,768]{2,1,0:T(8,128)(2,1)} %get-tuple-element.80), channel_id=1, source_target_pairs={{0,16},{8,24},{16,0},{24,8},{1,17},{9,25},{17,1},{25,9},{2,18},{10... | collective-permute-start | bytes 1179656 | tf_op jit(solution)/shard_map/ppermute | solution.py:206
  55.3 12.0 %collective-permute-start.11 = (bf16[2,128,768]{2,1,0:T(8,128)(2,1)}, bf16[2,128,768]{2,1,0:T(8,128)(2,1)}, u32[]{:S(2)}, u32[]{:S(2)}) collective-permute-start(bf16[2,128,768]{2,1,0:T(8,128)(2,1)} %get-tuple-element.81), channel_id=1, source_target_pairs={{0,8},{8,0},{16,24},{24,16},{1,9},{9,1},{17,25},{25,17},{2,10},{10... | collective-permute-start | bytes 1179656 | tf_op jit(solution)/shard_map/ppermute | solution.py:206
  343.7 119.6 %collective-permute-start.10 = (bf16[2,128,768]{2,1,0:T(8,128)(2,1)}, bf16[2,128,768]{2,1,0:T(8,128)(2,1)}, u32[]{:S(2)}, u32[]{:S(2)}) collective-permute-start(bf16[2,128,768]{2,1,0:T(8,128)(2,1)} %bitcast.35), channel_id=1, source_target_pairs={{0,24},{8,16},{16,8},{24,0},{1,25},{9,17},{17,9},{25,1},{2,26},{10... | collective-permute-start | bytes 1179656 | tf_op jit(solution)/shard_map/ppermute | solution.py:206
  345.0 118.6 %collective-permute-start.9 = (bf16[2,128,768]{2,1,0:T(8,128)(2,1)}, bf16[2,128,768]{2,1,0:T(8,128)(2,1)}, u32[]{:S(2)}, u32[]{:S(2)}) collective-permute-start(bf16[2,128,768]{2,1,0:T(8,128)(2,1)} %bitcast.33), channel_id=1, source_target_pairs={{0,16},{8,24},{16,0},{24,8},{1,17},{9,25},{17,1},{25,9},{2,18},{10... | collective-permute-start | bytes 1179656 | tf_op jit(solution)/shard_map/ppermute | solution.py:206
  345.6 118.5 %collective-permute-start.8 = (bf16[2,128,768]{2,1,0:T(8,128)(2,1)}, bf16[2,128,768]{2,1,0:T(8,128)(2,1)}, u32[]{:S(2)}, u32[]{:S(2)}) collective-permute-start(bf16[2,128,768]{2,1,0:T(8,128)(2,1)} %bitcast.31), channel_id=1, source_target_pairs={{0,8},{8,0},{16,24},{24,16},{1,9},{9,1},{17,25},{25,17},{2,10},{10... | collective-permute-start | bytes 1179656 | tf_op jit(solution)/shard_map/ppermute | solution.py:206
  372.5 87.2 %collective-permute-start.32 = (bf16[2,2,2,2,24,384]{5,4,1,2,0,3:T(8,128)(2,1)}, bf16[2,2,2,2,24,384]{5,4,1,2,0,3:T(8,128)(2,1)}, u32[]{:S(2)}, u32[]{:S(2)}) collective-permute-start(bf16[2,2,2,2,24,384]{5,4,1,2,0,3:T(8,128)(2,1)} %fusion.33), channel_id=1, source_target_pairs={{0,8},{8,0},{1,9},{9,1},{2,10},{10,2},{3,11},{11,3},{4,12},{12,4},... | collective-permute-start | bytes 884744 | tf_op jit(solution)/shard_map/ppermute | solution.py:120
  404.0 36.0 %collective-permute-start.37 = (f32[2,2,2,2,384]{4,3,2,1,0:T(2,128)}, f32[2,2,2,2,384]{4,3,2,1,0:T(2,128)}, u32[]{:S(2)}, u32[]{:S(2)}) collective-permute-start(f32[2,2,2,2,384]{4,3,2,1,0:T(2,128)} %fusion.56), channel_id=1, source_target_pairs={{0,8},{8,0},{1,9},{9,1},{2,10},{10,2},{3,11},{11,3},{4,12},{12,4},... | collective-permute-start | bytes 73736 | tf_op jit(solution)/shard_map/ppermute | solution.py:120
  457.1 11.7 %collective-permute-start.16 = (bf16[2,128,768]{2,1,0:T(8,128)(2,1)}, bf16[2,128,768]{2,1,0:T(8,128)(2,1)}, u32[]{:S(2)}, u32[]{:S(2)}) collective-permute-start(bf16[2,128,768]{2,1,0:T(8,128)(2,1)} %bitcast.61), channel_id=1, source_target_pairs={{0,24},{8,16},{16,8},{24,0},{1,25},{9,17},{17,9},{25,1},{2,26},{10... | collective-permute-start | bytes 1179656 | tf_op jit(solution)/shard_map/ppermute | solution.py:206
  462.1 13.9 %collective-permute-start.15 = (bf16[2,128,768]{2,1,0:T(8,128)(2,1)}, bf16[2,128,768]{2,1,0:T(8,128)(2,1)S(1)}, u32[]{:S(2)}, u32[]{:S(2)}) collective-permute-start(bf16[2,128,768]{2,1,0:T(8,128)(2,1)} %bitcast.411), channel_id=1, source_target_pairs={{0,16},{8,24},{16,0},{24,8},{1,17},{9,25},{17,1},{25,9},{2,18},{10... | collective-permute-start | bytes 1179656 | tf_op jit(solution)/shard_map/ppermute | solution.py:206
  463.4 13.1 %collective-permute-start.14 = (bf16[2,128,768]{2,1,0:T(8,128)(2,1)S(1)}, bf16[2,128,768]{2,1,0:T(8,128)(2,1)S(1)}, u32[]{:S(2)}, u32[]{:S(2)}) collective-permute-start(bf16[2,128,768]{2,1,0:T(8,128)(2,1)S(1)} %bitcast.410), channel_id=1, source_target_pairs={{0,8},{8,0},{16,24},{24,16},{1,9},{9,1},{17,25},{25,17},{2,10},{10... | collective-permute-start | bytes 1179656 | tf_op jit(solution)/shard_map/ppermute | solution.py:206
  463.6 50.6 %collective-permute-start.22 = (bf16[2,2,2,2,24,1152]{5,4,1,2,0,3:T(8,128)(2,1)S(1)}, bf16[2,2,2,2,24,1152]{5,4,1,2,0,3:T(8,128)(2,1)S(1)}, u32[]{:S(2)}, u32[]{:S(2)}) collective-permute-start(bf16[2,2,2,2,24,1152]{5,4,1,2,0,3:T(8,128)(2,1)S(1)} %copy-done.31), channel_id=1, source_target_pairs={{0,8},{8,0},{1,9},{9,1},{2,10},{10,2},{3,11},{11,3},{4,12},{12,4},... | collective-permute-start | bytes 2654216 | tf_op jit(solution)/shard_map/ppermute | solution.py:120
  464.0 50.9 %collective-permute-start.17 = (bf16[2,2,2,2,24,1152]{5,4,1,2,3,0:T(8,128)(2,1)S(1)}, bf16[2,2,2,2,24,1152]{5,4,1,2,3,0:T(8,128)(2,1)S(1)}, u32[]{:S(2)}, u32[]{:S(2)}) collective-permute-start(bf16[2,2,2,2,24,1152]{5,4,1,2,3,0:T(8,128)(2,1)S(1)} %copy-done.30), channel_id=1, source_target_pairs={{0,8},{8,0},{1,9},{9,1},{2,10},{10,2},{3,11},{11,3},{4,12},{12,4},... | collective-permute-start | bytes 2654216 | tf_op jit(solution)/shard_map/ppermute | solution.py:120
  468.9 48.0 %collective-permute-start.47 = (bf16[2,2,2,2,24,1536]{5,4,1,2,0,3:T(8,128)(2,1)S(1)}, bf16[2,2,2,2,24,1536]{5,4,1,2,0,3:T(8,128)(2,1)S(1)}, u32[]{:S(2)}, u32[]{:S(2)}) collective-permute-start(bf16[2,2,2,2,24,1536]{5,4,1,2,0,3:T(8,128)(2,1)S(1)} %copy-done.26), channel_id=1, source_target_pairs={{0,8},{8,0},{1,9},{9,1},{2,10},{10,2},{3,11},{11,3},{4,12},{12,4},... | collective-permute-start | bytes 3538952 | tf_op jit(solution)/shard_map/ppermute | solution.py:120
  476.0 41.8 %collective-permute-start.42 = (bf16[2,2,2,2,24,1536]{5,4,3,2,1,0:T(8,128)(2,1)S(1)}, bf16[2,2,2,2,24,1536]{5,4,3,2,1,0:T(8,128)(2,1)S(1)}, u32[]{:S(2)}, u32[]{:S(2)}) collective-permute-start(bf16[2,2,2,2,24,1536]{5,4,3,2,1,0:T(8,128)(2,1)S(1)} %copy-done.27), channel_id=1, source_target_pairs={{0,8},{8,0},{1,9},{9,1},{2,10},{10,2},{3,11},{11,3},{4,12},{12,4},... | collective-permute-start | bytes 3538952 | tf_op jit(solution)/shard_map/ppermute | solution.py:120
  476.4 5.9 collective-permute-start.33
  513.5 6.4 %collective-permute-start.57 = (bf16[2,2,2,2,96,384]{5,4,1,2,0,3:T(8,128)(2,1)S(1)}, bf16[2,2,2,2,96,384]{5,4,1,2,0,3:T(8,128)(2,1)S(1)}, u32[]{:S(2)}, u32[]{:S(2)}) collective-permute-start(bf16[2,2,2,2,96,384]{5,4,1,2,0,3:T(8,128)(2,1)S(1)} %copy-done.28), channel_id=1, source_target_pairs={{0,8},{8,0},{1,9},{9,1},{2,10},{10,2},{3,11},{11,3},{4,12},{12,4},... | collective-permute-start | bytes 3538952 | tf_op jit(solution)/shard_map/ppermute | solution.py:120
  514.2 6.7 %collective-permute-start.52 = (bf16[2,2,2,2,96,384]{5,4,1,2,3,0:T(8,128)(2,1)S(1)}, bf16[2,2,2,2,96,384]{5,4,1,2,3,0:T(8,128)(2,1)S(1)}, u32[]{:S(2)}, u32[]{:S(2)}) collective-permute-start(bf16[2,2,2,2,96,384]{5,4,1,2,3,0:T(8,128)(2,1)S(1)} %copy-done.29), channel_id=1, source_target_pairs={{0,8},{8,0},{1,9},{9,1},{2,10},{10,2},{3,11},{11,3},{4,12},{12,4},... | collective-permute-start | bytes 3538952 | tf_op jit(solution)/shard_map/ppermute | solution.py:120
  515.0 13.1 %collective-permute-start.23 = (bf16[2,2,2,24,1152]{4,3,1,2,0:T(8,128)(2,1)S(1)}, bf16[2,2,2,24,1152]{4,3,1,2,0:T(8,128)(2,1)S(1)}, u32[]{:S(2)}, u32[]{:S(2)}) collective-permute-start(bf16[2,2,2,24,1152]{4,3,1,2,0:T(8,128)(2,1)S(1)} %fusion.27), channel_id=1, source_target_pairs={{0,1},{1,0},{2,3},{3,2},{4,5},{5,4},{6,7},{7,6},{8,9},{9,8},{10,11... | collective-permute-start | bytes 1327112 | tf_op jit(solution)/shard_map/ppermute | solution.py:120
  516.8 13.1 %collective-permute-start.18 = (bf16[2,2,2,24,1152]{4,3,0,1,2:T(8,128)(2,1)S(1)}, bf16[2,2,2,24,1152]{4,3,0,1,2:T(8,128)(2,1)S(1)}, u32[]{:S(2)}, u32[]{:S(2)}) collective-permute-start(bf16[2,2,2,24,1152]{4,3,0,1,2:T(8,128)(2,1)S(1)} %fusion.26), channel_id=1, source_target_pairs={{0,16},{16,0},{1,17},{17,1},{2,18},{18,2},{3,19},{19,3},{4,20},{20... | collective-permute-start | bytes 1327112 | tf_op jit(solution)/shard_map/ppermute | solution.py:120
  517.8 69.9 %collective-permute-start.48 = (bf16[2,2,2,24,1536]{4,3,1,2,0:T(8,128)(2,1)S(1)}, bf16[2,2,2,24,1536]{4,3,1,2,0:T(8,128)(2,1)S(1)}, u32[]{:S(2)}, u32[]{:S(2)}) collective-permute-start(bf16[2,2,2,24,1536]{4,3,1,2,0:T(8,128)(2,1)S(1)} %fusion.23), channel_id=1, source_target_pairs={{0,1},{1,0},{2,3},{3,2},{4,5},{5,4},{6,7},{7,6},{8,9},{9,8},{10,11... | collective-permute-start | bytes 1769480 | tf_op jit(solution)/shard_map/ppermute | solution.py:120
  519.9 68.5 %collective-permute-start.43 = (bf16[2,2,2,24,1536]{4,3,2,1,0:T(8,128)(2,1)S(1)}, bf16[2,2,2,24,1536]{4,3,2,1,0:T(8,128)(2,1)S(1)}, u32[]{:S(2)}, u32[]{:S(2)}) collective-permute-start(bf16[2,2,2,24,1536]{4,3,2,1,0:T(8,128)(2,1)S(1)} %fusion.22), channel_id=1, source_target_pairs={{0,16},{16,0},{1,17},{17,1},{2,18},{18,2},{3,19},{19,3},{4,20},{20... | collective-permute-start | bytes 1769480 | tf_op jit(solution)/shard_map/ppermute | solution.py:120
  520.8 69.4 %collective-permute-start.58 = (bf16[2,2,2,96,384]{4,3,1,2,0:T(8,128)(2,1)S(1)}, bf16[2,2,2,96,384]{4,3,1,2,0:T(8,128)(2,1)S(1)}, u32[]{:S(2)}, u32[]{:S(2)}) collective-permute-start(bf16[2,2,2,96,384]{4,3,1,2,0:T(8,128)(2,1)S(1)} %fusion.25), channel_id=1, source_target_pairs={{0,1},{1,0},{2,3},{3,2},{4,5},{5,4},{6,7},{7,6},{8,9},{9,8},{10,11... | collective-permute-start | bytes 1769480 | tf_op jit(solution)/shard_map/ppermute | solution.py:120
  528.1 62.9 %collective-permute-start.53 = (bf16[2,2,2,96,384]{4,3,0,1,2:T(8,128)(2,1)S(1)}, bf16[2,2,2,96,384]{4,3,0,1,2:T(8,128)(2,1)S(1)}, u32[]{:S(2)}, u32[]{:S(2)}) collective-permute-start(bf16[2,2,2,96,384]{4,3,0,1,2:T(8,128)(2,1)S(1)} %fusion.24), channel_id=1, source_target_pairs={{0,16},{16,0},{1,17},{17,1},{2,18},{18,2},{3,19},{19,3},{4,20},{20... | collective-permute-start | bytes 1769480 | tf_op jit(solution)/shard_map/ppermute | solution.py:120
  530.0 28.8 %collective-permute-start.24 = (bf16[2,2,24,1152]{3,2,0,1:T(8,128)(2,1)S(1)}, bf16[2,2,24,1152]{3,2,0,1:T(8,128)(2,1)S(1)}, u32[]{:S(2)}, u32[]{:S(2)}) collective-permute-start(bf16[2,2,24,1152]{3,2,0,1:T(8,128)(2,1)S(1)} %fusion.35), channel_id=1, source_target_pairs={{0,16},{16,0},{1,17},{17,1},{2,18},{18,2},{3,19},{19,3},{4,20},{20... | collective-permute-start | bytes 663560 | tf_op jit(solution)/shard_map/ppermute | solution.py:120
  558.8 6.2 %collective-permute-start.19 = (bf16[2,2,24,1152]{3,2,0,1:T(8,128)(2,1)S(1)}, bf16[2,2,24,1152]{3,2,0,1:T(8,128)(2,1)S(1)}, u32[]{:S(2)}, u32[]{:S(2)}) collective-permute-start(bf16[2,2,24,1152]{3,2,0,1:T(8,128)(2,1)S(1)} %fusion.34), channel_id=1, source_target_pairs={{0,1},{1,0},{2,3},{3,2},{4,5},{5,4},{6,7},{7,6},{8,9},{9,8},{10,11... | collective-permute-start | bytes 663560 | tf_op jit(solution)/shard_map/ppermute | solution.py:120
  575.6 5.8 collective-permute-start.26
  581.4 5.6 collective-permute-start.21
  587.9 6.8 %collective-permute-start.49 = (bf16[2,2,24,1536]{3,2,0,1:T(8,128)(2,1)S(1)}, bf16[2,2,24,1536]{3,2,0,1:T(8,128)(2,1)S(1)}, u32[]{:S(2)}, u32[]{:S(2)}) collective-permute-start(bf16[2,2,24,1536]{3,2,0,1:T(8,128)(2,1)S(1)} %fusion.29), channel_id=1, source_target_pairs={{0,16},{16,0},{1,17},{17,1},{2,18},{18,2},{3,19},{19,3},{4,20},{20... | collective-permute-start | bytes 884744 | tf_op jit(solution)/shard_map/ppermute | solution.py:120
  588.6 6.8 %collective-permute-start.44 = (bf16[2,2,24,1536]{3,2,1,0:T(8,128)(2,1)S(1)}, bf16[2,2,24,1536]{3,2,1,0:T(8,128)(2,1)S(1)}, u32[]{:S(2)}, u32[]{:S(2)}) collective-permute-start(bf16[2,2,24,1536]{3,2,1,0:T(8,128)(2,1)S(1)} %fusion.28), channel_id=1, source_target_pairs={{0,1},{1,0},{2,3},{3,2},{4,5},{5,4},{6,7},{7,6},{8,9},{9,8},{10,11... | collective-permute-start | bytes 884744 | tf_op jit(solution)/shard_map/ppermute | solution.py:120
  590.4 7.5 %collective-permute-start.59 = (bf16[2,2,96,384]{3,2,0,1:T(8,128)(2,1)S(1)}, bf16[2,2,96,384]{3,2,0,1:T(8,128)(2,1)S(1)}, u32[]{:S(2)}, u32[]{:S(2)}) collective-permute-start(bf16[2,2,96,384]{3,2,0,1:T(8,128)(2,1)S(1)} %fusion.31), channel_id=1, source_target_pairs={{0,16},{16,0},{1,17},{17,1},{2,18},{18,2},{3,19},{19,3},{4,20},{20... | collective-permute-start | bytes 884744 | tf_op jit(solution)/shard_map/ppermute | solution.py:120
  591.1 7.4 %collective-permute-start.54 = (bf16[2,2,96,384]{3,2,0,1:T(8,128)(2,1)S(1)}, bf16[2,2,96,384]{3,2,0,1:T(8,128)(2,1)S(1)}, u32[]{:S(2)}, u32[]{:S(2)}) collective-permute-start(bf16[2,2,96,384]{3,2,0,1:T(8,128)(2,1)S(1)} %fusion.30), channel_id=1, source_target_pairs={{0,1},{1,0},{2,3},{3,2},{4,5},{5,4},{6,7},{7,6},{8,9},{9,8},{10,11... | collective-permute-start | bytes 884744 | tf_op jit(solution)/shard_map/ppermute | solution.py:120
  594.8 6.8 %collective-permute-start.50 = (bf16[2,24,1536]{2,1,0:T(8,128)(2,1)S(1)}, bf16[2,24,1536]{2,1,0:T(8,128)(2,1)S(1)}, u32[]{:S(2)}, u32[]{:S(2)}) collective-permute-start(bf16[2,24,1536]{2,1,0:T(8,128)(2,1)S(1)} %fusion.39), channel_id=1, source_target_pairs={{0,2},{1,3},{2,0},{3,1},{4,6},{5,7},{6,4},{7,5},{8,10},{9,11},{10,... | collective-permute-start | bytes 442376 | tf_op jit(solution)/shard_map/ppermute | solution.py:120
  595.5 7.7 %collective-permute-start.45 = (bf16[2,24,1536]{2,1,0:T(8,128)(2,1)S(1)}, bf16[2,24,1536]{2,1,0:T(8,128)(2,1)S(1)}, u32[]{:S(2)}, u32[]{:S(2)}) collective-permute-start(bf16[2,24,1536]{2,1,0:T(8,128)(2,1)S(1)} %fusion.38), channel_id=1, source_target_pairs={{0,2},{1,3},{2,0},{3,1},{4,6},{5,7},{6,4},{7,5},{8,10},{9,11},{10,... | collective-permute-start | bytes 442376 | tf_op jit(solution)/shard_map/ppermute | solution.py:120
  598.0 6.8 %collective-permute-start.60 = (bf16[2,96,384]{2,1,0:T(8,128)(2,1)S(1)}, bf16[2,96,384]{2,1,0:T(8,128)(2,1)S(1)}, u32[]{:S(2)}, u32[]{:S(2)}) collective-permute-start(bf16[2,96,384]{2,1,0:T(8,128)(2,1)S(1)} %fusion.41), channel_id=1, source_target_pairs={{0,2},{1,3},{2,0},{3,1},{4,6},{5,7},{6,4},{7,5},{8,10},{9,11},{10,... | collective-permute-start | bytes 442376 | tf_op jit(solution)/shard_map/ppermute | solution.py:120
  598.6 7.7 %collective-permute-start.55 = (bf16[2,96,384]{2,1,0:T(8,128)(2,1)S(1)}, bf16[2,96,384]{2,1,0:T(8,128)(2,1)S(1)}, u32[]{:S(2)}, u32[]{:S(2)}) collective-permute-start(bf16[2,96,384]{2,1,0:T(8,128)(2,1)S(1)} %fusion.40), channel_id=1, source_target_pairs={{0,2},{1,3},{2,0},{3,1},{4,6},{5,7},{6,4},{7,5},{8,10},{9,11},{10,... | collective-permute-start | bytes 442376 | tf_op jit(solution)/shard_map/ppermute | solution.py:120
  601.6 6.4 %collective-permute-start.51 = (bf16[24,1536]{1,0:T(8,128)(2,1)S(1)}, bf16[24,1536]{1,0:T(8,128)(2,1)S(1)}, u32[]{:S(2)}, u32[]{:S(2)}) collective-permute-start(bf16[24,1536]{1,0:T(8,128)(2,1)S(1)} %fusion.47), channel_id=1, source_target_pairs={{0,4},{1,5},{2,6},{3,7},{4,0},{5,1},{6,2},{7,3},{8,12},{9,13},{10,... | collective-permute-start | bytes 221192 | tf_op jit(solution)/shard_map/ppermute | solution.py:120
  603.2 5.6 collective-permute-start.46
  606.4 6.1 collective-permute-start.56
  (82 other events, 652.3 us)
Sparse Core Ops, SparseCore 0:
  10.9 66.5 all-gather.4
  80.4 53.9 all-gather.6
  137.4 62.3 all-gather.8
  202.6 61.8 all-gather.10

commit v2 on v1

--- a/solution.py
+++ b/solution.py
@@ -115,13 +115,8 @@
     )(queries, keys, values, grad_mixed, logs)
 
 
-def swap(array, axis_name, bit):
-    size = lax.axis_size(axis_name)
-    return lax.ppermute(array, axis_name, [(i, i ^ bit) for i in range(size)])
-
-
-def bit_of(axis_name, bit):
-    return (lax.axis_index(axis_name) // bit) % 2
+def after(array, *earlier):
+    return lax.optimization_barrier((array,) + earlier)[0]
 
 
 def device_bits():
@@ -134,30 +129,80 @@
     return bits
 
 
-def scatter_sum(part, order, send_type=BF16):
-    left = device_bits()
-    array = part.reshape((2,) * len(left) + part.shape[1:])
-    for step in order:
-        axis = left.index(step)
-        mine = bit_of(*step)
-        keep = lax.dynamic_index_in_dim(array, mine, axis, False)
-        send = lax.dynamic_index_in_dim(array, 1 - mine, axis, False).astype(send_type)
-        array = keep + swap(send, *step).astype(F32)
-        left.pop(axis)
-    return array
-
-
-def gather_all(shard, order):
+def make_stages(bits):
+    core = [b for b in bits if b[0] == "core"]
+    clip = [b for b in bits if b[0] == "clip"][::-1]
+    plane = [b for b in bits if b[0] == "sx"] + clip[:1]
+    stages = [core, plane] + [clip[i : i + 2] for i in range(1, len(clip), 2)]
+    return [sorted(stage, key=bits.index) for stage in stages]
+
+
+def partners(stage):
+    count = len(stage)
+    return [[(k >> i) & 1 for i in range(count)] for k in range(1, 1 << count)]
+
+
+def send_to(array, stage, flags):
+    axes = tuple(dict.fromkeys(step[0] for step in stage))
+    sizes = [lax.axis_size(name) for name in axes]
+    flip = [sum(s[1] for s, f in zip(stage, flags) if f and s[0] == name) for name in axes]
+    total = math.prod(sizes)
+    if len(axes) == 1:
+        return lax.ppermute(array, axes[0], [(i, i ^ flip[0]) for i in range(total)])
+    pairs = [(i, (i // sizes[1] ^ flip[0]) * sizes[1] + (i % sizes[1] ^ flip[1])) for i in range(total)]
+    return lax.ppermute(array, axes, pairs)
+
+
+def own_bit(step):
+    return (lax.axis_index(step[0]) // step[1]) % 2
+
+
+class Reduction:
+    def __init__(self, part, send_type=BF16):
+        self.left = device_bits()
+        self.stages = make_stages(self.left)
+        self.array = part.reshape((2,) * len(self.left) + part.shape[1:])
+        self.send_type = send_type
+
+    def pick(self, array, stage, flags):
+        left = list(self.left)
+        for step, flag in zip(stage, flags):
+            axis = left.index(step)
+            array = lax.dynamic_index_in_dim(array, own_bit(step) ^ flag, axis, False)
+            left.pop(axis)
+        return array
+
+    def send(self):
+        stage = self.stages.pop(0)
+        sent = [self.pick(self.array, stage, f).astype(self.send_type) for f in partners(stage)]
+        self.array = self.pick(self.array, stage, [0] * len(stage))
+        self.left = [step for step in self.left if step not in stage]
+        self.got = [send_to(array, stage, f) for array, f in zip(sent, partners(stage))]
+        return sent
+
+    def add(self, *earlier):
+        got = self.got
+        if earlier:
+            got = lax.optimization_barrier(tuple(got) + earlier)[: len(got)]
+        for array in got:
+            self.array = self.array + array.astype(F32)
+
+
+def gather_all(shard):
     bits = device_bits()
     array, have = shard, []
-    for step in order:
-        other = swap(array, *step)
-        have = sorted(have + [step], key=bits.index)
-        axis = have.index(step)
-        mine = bit_of(*step)
-        both = jnp.stack([array, other], axis=axis)
-        flip = jnp.stack([other, array], axis=axis)
-        array = jnp.where(mine == 0, both, flip)
+    for stage in make_stages(bits)[::-1]:
+        blocks = [([0] * len(stage), array)]
+        blocks += [(f, send_to(array, stage, f)) for f in partners(stage)]
+        have = sorted(have + stage, key=bits.index)
+        axes = [have.index(step) for step in stage]
+        array = jnp.expand_dims(array, axes)
+        shape = tuple(2 if i in axes else 1 for i in range(array.ndim))
+        for flags, block in blocks[1:]:
+            here = jnp.full(shape, True)
+            for step, flag, axis in zip(stage, flags, axes):
+                here &= lax.broadcasted_iota(jnp.int32, shape, axis) == (own_bit(step) ^ flag)
+            array = jnp.where(here, jnp.expand_dims(block, axes), array)
     return array.reshape((-1,) + shard.shape)
 
 
@@ -193,14 +238,6 @@
     row_total = seq_size * own_clips * local_len
     grid_shape = (seq_size, own_clips, local_len, width)
 
-    bits = device_bits()
-    clip_bits = [b for b in bits if b[0] == "clip"]
-    other_bits = [b for b in bits if b[0] == "sx"]
-    core_bits = [b for b in bits if b[0] == "core"]
-    low_first = clip_bits[::-1]
-    order_a = core_bits + other_bits + low_first
-    order_b = core_bits + low_first[:1] + other_bits + low_first[1:]
-
     def trade(chunks):
         return [chunks[0]] + [
             lax.ppermute(chunks[k], seq_names, [(i, i ^ k) for i in range(seq_size)])
@@ -220,25 +257,27 @@
         order = [lax.dynamic_index_in_dim(got, seq_here ^ k, 0, False) for k in range(seq_size)]
         return jnp.stack(order).reshape(patches.shape)
 
-    share = width // devices
-    up_share = up_bias.shape[0]
-    small = jnp.concatenate([mask_embed, gains.reshape(-1), biases.reshape(-1), up_bias])
-    small_size = small.shape[0]
-    small_padded = -(-small_size // 128) * 128
-    small = jnp.pad(small, (0, small_padded - small_size))
-    small_all = gather_all(small, clip_bits + other_bits + core_bits)
-
-    full_qkv = lax.all_gather(w_qkv, ALL, axis=0, tiled=True)
+    share = w_qkv.shape[0]
+    spread = up_bias.shape[0] // share
+    small = jnp.concatenate([mask_embed[None], gains, biases, up_bias.reshape(spread, share)], axis=0)
+    small = jnp.pad(small, ((0, 128 - small.shape[0]), (0, 0))).T
     patch_rows = rows_in(patches)
-    grad_final = rows_in(cotangent)
-    full_out = lax.all_gather(w_out, ALL, axis=0, tiled=True)
-    full_up = lax.all_gather(w_up, ALL, axis=0, tiled=True)
-    full_down = lax.all_gather(w_down, ALL, axis=0, tiled=True)
-
-    small_rows = small_all[:, : 9 * share].astype(F32).reshape(devices, 9, share)
-    small_rows = small_rows.transpose(1, 0, 2).reshape(9, width)
+    first_all = gather_all(jnp.concatenate([w_qkv, small], axis=1)).reshape(width, -1)
+    full_qkv = first_all[:, : 3 * width]
+    small_rows = first_all[:, 3 * width :].astype(F32).T
     mask_vector, gain_rows, bias_rows = small_rows[0], small_rows[1:3], small_rows[3:9]
-    up_shift = small_all[:, 9 * share : small_size].astype(F32).reshape(-1)
+    up_shift = small_rows[9 : 9 + spread].reshape(spread, devices, share)
+    up_shift = up_shift.transpose(1, 0, 2).reshape(-1)
+
+    others = [w_out] + [w_up[:, j * width : (j + 1) * width] for j in range(spread)] + [w_down]
+    others_all = lax.all_gather(jnp.concatenate(others, axis=0), ALL, axis=0)
+
+    def other_rows(block):
+        return others_all[:, block * share : (block + 1) * share].reshape(width, width)
+
+    full_out = other_rows(0)
+    full_up = jnp.concatenate([other_rows(1 + j) for j in range(spread)], axis=1)
+    full_down = others_all[:, (1 + spread) * share :].reshape(spread * width, width)
 
     slot_ids = lax.broadcasted_iota(jnp.int32, (seq_size, freq_rows, time_local), 0)
     freq_ids = lax.broadcasted_iota(jnp.int32, (seq_size, freq_rows, time_local), 1)
@@ -256,10 +295,11 @@
     start_rows = jnp.where(masked, mask_vector, patch_rows.astype(F32))
     normed_one, norm_pull_one = jax.vjp(layer_norm, start_rows, gain_rows[0], bias_rows[0])
     normed_low = normed_one.astype(BF16)
-    joined = jnp.dot(normed_low, full_qkv, preferred_element_type=F32)
+    grad_final = rows_in(after(cotangent, normed_low))
+    joined = jnp.dot(normed_low, first_all, preferred_element_type=F32)
     queries = (joined[:, :width] + bias_rows[1]).astype(BF16).reshape(grid_shape)
     keys = joined[:, width : 2 * width].astype(BF16).reshape(grid_shape)
-    values = (joined[:, 2 * width :] + bias_rows[2]).astype(BF16).reshape(grid_shape)
+    values = (joined[:, 2 * width : 3 * width] + bias_rows[2]).astype(BF16).reshape(grid_shape)
     mixed, logs = attend_forward(queries, keys, values, H)
     mixed_flat = mixed.reshape(row_total, width)
     middle = start_rows + (jnp.dot(mixed_flat, full_out, preferred_element_type=F32) + bias_rows[3])
@@ -268,50 +308,76 @@
     upper_rows = jnp.dot(second_low, full_up, preferred_element_type=F32) + up_shift
     active, gelu_pull = jax.vjp(exact_gelu, upper_rows)
     active_low = active.astype(BF16)
-    final_rows = middle + (jnp.dot(active_low, full_down, preferred_element_type=F32) + bias_rows[5])
-    activations = rows_out(final_rows.astype(BF16))
 
     def by_owner(part):
         return part.reshape(devices, -1, part.shape[1])
 
-    def send_grad(part):
-        half = part.shape[1] // 2
-        part = by_owner(part)
-        return jnp.concatenate(
-            [scatter_sum(part[..., :half], order_a), scatter_sum(part[..., half:], order_b)], axis=1
-        )
-
-    grad_down = send_grad(dot(active_low, grad_final, 0, 0))
-    grad_down_bias = jnp.sum(grad_final.astype(F32), axis=0)
-    grad_active = dot(grad_final, full_down, 1, 1)
+    down_sum = Reduction(by_owner(dot(active_low, grad_final, 0, 0)))
+    sent = down_sum.send()
+    (grad_final_b,) = (after(grad_final, *sent),)
+    grad_active = dot(grad_final_b, full_down, 1, 1)
     (grad_upper,) = gelu_pull(grad_active)
     grad_upper_low = grad_upper.astype(BF16)
-    grad_up = send_grad(dot(second_low, grad_upper_low, 0, 0))
+    down_sum.add(grad_upper_low)
+    sent = down_sum.send()
+    up_sum = Reduction(by_owner(dot(after(second_low, *sent), grad_upper_low, 0, 0)))
+    sent = up_sum.send()
     grad_up_shift = jnp.sum(grad_upper_low.astype(F32), axis=0)
-    grad_second = dot(grad_upper_low, full_up, 1, 1)
+    grad_second = dot(after(grad_upper_low, *sent), full_up, 1, 1)
     grad_mid_norm, grad_gain_two, grad_bias_two = norm_pull_two(grad_second)
     grad_middle = grad_final.astype(F32) + grad_mid_norm
     grad_branch = grad_middle.astype(BF16)
-    grad_out = send_grad(dot(mixed_flat, grad_branch, 0, 0))
+    up_sum.add(grad_branch)
+    sent = up_sum.send()
+    out_sum = Reduction(by_owner(dot(mixed_flat, after(grad_branch, *sent), 0, 0)))
+    sent = out_sum.send()
     grad_out_bias = jnp.sum(grad_branch.astype(F32), axis=0)
-    grad_mixed = dot(grad_branch, full_out, 1, 1).astype(BF16).reshape(grid_shape)
-    groups = 3
+    grad_mixed = dot(after(grad_branch, *sent), full_out, 1, 1).astype(BF16).reshape(grid_shape)
+    final_rows = middle + (jnp.dot(active_low, full_down, preferred_element_type=F32) + bias_rows[5])
+    activations = rows_out(after(final_rows.astype(BF16), grad_mixed))
+
+    groups = 2
     per_group = width // 128 // groups
-    pieces = [
-        attend_backward(queries, keys, values, grad_mixed, logs, H, g * per_group, per_group)
-        for g in range(groups)
-    ]
-    grad_joined = jnp.concatenate(
-        [p[i].reshape(row_total, -1) for i in range(3) for p in pieces], axis=1
-    )
-    grad_qkv = send_grad(dot(normed_low, grad_joined, 0, 0))
-    grad_query_bias = jnp.sum(grad_joined[:, :width].astype(F32), axis=0)
-    grad_value_bias = jnp.sum(grad_joined[:, 2 * width :].astype(F32), axis=0)
-    grad_first = dot(grad_joined, full_qkv, 1, 1)
+    group_width = width // groups
+    qkv_sums, joined_pieces = [], []
+    for g in range(groups):
+        piece = attend_backward(queries, keys, values, grad_mixed, logs, H, g * per_group, per_group)
+        piece = jnp.concatenate([p.reshape(row_total, -1) for p in piece], axis=1)
+        joined_pieces.append(piece)
+        if g == 0:
+            out_sum.add(piece)
+            sent = out_sum.send()
+            down_sum.add(piece)
+            sent += down_sum.send()
+            qkv_sums.append(Reduction(by_owner(dot(after(normed_low, *sent), piece, 0, 0))))
+            sent = qkv_sums[0].send()
+            grad_mixed = after(grad_mixed, *sent)
+        else:
+            up_sum.add(piece)
+            sent = up_sum.send()
+            qkv_sums[0].add(piece)
+            sent += qkv_sums[0].send()
+            qkv_sums.append(Reduction(by_owner(dot(after(normed_low, *sent), piece, 0, 0))))
+            sent = qkv_sums[1].send()
+    grad_first = 0.0
+    for g in range(groups):
+        cols = [slice(i * width + g * group_width, i * width + (g + 1) * group_width) for i in range(3)]
+        weight = jnp.concatenate([full_qkv[:, c] for c in cols], axis=1)
+        grad_first = grad_first + dot(after(joined_pieces[g], *sent), weight, 1, 1)
+    grad_query_bias = jnp.concatenate(
+        [jnp.sum(p[:, :group_width].astype(F32), axis=0) for p in joined_pieces]
+    )
+    grad_value_bias = jnp.concatenate(
+        [jnp.sum(p[:, 2 * group_width :].astype(F32), axis=0) for p in joined_pieces]
+    )
     grad_start_norm, grad_gain_one, grad_bias_one = norm_pull_one(grad_first)
     grad_start = grad_middle + grad_start_norm
-    input_grad = rows_out(jnp.where(masked, 0.0, grad_start).astype(BF16))
+    input_low = jnp.where(masked, 0.0, grad_start).astype(BF16)
+    qkv_sums[1].add(input_low)
+    qkv_sums[1].send()
+    input_grad = rows_out(input_low)
     grad_mask_part = jnp.sum(jnp.where(masked, grad_start, 0.0), axis=0)
+    grad_down_bias = jnp.sum(grad_final.astype(F32), axis=0)
     small_grads = jnp.stack(
         [
             grad_mask_part,
@@ -325,11 +391,24 @@
             grad_down_bias,
         ]
     )
-    small_grads = small_grads.reshape(9, devices, share).transpose(1, 0, 2).reshape(devices, -1)
-    small_grads = jnp.concatenate([small_grads, grad_up_shift.reshape(devices, up_share)], axis=1)
-    small_grads = jnp.pad(small_grads, ((0, 0), (0, small_padded - small_size)))
-    small_sum = scatter_sum(small_grads, order_a, F32)
-    own_rows = small_sum[: 9 * share].reshape(9, share)
+    up_rows = grad_up_shift.reshape(devices, spread, share).transpose(1, 0, 2).reshape(spread, width)
+    small_grads = jnp.concatenate([small_grads, up_rows], axis=0)
+    small_grads = jnp.pad(small_grads, ((0, 128 - 9 - spread), (0, 0))).T
+    small_sum = Reduction(by_owner(small_grads), F32)
+    small_sum.send()
+    for rest in (down_sum, out_sum, up_sum, qkv_sums[0], qkv_sums[1], small_sum):
+        while True:
+            rest.add()
+            if not rest.stages:
+                break
+            rest.send()
+    grad_down = down_sum.array.reshape(w_down.shape)
+    grad_up = up_sum.array.reshape(w_up.shape)
+    grad_out = out_sum.array.reshape(w_out.shape)
+    pieces = [r.array.reshape(share, 3, group_width) for r in qkv_sums]
+    grad_qkv = jnp.concatenate([p[:, i] for i in range(3) for p in pieces], axis=1)
+    own_rows = small_sum.array.reshape(share, 128).T
+    grad_up_bias = own_rows[9 : 9 + spread].reshape(-1)
 
     def moved(average, param):
         return 0.9 * average + 0.1 * param.astype(F32)
@@ -344,7 +423,7 @@
         own_rows[3:9],
         grad_up,
         grad_down,
-        small_sum[9 * share : small_size],
+        grad_up_bias,
         moved(avg_qkv, w_qkv),
         moved(avg_out, w_out),
         moved(avg_mask, mask_embed),

time: 625 us -> 444 us (0.71)
  waiting for transfers between devices: 274 us -> 78.5 us
  other arithmetic: 41.2 us -> 66.6 us
  local copies, waits for them, and re-layouts: 92.1 us -> 81.7 us
    all_gather x4 -> x1, waiting for transfers between devices: 148 us -> 0.01 us  [body(): others_all = lax.all_gather(jnp.concatenate(others, axis=0), ALL, axis=0)]
    ppermute x50 -> x49, waiting for transfers between devices: 108 us -> 78.5 us  [the longest x21 57.9 us: send_to(): return lax.ppermute(array, axes, pairs)]
    ppermute x12, waiting for transfers between devices: 15.8 us -> 0.03 us  [trade(): lax.ppermute(chunks[k], seq_names, [(i, i ^ k) for i in range(seq_size)])]
    add x46 -> x17, other arithmetic: 4.77 us -> 17.6 us  [add(): self.array = self.array + array.astype(F32)]
    another operation x10 -> x5, local copies, waits for them, and re-layouts: 11.6 us -> 1.2 us  [body(): jnp.stack([grad_mask_part, grad_gain_one, grad_gain_two, grad_bias_one, g...]
    unnamed x145 -> x200, local copies, waits for them, and re-layouts: 18.5 us -> 24.7 us
    ppermute x50 -> x49, starting transfers between devices: 54.7 us -> 59.9 us  [the longest x28 35.2 us: send_to(): lax.ppermute(array, axes[0], [(i, i ^ flip[0]) for i in range(total)])]
    dot_general x8 -> x10, matrix products: 52.6 us -> 47.8 us  [dot(): lax.dot_general(left_side, right_side, (((left_dim,), (right_dim,)), ((),...]
  transfers between devices with their start and end apart: 66 -> 62, of which waited for: 41 -> 17; matrix products, arithmetic and copies ran while one was open for 26% -> 34% of each run, Pallas kernels for 3% -> 11%
where the time goes in v2:
time: 444 us; the launch traced here: 438 us
  local copies, waits for them, and re-layouts  81.7 us (18%)
  matrix products  79.1 us (18%)
  waiting for transfers between devices  78.5 us (18%)
  starting transfers between devices  67.9 us (15%)
  other arithmetic  66.6 us (15%)
  Pallas kernels  48.1 us (11%)
  between operations  16 us (4%)
    ppermute x21, waiting for transfers between devices, send_to(): return lax.ppermute(array, axes, pairs)  57.9 us
    dot_general x10, matrix products, dot(): lax.dot_general(left_side, right_side, (((left_dim,), (right_dim,)), ((),...  47.8 us
    ppermute x28, starting transfers between devices, send_to(): lax.ppermute(array, axes[0], [(i, i ^ flip[0]) for i in range(total)])  35.2 us
    pallas_call x2, Pallas kernels, attend_backward(): pl.pallas_call(partial(backward_kernel, head_size=head_size, scale=1.0 /...  30.3 us
    unnamed x200, local copies, waits for them, and re-layouts  24.7 us
    ppermute x21, starting transfers between devices, send_to(): return lax.ppermute(array, axes, pairs)  24.7 us
    ppermute x28, waiting for transfers between devices, send_to(): lax.ppermute(array, axes[0], [(i, i ^ flip[0]) for i in range(total)])  20.6 us
    pallas_call x1, Pallas kernels, attend_forward(): pl.pallas_call(partial(forward_kernel, head_size=head_size, scale=1.0 / m...  17.8 us
  transfers between devices with their start and end apart: 62, of which 17 were waited for; matrix products, arithmetic and copies ran while one was open for 34% of the time, Pallas kernels for 11%

profile of v2, /device:TPU:0, one launch (start us, length us, event | category | flops | bytes accessed | tf_op | source)
XLA Modules:
  0.0 438.0 jit_solution(15417379505475493537)
XLA Ops:
  15.3 4.1 collective-permute-start.2
  21.0 2.5 constant_dynamic-slice_fusion.19
  33.7 31.7 %collective-permute-done.5 = bf16[2,2,24,2432]{3,2,1,0:T(8,128)(2,1)S(1)} collective-permute-done((bf16[2,2,24,2432]{3,2,1,0:T(8,128)(2,1)S(1)}, bf16[2,2,24,2432]{3,2,1,0:T(8,128)(2,1)S(1)}, u32[]{:S(2)}, u32[]{:S(2)}) %collective-permute-start.5) | collective-permute-done | bytes 466976 | tf_op jit(solution)/shard_map/ppermute | solution.py:153
  65.5 11.1 %collective-permute-done.3 = bf16[2,2,24,2432]{3,2,1,0:T(8,128)(2,1)S(1)} collective-permute-done((bf16[2,2,24,2432]{3,2,1,0:T(8,128)(2,1)S(1)}, bf16[2,2,24,2432]{3,2,1,0:T(8,128)(2,1)S(1)}, u32[]{:S(2)}, u32[]{:S(2)}) %collective-permute-start.3) | collective-permute-done | bytes 466976 | tf_op jit(solution)/shard_map/ppermute | solution.py:153
  77.4 2.1 select_select_fusion
  91.5 2.1 fusion.11
  102.7 4.2 fusion.128
  106.9 2.2 fusion.6
  111.0 17.8 %attend_forward.1 = (bf16[4,2,128,768]{3,2,1,0:T(8,128)(2,1)}, f32[2,6,2,512]{3,2,1,0:T(2,128)}) custom-call(bf16[4,2,128,768]{3,2,1,0:T(8,128)(2,1)} %bitcast.370, bf16[4,2,128,768]{3,2,1,0:T(8,128)(2,1)} %bitcast.364, bf16[4,2,128,768]{3,2,1,0:T(8,128)(2,1)} %bitcast.367), custom_call_target="tpu_custom_call" | custom-call | tf_op jit(solution)/shard_map/attend_forward/pallas_call | solution.py:84
  128.8 2.6 copy.156
  131.4 3.8 fusion.122
  137.6 3.1 fusion.121
  140.7 6.8 %slice.242 = bf16[32,96,768]{2,1,0:T(8,128)(2,1)} slice(bf16[32,216,768]{2,1,0:T(8,128)(2,1)} %bitcast.376), slice={[0:32], [120:216], [0:768]} | slice | bytes 9437184 | tf_op jit(solution)/shard_map/slice | solution.py:280
  151.0 12.3 %fusion.3 = (bf16[3072,1024]{0,1:T(8,128)(2,1)}, f32[1024,3072]{1,0:T(8,128)}) fusion(f32[3072]{0:T(1024)S(1)} %add.896, bf16[1024,768]{1,0:T(8,128)(2,1)S(1)} %add_convert_fusion.3, bf16[768,768]{1,0:T(8,128)(2,1)S(1)} %bitcast.416, bf16[768,768]{1,0:T(8,128)(2,1)S(1)} %bitcast.418, bf16[768,768]{1,0:T(8,128)(2,1)S(1)} %bitcast.420, ...), kind=kOutput, calls=%fused_computation.9 | convolution fusion | flops 4869586944 | bytes 25178112 | tf_op jit(solution)/shard_map/dot_general | solution.py:308
  163.3 8.6 %copy.152 = bf16[3072,1024]{1,0:T(8,128)(2,1)} copy(bf16[3072,1024]{0,1:T(8,128)(2,1)} %get-tuple-element.250) | data formatting | bytes 12582912 | tf_op jit(solution)/shard_map/convert_element_type | solution.py:310
  171.9 7.3 %fusion.129 = f32[2,2,2,2,2,96,768]{6,5,4,3,2,1,0:T(8,128)S(1)} fusion(bf16[2,2,2,2,2,96,1024]{6,5,4,3,2,1,0:T(8,128)(2,1)} %bitcast.377, bf16[1024,768,1,1,1,1,1]{1,0,6,5,4,3,2:T(8,128)(2,1)S(1)} %bitcast.373), kind=kOutput, calls=%fused_computation.321 | convolution fusion | flops 4831838208 | bytes 17301504 | tf_op jit(solution)/shard_map/dot_general | solution.py:29
  179.3 3.6 copy-done.7
  185.1 11.7 %convert_reduce_fusion = (f32[3072]{0:T(1024)S(1)}, bf16[1024,3072]{1,0:T(8,128)(2,1)}) fusion(f32[1024,3072]{1,0:T(8,128)S(1)} %copy-done.90, f32[3072]{0:T(1024)S(1)} %add.896, bf16[1024,768]{1,0:T(8,128)(2,1)S(1)} %bitcast.374, bf16[3072,768]{1,0:T(8,128)(2,1)} %bitcast.384), kind=kOutput, calls=%fused_computation.5 | convolution fusion | flops 4879021056 | bytes 25190400 | tf_op jit(solution)/shard_map/dot_general | solution.py:29
  197.1 13.1 %add_convert_fusion.2 = bf16[1024,768]{1,0:T(8,128)(2,1)} fusion(f32[1024,768]{1,0:T(8,128)} %copy-done, bf16[3072,768]{1,0:T(8,128)(2,1)} %bitcast.385, f32[1024,3072]{1,0:T(8,128)} %get-tuple-element.251, f32[3072]{0:T(1024)S(1)} %add.896, f32[768]{0:T(1024)S(1)} %get-tuple-element.140), kind=kOutput, calls=%fused_computation.38 | convolution fusion | flops 4853071872 | bytes 22035456 | tf_op jit(solution)/shard_map/dot_general | solution.py:336
  210.2 2.6 bitcast_add_fusion.1
  215.5 5.2 %fusion.130 = f32[768,3072]{1,0:T(8,128)S(1)} fusion(bf16[1024,768]{1,0:T(8,128)(2,1)S(1)} %copy-done.28, bf16[1024,3072]{1,0:T(8,128)(2,1)S(1)} %copy-done.89), kind=kOutput, calls=%fused_computation.322 | convolution fusion | flops 4831838208 | bytes 17301504 | tf_op jit(solution)/shard_map/dot_general | solution.py:29
  222.0 2.7 collective-permute-start.24
  224.7 9.7 %multiply_reduce_fusion = (f32[768]{0:T(1024)S(1)}, f32[1024]{0:T(1024)S(1)}, f32[768]{0:T(1024)S(1)}, f32[1024,768]{1,0:T(8,128)S(1)}) fusion(f32[1024,768]{1,0:T(8,128)S(1)} %copy-done.1, f32[1024]{0:T(1024)S(1)} %fusion.110, f32[1024]{0:T(1024)S(1)} %broadcast_multiply_fusion, f32[768]{0:T(1024)S(1)} %get-tuple-element.142, ...), kind=kOutput, calls=%fused_computation.29 | convolution fusion | flops 4857000960 | bytes 17323008 | tf_op jit(solution)/shard_map/dot_general | solution.py:29
  246.5 2.6 convolution_convert_fusion
  251.4 14.9 %attend_backward.2 = (bf16[4,2,128,384]{3,2,1,0:T(8,128)(2,1)}, bf16[4,2,128,384]{3,2,1,0:T(8,128)(2,1)}, bf16[4,2,128,384]{3,2,1,0:T(8,128)(2,1)}) custom-call(bf16[4,2,128,768]{3,2,1,0:T(8,128)(2,1)} %bitcast.371, bf16[4,2,128,768]{3,2,1,0:T(8,128)(2,1)} %bitcast.365, bf16[4,2,128,768]{3,2,1,0:T(8,128)(2,1)} %bitcast.368, ...), custom_call_target="tpu_custom_call" | custom-call | tf_op jit(solution)/shard_map/attend_backward/pallas_call | solution.py:107
  266.3 3.3 pad_maximum_fusion.1
  270.3 2.0 fusion.33
  272.4 3.4 collective-permute-start.60
  276.5 4.5 %collective-permute-done.60 = bf16[96,768]{1,0:T(8,128)(2,1)S(1)} collective-permute-done((bf16[96,768]{1,0:T(8,128)(2,1)S(1)}, bf16[96,768]{1,0:T(8,128)(2,1)S(1)}, u32[]{:S(2)}, u32[]{:S(2)}) %collective-permute-start.60) | collective-permute-done | bytes 147488 | tf_op jit(solution)/shard_map/ppermute | solution.py:151
  281.1 2.3 collective-permute-start.58
  285.0 4.4 %collective-permute-done.58 = bf16[96,768]{1,0:T(8,128)(2,1)S(1)} collective-permute-done((bf16[96,768]{1,0:T(8,128)(2,1)S(1)}, bf16[96,768]{1,0:T(8,128)(2,1)S(1)}, u32[]{:S(2)}, u32[]{:S(2)}) %collective-permute-start.58) | collective-permute-done | bytes 147488 | tf_op jit(solution)/shard_map/ppermute | solution.py:151
  291.6 2.0 collective-permute-start.20
  299.1 2.3 fusion.117
  305.2 15.4 %attend_backward.3 = (bf16[4,2,128,384]{3,2,1,0:T(8,128)(2,1)}, bf16[4,2,128,384]{3,2,1,0:T(8,128)(2,1)}, bf16[4,2,128,384]{3,2,1,0:T(8,128)(2,1)}) custom-call(bf16[4,2,128,768]{3,2,1,0:T(8,128)(2,1)} %bitcast.372, bf16[4,2,128,768]{3,2,1,0:T(8,128)(2,1)} %bitcast.366, bf16[4,2,128,768]{3,2,1,0:T(8,128)(2,1)} %bitcast.369, ...), custom_call_target="tpu_custom_call" | custom-call | tf_op jit(solution)/shard_map/attend_backward/pallas_call | solution.py:107
  327.7 2.1 fusion.35
  329.9 3.0 collective-permute-start.57
  335.5 3.0 collective-permute-start.47
  339.7 3.5 collective-permute-done.56
  343.9 2.2 collective-permute-done.55
  352.4 2.3 fusion.116
  359.4 2.2 fusion.21
  361.8 3.1 multiply_reduce_fusion.1
  377.8 5.7 %collective-permute-done.51 = f32[2,2,24,128]{3,2,1,0:T(8,128)S(1)} collective-permute-done((f32[2,2,24,128]{3,2,1,0:T(8,128)S(1)}, f32[2,2,24,128]{3,2,1,0:T(8,128)S(1)}, u32[]{:S(2)}, u32[]{:S(2)}) %collective-permute-start.51) | collective-permute-done | bytes 49184 | tf_op jit(solution)/shard_map/ppermute | solution.py:153
  384.5 2.6 collective-permute-start.54
  390.1 2.5 collective-permute-start.34
  413.2 4.2 collective-permute-done.38
  417.4 4.2 collective-permute-done.37
  421.8 2.6 collective-permute-start.41
  (441 shorter events, 150.4 us)
Async XLA Ops:
  7.3 130.3 %all-gather.3.cloned.1.call-start = ((), (), s32[]{:S(2)}) async-start(), calls=%async_computation | async-start | bytes 10948608 | tf_op jit(solution)/shard_map/all_gather | solution.py:273
  15.3 13.2 %collective-permute-start.2 = (bf16[24,2432]{1,0:T(8,128)(2,1)S(1)}, bf16[24,2432]{1,0:T(8,128)(2,1)S(1)}, u32[]{:S(2)}, u32[]{:S(2)}) collective-permute-start(bf16[24,2432]{1,0:T(8,128)(2,1)S(1)} %pad_maximum_fusion.11), channel_id=1, source_target_pairs={{0,4},{1,5},{2,6},{3,7},{4,0},{5,1},{6,2},{7,3},{8,12},{9,13},{10,... | collective-permute-start | bytes 350216 | tf_op jit(solution)/shard_map/ppermute | solution.py:151
  19.5 9.0 %collective-permute-start.1 = (bf16[24,2432]{1,0:T(8,128)(2,1)S(1)}, bf16[24,2432]{1,0:T(8,128)(2,1)S(1)}, u32[]{:S(2)}, u32[]{:S(2)}) collective-permute-start(bf16[24,2432]{1,0:T(8,128)(2,1)S(1)} %pad_maximum_fusion.11), channel_id=1, source_target_pairs={{0,2},{1,3},{2,0},{3,1},{4,6},{5,7},{6,4},{7,5},{8,10},{9,11},{10,... | collective-permute-start | bytes 350216 | tf_op jit(solution)/shard_map/ppermute | solution.py:151
  23.6 67.9 %collective-permute-start.9 = (bf16[2,128,768]{2,1,0:T(8,128)(2,1)}, bf16[2,128,768]{2,1,0:T(8,128)(2,1)}, u32[]{:S(2)}, u32[]{:S(2)}) collective-permute-start(bf16[2,128,768]{2,1,0:T(8,128)(2,1)} %get-tuple-element.207), channel_id=1, source_target_pairs={{0,24},{8,16},{16,8},{24,0},{1,25},{9,17},{17,9},{25,1},{2,26},{10... | collective-permute-start | bytes 1179656 | tf_op jit(solution)/shard_map/ppermute | solution.py:243
  23.9 67.5 %collective-permute-start.8 = (bf16[2,128,768]{2,1,0:T(8,128)(2,1)}, bf16[2,128,768]{2,1,0:T(8,128)(2,1)}, u32[]{:S(2)}, u32[]{:S(2)}) collective-permute-start(bf16[2,128,768]{2,1,0:T(8,128)(2,1)} %get-tuple-element.208), channel_id=1, source_target_pairs={{0,16},{8,24},{16,0},{24,8},{1,17},{9,25},{17,1},{25,9},{2,18},{10... | collective-permute-start | bytes 1179656 | tf_op jit(solution)/shard_map/ppermute | solution.py:243
  29.5 36.0 %collective-permute-start.5 = (bf16[2,2,24,2432]{3,2,1,0:T(8,128)(2,1)S(1)}, bf16[2,2,24,2432]{3,2,1,0:T(8,128)(2,1)S(1)}, u32[]{:S(2)}, u32[]{:S(2)}) collective-permute-start(bf16[2,2,24,2432]{3,2,1,0:T(8,128)(2,1)S(1)} %select_select_fusion.1), channel_id=1, source_target_pairs={{0,16},{1,17},{2,18},{3,19},{4,20},{5,21},{6,22},{7,23},{16,0},{17... | collective-permute-start | bytes 1400840 | tf_op jit(solution)/shard_map/ppermute | solution.py:153
  31.1 34.4 %collective-permute-start.4 = (bf16[2,2,24,2432]{3,2,1,0:T(8,128)(2,1)S(1)}, bf16[2,2,24,2432]{3,2,1,0:T(8,128)(2,1)S(1)}, u32[]{:S(2)}, u32[]{:S(2)}) collective-permute-start(bf16[2,2,24,2432]{3,2,1,0:T(8,128)(2,1)S(1)} %select_select_fusion.1), channel_id=1, source_target_pairs={{0,1},{1,0},{2,3},{3,2},{4,5},{5,4},{6,7},{7,6},{16,17},{17,16},{1... | collective-permute-start | bytes 1400840 | tf_op jit(solution)/shard_map/ppermute | solution.py:153
  32.6 44.0 %collective-permute-start.3 = (bf16[2,2,24,2432]{3,2,1,0:T(8,128)(2,1)S(1)}, bf16[2,2,24,2432]{3,2,1,0:T(8,128)(2,1)S(1)}, u32[]{:S(2)}, u32[]{:S(2)}) collective-permute-start(bf16[2,2,24,2432]{3,2,1,0:T(8,128)(2,1)S(1)} %select_select_fusion.1), channel_id=1, source_target_pairs={{0,17},{1,16},{2,19},{3,18},{4,21},{5,20},{6,23},{7,22},{16,1},{17... | collective-permute-start | bytes 1400840 | tf_op jit(solution)/shard_map/ppermute | solution.py:153
  65.5 26.0 %collective-permute-start.7 = (bf16[2,128,768]{2,1,0:T(8,128)(2,1)}, bf16[2,128,768]{2,1,0:T(8,128)(2,1)}, u32[]{:S(2)}, u32[]{:S(2)}) collective-permute-start(bf16[2,128,768]{2,1,0:T(8,128)(2,1)} %get-tuple-element.209), channel_id=1, source_target_pairs={{0,8},{8,0},{16,24},{24,16},{1,9},{9,1},{17,25},{25,17},{2,10},{10... | collective-permute-start | bytes 1179656 | tf_op jit(solution)/shard_map/ppermute | solution.py:243
  97.7 37.5 %collective-permute-start.12 = (bf16[2,128,768]{2,1,0:T(8,128)(2,1)}, bf16[2,128,768]{2,1,0:T(8,128)(2,1)}, u32[]{:S(2)}, u32[]{:S(2)}) collective-permute-start(bf16[2,128,768]{2,1,0:T(8,128)(2,1)} %get-tuple-element.203), channel_id=1, source_target_pairs={{0,24},{8,16},{16,8},{24,0},{1,25},{9,17},{17,9},{25,1},{2,26},{10... | collective-permute-start | bytes 1179656 | tf_op jit(solution)/shard_map/ppermute | solution.py:243
  97.9 37.3 %collective-permute-start.11 = (bf16[2,128,768]{2,1,0:T(8,128)(2,1)}, bf16[2,128,768]{2,1,0:T(8,128)(2,1)}, u32[]{:S(2)}, u32[]{:S(2)}) collective-permute-start(bf16[2,128,768]{2,1,0:T(8,128)(2,1)} %get-tuple-element.204), channel_id=1, source_target_pairs={{0,16},{8,24},{16,0},{24,8},{1,17},{9,25},{17,1},{25,9},{2,18},{10... | collective-permute-start | bytes 1179656 | tf_op jit(solution)/shard_map/ppermute | solution.py:243
  99.8 35.4 %collective-permute-start.10 = (bf16[2,128,768]{2,1,0:T(8,128)(2,1)}, bf16[2,128,768]{2,1,0:T(8,128)(2,1)}, u32[]{:S(2)}, u32[]{:S(2)}) collective-permute-start(bf16[2,128,768]{2,1,0:T(8,128)(2,1)} %get-tuple-element.205), channel_id=1, source_target_pairs={{0,8},{8,0},{16,24},{24,16},{1,9},{9,1},{17,25},{25,17},{2,10},{10... | collective-permute-start | bytes 1179656 | tf_op jit(solution)/shard_map/ppermute | solution.py:243
  184.6 25.5 %collective-permute-start.13 = (bf16[2,2,2,2,96,768]{5,4,3,2,1,0:T(8,128)(2,1)}, bf16[2,2,2,2,96,768]{5,4,3,2,1,0:T(8,128)(2,1)}, u32[]{:S(2)}, u32[]{:S(2)}) collective-permute-start(bf16[2,2,2,2,96,768]{5,4,3,2,1,0:T(8,128)(2,1)} %fusion.12), channel_id=1, source_target_pairs={{0,8},{8,0},{1,9},{9,1},{2,10},{10,2},{3,11},{11,3},{4,12},{12,4},... | collective-permute-start | bytes 7077896 | tf_op jit(solution)/shard_map/ppermute | solution.py:151
  221.1 18.5 %collective-permute-start.14 = (bf16[2,2,2,2,24,3072]{5,4,2,1,3,0:T(8,128)(2,1)S(1)}, bf16[2,2,2,2,24,3072]{5,4,2,1,3,0:T(8,128)(2,1)S(1)}, u32[]{:S(2)}, u32[]{:S(2)}) collective-permute-start(bf16[2,2,2,2,24,3072]{5,4,2,1,3,0:T(8,128)(2,1)S(1)} %fusion.13), channel_id=1, source_target_pairs={{0,8},{8,0},{1,9},{9,1},{2,10},{10,2},{3,11},{11,3},{4,12},{12,4},... | collective-permute-start | bytes 7077896 | tf_op jit(solution)/shard_map/ppermute | solution.py:151
  221.2 48.4 %collective-permute-start.22 = (bf16[2,2,96,768]{3,2,1,0:T(8,128)(2,1)}, bf16[2,2,96,768]{3,2,1,0:T(8,128)(2,1)}, u32[]{:S(2)}, u32[]{:S(2)}) collective-permute-start(bf16[2,2,96,768]{3,2,1,0:T(8,128)(2,1)} %get-tuple-element.172), channel_id=1, source_target_pairs={{0,16},{1,17},{2,18},{3,19},{4,20},{5,21},{6,22},{7,23},{16,0},{17... | collective-permute-start | bytes 1769480 | tf_op jit(solution)/shard_map/ppermute | solution.py:153
  221.6 48.7 %collective-permute-start.23 = (bf16[2,2,96,768]{3,2,1,0:T(8,128)(2,1)}, bf16[2,2,96,768]{3,2,1,0:T(8,128)(2,1)}, u32[]{:S(2)}, u32[]{:S(2)}) collective-permute-start(bf16[2,2,96,768]{3,2,1,0:T(8,128)(2,1)} %get-tuple-element.173), channel_id=1, source_target_pairs={{0,1},{1,0},{2,3},{3,2},{4,5},{5,4},{6,7},{7,6},{16,17},{17,16},{1... | collective-permute-start | bytes 1769480 | tf_op jit(solution)/shard_map/ppermute | solution.py:153
  222.0 48.3 %collective-permute-start.24 = (bf16[2,2,96,768]{3,2,1,0:T(8,128)(2,1)}, bf16[2,2,96,768]{3,2,1,0:T(8,128)(2,1)}, u32[]{:S(2)}, u32[]{:S(2)}) collective-permute-start(bf16[2,2,96,768]{3,2,1,0:T(8,128)(2,1)} %get-tuple-element.171), channel_id=1, source_target_pairs={{0,17},{1,16},{2,19},{3,18},{4,21},{5,20},{6,23},{7,22},{16,1},{17... | collective-permute-start | bytes 1769480 | tf_op jit(solution)/shard_map/ppermute | solution.py:153
  250.2 40.9 %collective-permute-start.17 = (bf16[2,128,768]{2,1,0:T(8,128)(2,1)}, bf16[2,128,768]{2,1,0:T(8,128)(2,1)}, u32[]{:S(2)}, u32[]{:S(2)}) collective-permute-start(bf16[2,128,768]{2,1,0:T(8,128)(2,1)} %bitcast.68), channel_id=1, source_target_pairs={{0,24},{8,16},{16,8},{24,0},{1,25},{9,17},{17,9},{25,1},{2,26},{10... | collective-permute-start | bytes 1179656 | tf_op jit(solution)/shard_map/ppermute | solution.py:243
  250.2 41.5 %collective-permute-start.16 = (bf16[2,128,768]{2,1,0:T(8,128)(2,1)}, bf16[2,128,768]{2,1,0:T(8,128)(2,1)}, u32[]{:S(2)}, u32[]{:S(2)}) collective-permute-start(bf16[2,128,768]{2,1,0:T(8,128)(2,1)} %bitcast.66), channel_id=1, source_target_pairs={{0,16},{8,24},{16,0},{24,8},{1,17},{9,25},{17,1},{25,9},{2,18},{10... | collective-permute-start | bytes 1179656 | tf_op jit(solution)/shard_map/ppermute | solution.py:243
  269.6 24.1 %collective-permute-start.15 = (bf16[2,128,768]{2,1,0:T(8,128)(2,1)S(1)}, bf16[2,128,768]{2,1,0:T(8,128)(2,1)S(1)}, u32[]{:S(2)}, u32[]{:S(2)}) collective-permute-start(bf16[2,128,768]{2,1,0:T(8,128)(2,1)S(1)} %bitcast.428), channel_id=1, source_target_pairs={{0,8},{8,0},{16,24},{24,16},{1,9},{9,1},{17,25},{25,17},{2,10},{10... | collective-permute-start | bytes 1179656 | tf_op jit(solution)/shard_map/ppermute | solution.py:243
  272.4 8.6 %collective-permute-start.60 = (bf16[96,768]{1,0:T(8,128)(2,1)S(1)}, bf16[96,768]{1,0:T(8,128)(2,1)S(1)}, u32[]{:S(2)}, u32[]{:S(2)}) collective-permute-start(bf16[96,768]{1,0:T(8,128)(2,1)S(1)} %get-tuple-element.213), channel_id=1, source_target_pairs={{0,6},{1,7},{2,4},{3,5},{4,2},{5,3},{6,0},{7,1},{8,14},{9,15},{10,... | collective-permute-start | bytes 442376 | tf_op jit(solution)/shard_map/ppermute | solution.py:151
  275.8 9.2 %collective-permute-start.59 = (bf16[96,768]{1,0:T(8,128)(2,1)S(1)}, bf16[96,768]{1,0:T(8,128)(2,1)S(1)}, u32[]{:S(2)}, u32[]{:S(2)}) collective-permute-start(bf16[96,768]{1,0:T(8,128)(2,1)S(1)} %get-tuple-element.214), channel_id=1, source_target_pairs={{0,2},{1,3},{2,0},{3,1},{4,6},{5,7},{6,4},{7,5},{8,10},{9,11},{10,... | collective-permute-start | bytes 442376 | tf_op jit(solution)/shard_map/ppermute | solution.py:151
  281.1 8.3 %collective-permute-start.58 = (bf16[96,768]{1,0:T(8,128)(2,1)S(1)}, bf16[96,768]{1,0:T(8,128)(2,1)S(1)}, u32[]{:S(2)}, u32[]{:S(2)}) collective-permute-start(bf16[96,768]{1,0:T(8,128)(2,1)S(1)} %get-tuple-element.215), channel_id=1, source_target_pairs={{0,4},{1,5},{2,6},{3,7},{4,0},{5,1},{6,2},{7,3},{8,12},{9,13},{10,... | collective-permute-start | bytes 442376 | tf_op jit(solution)/shard_map/ppermute | solution.py:151
  285.0 11.5 %collective-permute-start.21 = (bf16[2,2,2,2,24,768]{5,4,3,2,1,0:T(8,128)(2,1)S(1)}, bf16[2,2,2,2,24,768]{5,4,3,2,1,0:T(8,128)(2,1)S(1)}, u32[]{:S(2)}, u32[]{:S(2)}) collective-permute-start(bf16[2,2,2,2,24,768]{5,4,3,2,1,0:T(8,128)(2,1)S(1)} %copy-done.48), channel_id=1, source_target_pairs={{0,8},{8,0},{1,9},{9,1},{2,10},{10,2},{3,11},{11,3},{4,12},{12,4},... | collective-permute-start | bytes 1769480 | tf_op jit(solution)/shard_map/ppermute | solution.py:151
  289.4 35.6 %collective-permute-start.18 = (bf16[2,2,24,3072]{3,2,1,0:T(8,128)(2,1)}, bf16[2,2,24,3072]{3,2,1,0:T(8,128)(2,1)}, u32[]{:S(2)}, u32[]{:S(2)}) collective-permute-start(bf16[2,2,24,3072]{3,2,1,0:T(8,128)(2,1)} %get-tuple-element.170), channel_id=1, source_target_pairs={{0,16},{1,17},{2,18},{3,19},{4,20},{5,21},{6,22},{7,23},{16,0},{17... | collective-permute-start | bytes 1769480 | tf_op jit(solution)/shard_map/ppermute | solution.py:153
  291.1 35.5 %collective-permute-start.19 = (bf16[2,2,24,3072]{3,2,1,0:T(8,128)(2,1)}, bf16[2,2,24,3072]{3,2,1,0:T(8,128)(2,1)}, u32[]{:S(2)}, u32[]{:S(2)}) collective-permute-start(bf16[2,2,24,3072]{3,2,1,0:T(8,128)(2,1)} %get-tuple-element.169), channel_id=1, source_target_pairs={{0,1},{1,0},{2,3},{3,2},{4,5},{5,4},{6,7},{7,6},{16,17},{17,16},{1... | collective-permute-start | bytes 1769480 | tf_op jit(solution)/shard_map/ppermute | solution.py:153
  291.6 36.1 %collective-permute-start.20 = (bf16[2,2,24,3072]{3,2,1,0:T(8,128)(2,1)}, bf16[2,2,24,3072]{3,2,1,0:T(8,128)(2,1)}, u32[]{:S(2)}, u32[]{:S(2)}) collective-permute-start(bf16[2,2,24,3072]{3,2,1,0:T(8,128)(2,1)} %get-tuple-element.168), channel_id=1, source_target_pairs={{0,17},{1,16},{2,19},{3,18},{4,21},{5,20},{6,23},{7,22},{16,1},{17... | collective-permute-start | bytes 1769480 | tf_op jit(solution)/shard_map/ppermute | solution.py:153
  304.3 44.6 %collective-permute-start.25 = (bf16[2,2,2,2,24,1152]{5,4,2,1,3,0:T(8,128)(2,1)}, bf16[2,2,2,2,24,1152]{5,4,2,1,3,0:T(8,128)(2,1)}, u32[]{:S(2)}, u32[]{:S(2)}) collective-permute-start(bf16[2,2,2,2,24,1152]{5,4,2,1,3,0:T(8,128)(2,1)} %fusion.36), channel_id=1, source_target_pairs={{0,8},{8,0},{1,9},{9,1},{2,10},{10,2},{3,11},{11,3},{4,12},{12,4},... | collective-permute-start | bytes 2654216 | tf_op jit(solution)/shard_map/ppermute | solution.py:151
  304.3 28.7 %collective-permute-start.44 = (bf16[2,2,24,768]{3,2,1,0:T(8,128)(2,1)}, bf16[2,2,24,768]{3,2,1,0:T(8,128)(2,1)S(1)}, u32[]{:S(2)}, u32[]{:S(2)}) collective-permute-start(bf16[2,2,24,768]{3,2,1,0:T(8,128)(2,1)} %get-tuple-element.216), channel_id=1, source_target_pairs={{0,17},{1,16},{2,19},{3,18},{4,21},{5,20},{6,23},{7,22},{16,1},{17... | collective-permute-start | bytes 442376 | tf_op jit(solution)/shard_map/ppermute | solution.py:153
  329.9 8.6 %collective-permute-start.57 = (bf16[24,3072]{1,0:T(8,128)(2,1)S(1)}, bf16[24,3072]{1,0:T(8,128)(2,1)S(1)}, u32[]{:S(2)}, u32[]{:S(2)}) collective-permute-start(bf16[24,3072]{1,0:T(8,128)(2,1)S(1)} %get-tuple-element.210), channel_id=1, source_target_pairs={{0,6},{1,7},{2,4},{3,5},{4,2},{5,3},{6,0},{7,1},{8,14},{9,15},{10,... | collective-permute-start | bytes 442376 | tf_op jit(solution)/shard_map/ppermute | solution.py:151
  333.0 10.2 %collective-permute-start.56 = (bf16[24,3072]{1,0:T(8,128)(2,1)S(1)}, bf16[24,3072]{1,0:T(8,128)(2,1)S(1)}, u32[]{:S(2)}, u32[]{:S(2)}) collective-permute-start(bf16[24,3072]{1,0:T(8,128)(2,1)S(1)} %get-tuple-element.211), channel_id=1, source_target_pairs={{0,2},{1,3},{2,0},{3,1},{4,6},{5,7},{6,4},{7,5},{8,10},{9,11},{10,... | collective-permute-start | bytes 442376 | tf_op jit(solution)/shard_map/ppermute | solution.py:151
  333.0 13.1 %collective-permute-start.55 = (bf16[24,3072]{1,0:T(8,128)(2,1)S(1)}, bf16[24,3072]{1,0:T(8,128)(2,1)S(1)}, u32[]{:S(2)}, u32[]{:S(2)}) collective-permute-start(bf16[24,3072]{1,0:T(8,128)(2,1)S(1)} %get-tuple-element.212), channel_id=1, source_target_pairs={{0,4},{1,5},{2,6},{3,7},{4,0},{5,1},{6,2},{7,3},{8,12},{9,13},{10,... | collective-permute-start | bytes 442376 | tf_op jit(solution)/shard_map/ppermute | solution.py:151
  335.5 11.4 %collective-permute-start.47 = (bf16[24,768]{1,0:T(8,128)(2,1)S(1)}, bf16[24,768]{1,0:T(8,128)(2,1)S(1)}, u32[]{:S(2)}, u32[]{:S(2)}) collective-permute-start(bf16[24,768]{1,0:T(8,128)(2,1)S(1)} %get-tuple-element.226), channel_id=1, source_target_pairs={{0,6},{1,7},{2,4},{3,5},{4,2},{5,3},{6,0},{7,1},{8,14},{9,15},{10,... | collective-permute-start | bytes 110600 | tf_op jit(solution)/shard_map/ppermute | solution.py:151
  338.5 8.4 %collective-permute-start.46 = (bf16[24,768]{1,0:T(8,128)(2,1)S(1)}, bf16[24,768]{1,0:T(8,128)(2,1)S(1)}, u32[]{:S(2)}, u32[]{:S(2)}) collective-permute-start(bf16[24,768]{1,0:T(8,128)(2,1)S(1)} %get-tuple-element.227), channel_id=1, source_target_pairs={{0,2},{1,3},{2,0},{3,1},{4,6},{5,7},{6,4},{7,5},{8,10},{9,11},{10,... | collective-permute-start | bytes 110600 | tf_op jit(solution)/shard_map/ppermute | solution.py:151
  355.8 17.0 %collective-permute-start.31 = (bf16[2,2,24,1152]{3,2,1,0:T(8,128)(2,1)}, bf16[2,2,24,1152]{3,2,1,0:T(8,128)(2,1)}, u32[]{:S(2)}, u32[]{:S(2)}) collective-permute-start(bf16[2,2,24,1152]{3,2,1,0:T(8,128)(2,1)} %get-tuple-element.183), channel_id=1, source_target_pairs={{0,17},{1,16},{2,19},{3,18},{4,21},{5,20},{6,23},{7,22},{16,1},{17... | collective-permute-start | bytes 663560 | tf_op jit(solution)/shard_map/ppermute | solution.py:153
  356.5 17.1 %collective-permute-start.30 = (bf16[2,2,24,1152]{3,2,1,0:T(8,128)(2,1)}, bf16[2,2,24,1152]{3,2,1,0:T(8,128)(2,1)}, u32[]{:S(2)}, u32[]{:S(2)}) collective-permute-start(bf16[2,2,24,1152]{3,2,1,0:T(8,128)(2,1)} %get-tuple-element.184), channel_id=1, source_target_pairs={{0,1},{1,0},{2,3},{3,2},{4,5},{5,4},{6,7},{7,6},{16,17},{17,16},{1... | collective-permute-start | bytes 663560 | tf_op jit(solution)/shard_map/ppermute | solution.py:153
  358.3 17.1 %collective-permute-start.29 = (bf16[2,2,24,1152]{3,2,1,0:T(8,128)(2,1)}, bf16[2,2,24,1152]{3,2,1,0:T(8,128)(2,1)}, u32[]{:S(2)}, u32[]{:S(2)}) collective-permute-start(bf16[2,2,24,1152]{3,2,1,0:T(8,128)(2,1)} %get-tuple-element.185), channel_id=1, source_target_pairs={{0,16},{1,17},{2,18},{3,19},{4,20},{5,21},{6,22},{7,23},{16,0},{17... | collective-permute-start | bytes 663560 | tf_op jit(solution)/shard_map/ppermute | solution.py:153
  359.3 47.3 %collective-permute-start.35 = (bf16[2,2,2,2,24,1152]{5,4,2,1,3,0:T(8,128)(2,1)}, bf16[2,2,2,2,24,1152]{5,4,2,1,3,0:T(8,128)(2,1)}, u32[]{:S(2)}, u32[]{:S(2)}) collective-permute-start(bf16[2,2,2,2,24,1152]{5,4,2,1,3,0:T(8,128)(2,1)} %fusion.37), channel_id=1, source_target_pairs={{0,8},{8,0},{1,9},{9,1},{2,10},{10,2},{3,11},{11,3},{4,12},{12,4},... | collective-permute-start | bytes 2654216 | tf_op jit(solution)/shard_map/ppermute | solution.py:151
  370.7 39.9 %collective-permute-start.28 = (bf16[2,128,768]{2,1,0:T(8,128)(2,1)}, bf16[2,128,768]{2,1,0:T(8,128)(2,1)}, u32[]{:S(2)}, u32[]{:S(2)}) collective-permute-start(bf16[2,128,768]{2,1,0:T(8,128)(2,1)} %bitcast.102), channel_id=1, source_target_pairs={{0,24},{8,16},{16,8},{24,0},{1,25},{9,17},{17,9},{25,1},{2,26},{10... | collective-permute-start | bytes 1179656 | tf_op jit(solution)/shard_map/ppermute | solution.py:243
  372.8 10.8 %collective-permute-start.51 = (f32[2,2,24,128]{3,2,1,0:T(8,128)S(1)}, f32[2,2,24,128]{3,2,1,0:T(8,128)S(1)}, u32[]{:S(2)}, u32[]{:S(2)}) collective-permute-start(f32[2,2,24,128]{3,2,1,0:T(8,128)S(1)} %get-tuple-element.229), channel_id=1, source_target_pairs={{0,17},{1,16},{2,19},{3,18},{4,21},{5,20},{6,23},{7,22},{16,1},{17... | collective-permute-start | bytes 147464 | tf_op jit(solution)/shard_map/ppermute | solution.py:153
  373.6 10.0 %collective-permute-start.50 = (f32[2,2,24,128]{3,2,1,0:T(8,128)S(1)}, f32[2,2,24,128]{3,2,1,0:T(8,128)S(1)}, u32[]{:S(2)}, u32[]{:S(2)}) collective-permute-start(f32[2,2,24,128]{3,2,1,0:T(8,128)S(1)} %get-tuple-element.230), channel_id=1, source_target_pairs={{0,1},{1,0},{2,3},{3,2},{4,5},{5,4},{6,7},{7,6},{16,17},{17,16},{1... | collective-permute-start | bytes 147464 | tf_op jit(solution)/shard_map/ppermute | solution.py:153
  375.4 9.1 %collective-permute-start.49 = (f32[2,2,24,128]{3,2,1,0:T(8,128)S(1)}, f32[2,2,24,128]{3,2,1,0:T(8,128)S(1)}, u32[]{:S(2)}, u32[]{:S(2)}) collective-permute-start(f32[2,2,24,128]{3,2,1,0:T(8,128)S(1)} %get-tuple-element.228), channel_id=1, source_target_pairs={{0,16},{1,17},{2,18},{3,19},{4,20},{5,21},{6,22},{7,23},{16,0},{17... | collective-permute-start | bytes 147464 | tf_op jit(solution)/shard_map/ppermute | solution.py:153
  390.1 9.8 %collective-permute-start.34 = (bf16[24,1152]{1,0:T(8,128)(2,1)}, bf16[24,1152]{1,0:T(8,128)(2,1)}, u32[]{:S(2)}, u32[]{:S(2)}) collective-permute-start(bf16[24,1152]{1,0:T(8,128)(2,1)} %get-tuple-element.223), channel_id=1, source_target_pairs={{0,6},{1,7},{2,4},{3,5},{4,2},{5,3},{6,0},{7,1},{8,14},{9,15},{10,... | collective-permute-start | bytes 165896 | tf_op jit(solution)/shard_map/ppermute | solution.py:151
  399.9 11.7 %collective-permute-start.27 = (bf16[2,128,768]{2,1,0:T(8,128)(2,1)}, bf16[2,128,768]{2,1,0:T(8,128)(2,1)}, u32[]{:S(2)}, u32[]{:S(2)}) collective-permute-start(bf16[2,128,768]{2,1,0:T(8,128)(2,1)} %bitcast.427), channel_id=1, source_target_pairs={{0,16},{8,24},{16,0},{24,8},{1,17},{9,25},{17,1},{25,9},{2,18},{10... | collective-permute-start | bytes 1179656 | tf_op jit(solution)/shard_map/ppermute | solution.py:243
  400.9 10.7 %collective-permute-start.26 = (bf16[2,128,768]{2,1,0:T(8,128)(2,1)}, bf16[2,128,768]{2,1,0:T(8,128)(2,1)}, u32[]{:S(2)}, u32[]{:S(2)}) collective-permute-start(bf16[2,128,768]{2,1,0:T(8,128)(2,1)} %bitcast.426), channel_id=1, source_target_pairs={{0,8},{8,0},{16,24},{24,16},{1,9},{9,1},{17,25},{25,17},{2,10},{10... | collective-permute-start | bytes 1179656 | tf_op jit(solution)/shard_map/ppermute | solution.py:243
  408.1 9.3 %collective-permute-start.38 = (bf16[2,2,24,1152]{3,2,1,0:T(8,128)(2,1)S(1)}, bf16[2,2,24,1152]{3,2,1,0:T(8,128)(2,1)S(1)}, u32[]{:S(2)}, u32[]{:S(2)}) collective-permute-start(bf16[2,2,24,1152]{3,2,1,0:T(8,128)(2,1)S(1)} %get-tuple-element.181), channel_id=1, source_target_pairs={{0,17},{1,16},{2,19},{3,18},{4,21},{5,20},{6,23},{7,22},{16,1},{17... | collective-permute-start | bytes 663560 | tf_op jit(solution)/shard_map/ppermute | solution.py:153
  409.6 12.1 %collective-permute-start.37 = (bf16[2,2,24,1152]{3,2,1,0:T(8,128)(2,1)S(1)}, bf16[2,2,24,1152]{3,2,1,0:T(8,128)(2,1)S(1)}, u32[]{:S(2)}, u32[]{:S(2)}) collective-permute-start(bf16[2,2,24,1152]{3,2,1,0:T(8,128)(2,1)S(1)} %get-tuple-element.182), channel_id=1, source_target_pairs={{0,1},{1,0},{2,3},{3,2},{4,5},{5,4},{6,7},{7,6},{16,17},{17,16},{1... | collective-permute-start | bytes 663560 | tf_op jit(solution)/shard_map/ppermute | solution.py:153
  410.6 11.0 %collective-permute-start.36 = (bf16[2,2,24,1152]{3,2,1,0:T(8,128)(2,1)S(1)}, bf16[2,2,24,1152]{3,2,1,0:T(8,128)(2,1)S(1)}, u32[]{:S(2)}, u32[]{:S(2)}) collective-permute-start(bf16[2,2,24,1152]{3,2,1,0:T(8,128)(2,1)S(1)} %get-tuple-element.180), channel_id=1, source_target_pairs={{0,16},{1,17},{2,18},{3,19},{4,20},{5,21},{6,22},{7,23},{16,0},{17... | collective-permute-start | bytes 663560 | tf_op jit(solution)/shard_map/ppermute | solution.py:153
  (108 other events, 937.2 us)
Sparse Core Ops, SparseCore 0:
  13.0 100.9 all-gather.2

commit v3 on v2

v3 whole, which is shorter than its diff:
```python
import math
from functools import partial

import jax
import jax.numpy as jnp
from jax import lax
from jax.experimental import pallas as pl
from jax.experimental.pallas import tpu as pltpu
from jax.sharding import Mesh, PartitionSpec as P

H = 12
norm_eps = 1e-06
F32 = jnp.float32
BF16 = jnp.bfloat16
ALL = ("sx", "core", "clip")


def layer_norm(hidden, gain_row, shift_row):
    center = hidden - jnp.mean(hidden, axis=-1, keepdims=True)
    spread = jnp.mean(center * center, axis=-1, keepdims=True)
    return center * lax.rsqrt(spread + norm_eps) * gain_row + shift_row


def dot(left_side, right_side, left_dim, right_dim):
    return lax.dot_general(
        left_side, right_side, (((left_dim,), (right_dim,)), ((), ())), preferred_element_type=F32
    )


def load_rows(ref):
    return ref[...].reshape(ref.shape[0] * ref.shape[2], ref.shape[3])


def forward_kernel(q_ref, k_ref, v_ref, o_ref, log_ref, *, head_size, scale):
    query, key, value = load_rows(q_ref) * scale, load_rows(k_ref), load_rows(v_ref)
    mixed = []
    for i in range(query.shape[1] // head_size):
        cols = slice(i * head_size, (i + 1) * head_size)
        scores = dot(key[:, cols], query[:, cols], 1, 1)
        top = jnp.max(scores, axis=0, keepdims=True)
        shifted = jnp.exp(scores - top)
        total = jnp.sum(shifted, axis=0, keepdims=True)
        mixed.append(dot(value[:, cols], shifted.astype(BF16), 0, 0) / total)
        log_ref[0, 0, i : i + 1, :] = top + jnp.log(total)
    mixed = jnp.concatenate(mixed, axis=0).T.astype(BF16)
    o_ref[...] = mixed.reshape(o_ref.shape)


def backward_kernel(q_ref, k_ref, v_ref, g_ref, log_ref, d_ref, *, head_size, scale):
    query, key, value = load_rows(q_ref) * scale, load_rows(k_ref), load_rows(v_ref)
    grad = load_rows(g_ref)
    grad_query, grad_key, grad_value = [], [], []
    for i in range(query.shape[1] // head_size):
        cols = slice(i * head_size, (i + 1) * head_size)
        scores = dot(key[:, cols], query[:, cols], 1, 1)
        prob = jnp.exp(scores - log_ref[0, 0, i : i + 1, :])
        grad_prob = dot(value[:, cols], grad[:, cols], 1, 1)
        inner = jnp.sum(grad_prob * prob, axis=0, keepdims=True)
        grad_scores = (prob * (grad_prob - inner)).astype(BF16)
        grad_query.append(dot(key[:, cols], grad_scores, 0, 0))
        grad_key.append(dot(grad_scores, query[:, cols], 1, 0))
        grad_value.append(dot(prob.astype(BF16), grad[:, cols], 1, 0))
    rows = d_ref.shape[:3]
    wide = query.shape[1]
    dq = (jnp.concatenate(grad_query, axis=0) * scale).T.astype(BF16)
    d_ref[..., :wide] = dq.reshape(rows + (wide,))
    d_ref[..., wide : 2 * wide] = jnp.concatenate(grad_key, axis=1).astype(BF16).reshape(rows + (wide,))
    d_ref[..., 2 * wide :] = jnp.concatenate(grad_value, axis=1).astype(BF16).reshape(rows + (wide,))


PAIR = 128


def pair_spec(grid_shape, first, wide=PAIR):
    slots, _, rows, _ = grid_shape
    return pl.BlockSpec((slots, 1, rows, wide), lambda c, j: (0, c, 0, j + first))


def attend_forward(joined, grid_shape, head_count):
    slots, clips, rows, width = grid_shape
    head_size = width // head_count
    blocks, per_block = width // PAIR, PAIR // head_size
    return pl.pallas_call(
        partial(forward_kernel, head_size=head_size, scale=1.0 / math.sqrt(head_size)),
        grid=(clips, blocks),
        in_specs=[pair_spec(grid_shape, i * blocks) for i in range(3)],
        out_specs=[
            pair_spec(grid_shape, 0),
            pl.BlockSpec((1, 1, per_block, slots * rows), lambda c, j: (c, j, 0, 0)),
        ],
        out_shape=[
            jax.ShapeDtypeStruct(grid_shape, BF16),
            jax.ShapeDtypeStruct((clips, blocks, per_block, slots * rows), F32),
        ],
        name="attend_forward",
    )(joined, joined, joined)


def attend_backward(joined, grad_mixed, logs, head_count, first, count):
    slots, clips, rows, width = grid_shape = grad_mixed.shape
    head_size = width // head_count
    per_block = PAIR // head_size
    return pl.pallas_call(
        partial(backward_kernel, head_size=head_size, scale=1.0 / math.sqrt(head_size)),
        grid=(clips, count),
        in_specs=[pair_spec(grid_shape, i * (width // PAIR) + first) for i in range(3)]
        + [
            pair_spec(grid_shape, first),
            pl.BlockSpec((1, 1, per_block, slots * rows), lambda c, j: (c, j + first, 0, 0)),
        ],
        out_specs=pair_spec(grid_shape, 0, 3 * PAIR),
        out_shape=jax.ShapeDtypeStruct((slots, clips, rows, count * 3 * PAIR), BF16),
        name="attend_backward",
    )(joined, joined, joined, grad_mixed, logs)


def first_kernel(one_ref, two_ref, q_ref, k_ref, v_ref, grad_ref):
    weights = (q_ref, k_ref, v_ref)
    cols = [slice(c, c + PAIR) for c in range(0, q_ref.shape[1], PAIR)]
    weight = jnp.concatenate([ref[:, c] for c in cols for ref in weights], axis=1)
    cut = one_ref.shape[1]
    grad_ref[...] = dot(one_ref[...], weight[:, :cut], 1, 1) + dot(two_ref[...], weight[:, cut:], 1, 1)


def feed_first(piece_one, piece_two, w_qkv):
    rows, width = piece_one.shape[0], w_qkv.shape[0]
    tile = rows // 2
    return pl.pallas_call(
        first_kernel,
        grid=(rows // tile,),
        in_specs=[pl.BlockSpec((tile, p.shape[1]), lambda r: (r, 0)) for p in (piece_one, piece_two)]
        + [pl.BlockSpec((width, width), lambda r, i=i: (0, i)) for i in range(3)],
        out_specs=pl.BlockSpec((tile, width), lambda r: (r, 0)),
        out_shape=jax.ShapeDtypeStruct((rows, width), F32),
        name="feed_first",
    )(piece_one, piece_two, w_qkv, w_qkv, w_qkv)


def order_kernel(one_ref, two_ref, out_ref):
    joined = jnp.concatenate([one_ref[...], two_ref[...]], axis=1)
    pairs = joined.shape[1] // (3 * PAIR)
    for i in range(3):
        for p in range(pairs):
            to, at = i * pairs + p, 3 * p + i
            out_ref[:, to * PAIR : (to + 1) * PAIR] = joined[:, at * PAIR : (at + 1) * PAIR]


def natural_order(one, two):
    shape = (one.shape[0], one.shape[1] + two.shape[1])
    return pl.pallas_call(order_kernel, out_shape=jax.ShapeDtypeStruct(shape, F32), name="natural_order")(one, two)


DOWN_ROWS = 96
HIDDEN = 8 * DOWN_ROWS
CHUNK = 256


def up_kernel(second_ref, w_ref, bias_ref, cot_ref, active_ref, slope_ref, grad_ref):
    total = 0.0
    for r in range(0, second_ref.shape[0], CHUNK):
        rows = slice(r, r + CHUNK)
        upper = dot(second_ref[rows, :], w_ref[...], 1, 0) + bias_ref[...]
        below = 0.5 + 0.5 * lax.erf(upper * math.sqrt(0.5))
        bell = jnp.exp(upper * upper * -0.5) * (1.0 / math.sqrt(2.0 * math.pi))
        active = (upper * below).astype(BF16)
        active_ref[rows, :] = active
        slope_ref[rows, :] = below + upper * bell
        total = total + dot(active, cot_ref[rows, :], 0, 0)
    grad_ref[...] = total.astype(BF16)


def down_spec(w_down):
    return pl.BlockSpec((HIDDEN // DOWN_ROWS, DOWN_ROWS, w_down.shape[2]), lambda j: (j, 0, 0))


def feed_up(second, w_up, bias, cot):
    rows, width = second.shape
    hidden = bias.shape[1]
    whole = pl.BlockSpec((rows, width), lambda j: (0, 0))
    tall = pl.BlockSpec((rows, HIDDEN), lambda j: (0, j))
    return pl.pallas_call(
        up_kernel,
        grid=(hidden // HIDDEN,),
        in_specs=[
            whole,
            pl.BlockSpec((width, HIDDEN), lambda j: (0, j)),
            pl.BlockSpec((1, HIDDEN), lambda j: (0, j)),
            whole,
        ],
        out_specs=[tall, tall, pl.BlockSpec((HIDDEN, width), lambda j: (j, 0))],
        out_shape=[
            jax.ShapeDtypeStruct((rows, hidden), BF16),
            jax.ShapeDtypeStruct((rows, hidden), F32),
            jax.ShapeDtypeStruct((hidden, width), BF16),
        ],
        name="feed_up",
    )(second, w_up, bias, cot)


def final_kernel(active_ref, w_ref, middle_ref, bias_ref, out_ref):
    weight = w_ref[...].reshape(active_ref.shape[1], -1)
    total = dot(active_ref[...], weight, 1, 0) + bias_ref[...]
    out_ref[...] = (middle_ref[...] + total).astype(BF16)


def feed_final(active, w_down, middle, bias):
    rows, width = middle.shape
    hidden = active.shape[1]
    return pl.pallas_call(
        final_kernel,
        grid=(rows // CHUNK,),
        in_specs=[
            pl.BlockSpec((CHUNK, hidden), lambda r: (r, 0)),
            pl.BlockSpec((hidden // DOWN_ROWS, DOWN_ROWS, width), lambda r: (0, 0, 0)),
            pl.BlockSpec((CHUNK, width), lambda r: (r, 0)),
            pl.BlockSpec((1, width), lambda r: (0, 0)),
        ],
        out_specs=pl.BlockSpec((CHUNK, width), lambda r: (r, 0)),
        out_shape=jax.ShapeDtypeStruct((rows, width), BF16),
        name="feed_final",
    )(active, w_down, middle, bias)


def back_kernel(second_ref, cot_ref, w_up_ref, w_down_ref, slope_ref, grad_up_ref, bias_ref, grad_ref):
    @pl.when(pl.program_id(0) == 0)
    def _():
        grad_ref[...] = jnp.zeros_like(grad_ref)

    w_down = w_down_ref[...].reshape(HIDDEN, -1)
    total, column = 0.0, 0.0
    for r in range(0, second_ref.shape[0], CHUNK):
        rows = slice(r, r + CHUNK)
        upper = dot(cot_ref[rows, :], w_down, 1, 1) * slope_ref[rows, :]
        upper = upper.astype(BF16)
        column = column + jnp.sum(upper.astype(F32), axis=0, keepdims=True)
        grad_ref[rows, :] += dot(upper, w_up_ref[...], 1, 1)
        total = total + dot(second_ref[rows, :], upper, 0, 0)
    grad_up_ref[...] = total.astype(BF16)
    bias_ref[...] = column


def feed_back(second, cot, w_up, w_down, slope):
    rows, width = second.shape
    hidden = slope.shape[1]
    whole = pl.BlockSpec((rows, width), lambda j: (0, 0))
    return pl.pallas_call(
        back_kernel,
        grid=(hidden // HIDDEN,),
        in_specs=[
            whole,
            whole,
            pl.BlockSpec((width, HIDDEN), lambda j: (0, j)),
            down_spec(w_down),
            pl.BlockSpec((rows, HIDDEN), lambda j: (0, j)),
        ],
        out_specs=[
            pl.BlockSpec((width, HIDDEN), lambda j: (0, j)),
            pl.BlockSpec((1, HIDDEN), lambda j: (0, j)),
            whole,
        ],
        out_shape=[
            jax.ShapeDtypeStruct((width, hidden), BF16),
            jax.ShapeDtypeStruct((1, hidden), F32),
            jax.ShapeDtypeStruct((rows, width), F32),
        ],
        name="feed_back",
    )(second, cot, w_up, w_down, slope)


def after(array, *earlier):
    return lax.optimization_barrier((array,) + earlier)[0]


def device_bits():
    bits = []
    for axis_name in ALL:
        bit = lax.axis_size(axis_name) // 2
        while bit:
            bits.append((axis_name, bit))
            bit //= 2
    return bits


def make_stages(bits, form="direct"):
    core = [b for b in bits if b[0] == "core"]
    across = [b for b in bits if b[0] == "sx"]
    clip = [b for b in bits if b[0] == "clip"][::-1]
    plane = {"direct": [across + clip[:1]], "x": [across, clip[:1]], "y": [clip[:1], across]}[form]
    stages = [core] + plane + [clip[i : i + 2] for i in range(1, len(clip), 2)]
    return [sorted(stage, key=bits.index) for stage in stages if stage]


def partners(stage):
    count = len(stage)
    return [[(k >> i) & 1 for i in range(count)] for k in range(1, 1 << count)]


def send_to(array, stage, flags):
    axes = tuple(dict.fromkeys(step[0] for step in stage))
    sizes = [lax.axis_size(name) for name in axes]
    flip = [sum(s[1] for s, f in zip(stage, flags) if f and s[0] == name) for name in axes]
    total = math.prod(sizes)
    if len(axes) == 1:
        return lax.ppermute(array, axes[0], [(i, i ^ flip[0]) for i in range(total)])
    pairs = [(i, (i // sizes[1] ^ flip[0]) * sizes[1] + (i % sizes[1] ^ flip[1])) for i in range(total)]
    return lax.ppermute(array, axes, pairs)


def own_bit(step):
    return (lax.axis_index(step[0]) // step[1]) % 2


class Reduction:
    def __init__(self, parts, form="direct", send_type=BF16):
        self.left = device_bits()
        self.stages = make_stages(self.left, form)
        self.arrays = [part.reshape((2,) * len(self.left) + part.shape[1:]) for part in parts]
        self.send_type = send_type

    def pick(self, array, stage, flags):
        left = list(self.left)
        for step, flag in zip(stage, flags):
            axis = left.index(step)
            array = lax.dynamic_index_in_dim(array, own_bit(step) ^ flag, axis, False)
            left.pop(axis)
        return array

    def send(self):
        stage = self.stages.pop(0)
        sent = []
        for flags in partners(stage):
            picked = [self.pick(a, stage, flags).astype(self.send_type) for a in self.arrays]
            sent.append(picked[0] if len(picked) == 1 else jnp.concatenate(picked, axis=-1))
        self.arrays = [self.pick(a, stage, [0] * len(stage)) for a in self.arrays]
        self.left = [step for step in self.left if step not in stage]
        self.got = [send_to(array, stage, f) for array, f in zip(sent, partners(stage))]
        return sent

    def add(self, *earlier):
        got = self.got
        if earlier:
            got = lax.optimization_barrier(tuple(got) + earlier)[: len(got)]
        first = 0
        for i, array in enumerate(self.arrays):
            last = first + array.shape[-1]
            array = array.astype(F32)
            for piece in got:
                array = array + piece[..., first:last].astype(F32)
            self.arrays[i] = array
            first = last


def gather_all(shard, *earlier):
    bits = device_bits()
    array, have = shard, []
    for stage in make_stages(bits)[::-1]:
        if earlier and stage[0][0] == "core":
            array = after(array, *earlier)
        blocks = [([0] * len(stage), array)]
        blocks += [(f, send_to(array, stage, f)) for f in partners(stage)]
        have = sorted(have + stage, key=bits.index)
        axes = [have.index(step) for step in stage]
        array = jnp.expand_dims(array, axes)
        shape = tuple(2 if i in axes else 1 for i in range(array.ndim))
        for flags, block in blocks[1:]:
            here = jnp.full(shape, True)
            for step, flag, axis in zip(stage, flags, axes):
                here &= lax.broadcasted_iota(jnp.int32, shape, axis) == (own_bit(step) ^ flag)
            array = jnp.where(here, jnp.expand_dims(block, axes), array)
    return array.reshape((-1,) + shard.shape)


def body(
    patches,
    mask_index,
    mask_count,
    cotangent,
    w_qkv,
    w_out,
    mask_embed,
    gains,
    biases,
    w_up,
    w_down,
    up_bias,
    avg_qkv,
    avg_out,
    avg_mask,
    avg_gains,
    avg_biases,
    avg_up,
    avg_down,
    avg_up_bias,
):
    clip_count, freq_rows, time_local, width = patches.shape
    seq_names = ("sx", "core")
    seq_size = lax.axis_size("sx") * lax.axis_size("core")
    seq_here = lax.axis_index(seq_names)
    devices = seq_size * lax.axis_size("clip")
    local_len = freq_rows * time_local
    own_clips = clip_count // seq_size
    row_total = seq_size * own_clips * local_len
    grid_shape = (seq_size, own_clips, local_len, width)

    def trade(chunks):
        return [chunks[0]] + [
            lax.ppermute(chunks[k], seq_names, [(i, i ^ k) for i in range(seq_size)])
            for k in range(1, seq_size)
        ]

    def rows_in(array):
        array = array.reshape(seq_size, own_clips, local_len, width)
        return trade([lax.dynamic_index_in_dim(array, seq_here ^ k, 0, False) for k in range(seq_size)])

    def rows_out(array):
        array = array.reshape(grid_shape)
        return trade([array[k] for k in range(seq_size)])

    def in_place(got):
        got = jnp.stack(got)
        order = [lax.dynamic_index_in_dim(got, seq_here ^ k, 0, False) for k in range(seq_size)]
        return jnp.stack(order).reshape(patches.shape)

    share = w_qkv.shape[0]
    spread = up_bias.shape[0] // share
    pairs = width // PAIR

    small = jnp.concatenate([mask_embed[None], gains, biases, up_bias.reshape(spread, share)], axis=0)
    small = jnp.pad(small, ((0, 128 - small.shape[0]), (0, 0))).T
    small_all = gather_all(small)
    patch_rows = jnp.stack(rows_in(patches)).reshape(row_total, width)
    moved_all = tuple(
        0.9 * average + 0.1 * param.astype(F32)
        for average, param in (
            (avg_qkv, w_qkv),
            (avg_out, w_out),
            (avg_mask, mask_embed),
            (avg_gains, gains),
            (avg_biases, biases),
            (avg_up, w_up),
            (avg_down, w_down),
            (avg_up_bias, up_bias),
        )
    )
    small_rows = small_all.reshape(width, -1).astype(F32).T
    mask_vector, gain_rows, bias_rows = small_rows[0], small_rows[1:3], small_rows[3:9]
    up_shift = small_rows[9 : 9 + spread].reshape(spread, devices, share)
    up_shift = up_shift.transpose(1, 0, 2).reshape(1, -1)
    joined_bias = jnp.concatenate([bias_rows[1], jnp.zeros_like(bias_rows[1]), bias_rows[2]])

    hidden = spread * width
    down_share = w_down.shape[0]
    others = [w_down] + [w_up[:, j * width : (j + 1) * width] for j in range(spread)] + [w_out]
    others_all = lax.all_gather(jnp.concatenate(others, axis=0), ALL, axis=0)

    def other_rows(block):
        first = down_share + block * share
        return others_all[:, first : first + share].reshape(width, width)

    full_up = jnp.concatenate([other_rows(j) for j in range(spread)], axis=1)
    full_out = other_rows(spread)
    if down_share == DOWN_ROWS:
        full_down = others_all
    else:
        full_down = others_all[:, :down_share].reshape(-1, DOWN_ROWS, width)

    slot_ids = lax.broadcasted_iota(jnp.int32, (seq_size, freq_rows, time_local), 0)
    freq_ids = lax.broadcasted_iota(jnp.int32, (seq_size, freq_rows, time_local), 1)
    time_ids = lax.broadcasted_iota(jnp.int32, (seq_size, freq_rows, time_local), 2)
    time_ids = time_ids + (slot_ids ^ seq_here) * time_local
    positions = (freq_ids * (time_local * seq_size) + time_ids).reshape(-1)
    own_index = lax.dynamic_slice_in_dim(mask_index, seq_here * own_clips, own_clips, 0)
    own_count = lax.dynamic_slice_in_dim(mask_count, seq_here * own_clips, own_clips, 0)
    live = lax.broadcasted_iota(jnp.int32, own_index.shape, 1) < own_count[:, None]
    live_index = jnp.where(live, own_index, -1)
    hits = live_index[:, :, None] == positions[None, None, :]
    masked = jnp.any(hits, axis=1).reshape(own_clips, seq_size, local_len)
    masked = masked.transpose(1, 0, 2).reshape(row_total, 1)

    start_rows = jnp.where(masked, mask_vector, patch_rows.astype(F32))
    normed_one, norm_pull_one = jax.vjp(layer_norm, start_rows, gain_rows[0], bias_rows[0])
    normed_low = normed_one.astype(BF16)
    full_qkv = gather_all(w_qkv, normed_low).reshape(width, -1)
    joined = (jnp.dot(normed_low, full_qkv, preferred_element_type=F32) + joined_bias).astype(BF16)
    joined = joined.reshape(grid_shape[:3] + (-1,))
    cot_parts = rows_in(after(cotangent, joined))
    mixed, logs = attend_forward(joined, grid_shape, H)
    cot_parts = lax.optimization_barrier(tuple(cot_parts) + (mixed,))[:-1]
    grad_final = jnp.stack(cot_parts).reshape(row_total, width)
    mixed_flat = mixed.reshape(row_total, width)
    middle = start_rows + (jnp.dot(mixed_flat, full_out, preferred_element_type=F32) + bias_rows[3])
    normed_two, norm_pull_two = jax.vjp(layer_norm, middle, gain_rows[1], bias_rows[4])
    second_low = normed_two.astype(BF16)

    def by_owner(part):
        return part.reshape(devices, -1, part.shape[1])

    active_low, slope, grad_down_part = feed_up(second_low, full_up, up_shift, grad_final)
    grad_down = lax.psum_scatter(grad_down_part, ALL, scatter_dimension=0, tiled=True).astype(F32)
    final_low = feed_final(active_low, full_down, middle, bias_rows[5:6])
    grad_up_part, grad_up_shift, grad_second = feed_back(second_low, grad_final, full_up, full_down, slope)
    up_sum = Reduction([by_owner(grad_up_part)])
    sent = up_sum.send()
    grad_second = after(grad_second, *sent)
    grad_mid_norm, grad_gain_two, grad_bias_two = norm_pull_two(grad_second)
    grad_middle = grad_final.astype(F32) + grad_mid_norm
    grad_branch = grad_middle.astype(BF16)
    out_sum = Reduction([by_owner(dot(mixed_flat, grad_branch, 0, 0))])
    sent = out_sum.send()
    grad_out_bias = jnp.sum(grad_branch.astype(F32), axis=0)
    grad_mixed = dot(after(grad_branch, *sent), full_out, 1, 1).astype(BF16).reshape(grid_shape)
    up_sum.add(grad_mixed)
    out_sum.add(grad_mixed)
    up_sum.arrays += out_sum.arrays
    sent = up_sum.send()
    grad_mixed = after(grad_mixed, *sent)

    half = pairs // 2
    piece_one = attend_backward(joined, grad_mixed, logs, H, 0, half).reshape(row_total, -1)
    part_one = dot(normed_low, piece_one, 0, 0)
    mid_sum = Reduction([by_owner(part_one)])
    sent = mid_sum.send()
    up_sum.add(part_one, *sent)
    sent = up_sum.send()
    activations = rows_out(after(final_low, *sent))
    mid_sum.add(*sent)
    sent = mid_sum.send()
    grad_mixed = after(grad_mixed, *sent)
    piece_two = attend_backward(joined, grad_mixed, logs, H, half, pairs - half).reshape(row_total, -1)
    part_two = dot(after(normed_low, piece_two), piece_two, 0, 0)
    last_sum = Reduction([by_owner(part_two)])
    sent = last_sum.send()
    grad_first = feed_first(piece_one, after(piece_two, *sent), full_qkv)
    last_sum.add(grad_first)
    sent = last_sum.send()
    grad_first = after(grad_first, *sent)

    def column_sums(index):
        parts = [
            piece[:, (3 * p + index) * PAIR : (3 * p + index + 1) * PAIR]
            for piece, count in ((piece_one, half), (piece_two, pairs - half))
            for p in range(count)
        ]
        return jnp.concatenate([jnp.sum(part.astype(F32), axis=0) for part in parts])

    grad_query_bias = column_sums(0)
    grad_value_bias = column_sums(2)
    grad_start_norm, grad_gain_one, grad_bias_one = norm_pull_one(grad_first)
    grad_start = grad_middle + grad_start_norm
    input_low = jnp.where(masked, 0.0, grad_start).astype(BF16)
    input_grad = rows_out(input_low)
    activations = in_place(lax.optimization_barrier(tuple(activations) + (input_low,))[:-1])
    grad_mask_part = jnp.sum(jnp.where(masked, grad_start, 0.0), axis=0)
    grad_down_bias = jnp.sum(grad_final.astype(F32), axis=0)
    small_grads = jnp.stack(
        [
            grad_mask_part,
            grad_gain_one,
            grad_gain_two,
            grad_bias_one,
            grad_query_bias,
            grad_value_bias,
            grad_out_bias,
            grad_bias_two,
            grad_down_bias,
        ]
    )
    up_rows = grad_up_shift.reshape(devices, spread, share).transpose(1, 0, 2).reshape(spread, width)
    small_grads = jnp.concatenate([small_grads, up_rows], axis=0)
    small_grads = jnp.pad(small_grads, ((0, 128 - 9 - spread), (0, 0))).T
    small_sum = Reduction([by_owner(small_grads)], send_type=F32)
    small_sum.send()
    up_sum.add(input_low)
    mid_sum.add(input_low)
    small_sum.add(input_low)
    small_sum.send()
    last_sum.add(small_grads)
    small_sum.add()
    last_sum.arrays = mid_sum.arrays + last_sum.arrays + small_sum.arrays
    last_sum.send()
    last_sum.add()
    input_grad = in_place(input_grad)
    for reduction in (up_sum, last_sum):
        while reduction.stages:
            reduction.send()
            reduction.add()
    grad_up = up_sum.arrays[0]
    grad_out = up_sum.arrays[1]
    grad_qkv = natural_order(last_sum.arrays[0], last_sum.arrays[1])
    own_rows = last_sum.arrays[2].T
    grad_up_bias = own_rows[9 : 9 + spread].reshape(-1)

    return (
        activations,
        input_grad,
        grad_qkv,
        grad_out,
        own_rows[0],
        own_rows[1:3],
        own_rows[3:9],
        grad_up,
        grad_down,
        grad_up_bias,
    ) + moved_all


def solution(mesh):
    seq_size, clip_size = mesh.shape["seq"], mesh.shape["clip"]
    fine = Mesh(mesh.devices.reshape(seq_size // 2, 2, clip_size), ALL)
    rows = P("clip", None, ("sx", "core"), None)
    first, second, only = P(ALL, None), P(None, ALL), P(ALL)
    params = (first, first, only, second, second, first, first, only)
    return jax.shard_map(
        body,
        mesh=fine,
        in_specs=(rows, P("clip", None), P("clip"), rows) + params + params,
        out_specs=(rows, rows) + params + params,
        check_vma=False,
    )
```

time: 444 us -> 398 us (0.90)
  Pallas kernels: 48.1 us -> 111 us
  matrix products: 79.1 us -> 18.8 us
  local copies, waits for them, and re-layouts: 81.7 us -> 52.9 us
  starting transfers between devices: 67.9 us -> 55.5 us
    pallas_call x0 -> x5, Pallas kernels: none -> 62.8 us  [the longest x1 23 us: feed_back(): pl.pallas_call(back_kernel, grid=(hidden // HIDDEN,), in_specs=[whole, wh...]
    dot_general x10 -> x4, matrix products: 47.8 us -> 11.7 us  [dot(): lax.dot_general(left_side, right_side, (((left_dim,), (right_dim,)), ((),...]
    dot_general x3 -> x1, matrix products: 29.6 us -> 5.39 us  [body(): jnp.dot(normed_low, full_qkv, preferred_element_type=F32) + joined_bias]
    ppermute x12, waiting for transfers between devices: 0.03 us -> 17.3 us  [trade(): lax.ppermute(chunks[k], seq_names, [(i, i ^ k) for i in range(seq_size)])]
    convert_element_type x16 -> x12, local copies, waits for them, and re-layouts: 18.8 us -> 3.54 us  [send(): self.pick(a, stage, flags).astype(self.send_type)]
    slice x9 -> x4, local copies, waits for them, and re-layouts: 21.2 us -> 6.07 us  [the longest x1 3.23 us: other_rows(): return others_all[:, first:first + share].reshape(width, width)]
    ppermute x28 -> x19, starting transfers between devices: 35.2 us -> 22.7 us  [send_to(): lax.ppermute(array, axes[0], [(i, i ^ flip[0]) for i in range(total)])]
    ppermute x28 -> x19, waiting for transfers between devices: 20.6 us -> 8.47 us  [send_to(): lax.ppermute(array, axes[0], [(i, i ^ flip[0]) for i in range(total)])]
  transfers between devices with their start and end apart: 62 -> 51, of which waited for: 17 -> 15; matrix products, arithmetic and copies ran while one was open for 34% -> 26% of each run, Pallas kernels for 11% -> 17%
where the time goes in v3:
time: 398 us; the launch traced here: 394 us
  Pallas kernels  111 us (28%)
  waiting for transfers between devices  76.8 us (19%)
  other arithmetic  62.9 us (16%)
  starting transfers between devices  55.5 us (14%)
  local copies, waits for them, and re-layouts  52.9 us (13%)
  matrix products  18.8 us (5%)
  between operations  15.6 us (4%)
    ppermute x18, waiting for transfers between devices, send_to(): return lax.ppermute(array, axes, pairs)  51 us
    pallas_call x2, Pallas kernels, attend_backward(): pl.pallas_call(partial(backward_kernel, head_size=head_size, scale=1.0 /...  30.3 us
    ppermute x18, starting transfers between devices, send_to(): return lax.ppermute(array, axes, pairs)  26.3 us
    pallas_call x1, Pallas kernels, feed_back(): pl.pallas_call(back_kernel, grid=(hidden // HIDDEN,), in_specs=[whole, wh...  23 us
    ppermute x19, starting transfers between devices, send_to(): lax.ppermute(array, axes[0], [(i, i ^ flip[0]) for i in range(total)])  22.7 us
    pallas_call x1, Pallas kernels, feed_up(): pl.pallas_call(up_kernel, grid=(hidden // HIDDEN,), in_specs=[whole, pl.B...  19.6 us
    pallas_call x1, Pallas kernels, attend_forward(): pl.pallas_call(partial(forward_kernel, head_size=head_size, scale=1.0 / m...  18.1 us
    ppermute x12, waiting for transfers between devices, trade(): lax.ppermute(chunks[k], seq_names, [(i, i ^ k) for i in range(seq_size)])  17.3 us
  transfers between devices with their start and end apart: 51, of which 15 were waited for; matrix products, arithmetic and copies ran while one was open for 26% of the time, Pallas kernels for 17%

profile of v3, /device:TPU:0, one launch (start us, length us, event | category | flops | bytes accessed | tf_op | source)
XLA Modules:
  0.0 393.5 jit_solution(1370134713116223242)
XLA Ops:
  14.3 4.1 %collective-permute-start.2 = (bf16[24,128]{0,1:T(8,128)(2,1)S(1)}, bf16[24,128]{0,1:T(8,128)(2,1)S(1)}, u32[]{:S(2)}, u32[]{:S(2)}) collective-permute-start(bf16[24,128]{0,1:T(8,128)(2,1)S(1)} %fusion.59), channel_id=1, source_target_pairs={{0,4},{1,5},{2,6},{3,7},{4,0},{5,1},{6,2},{7,3},{8,12},{9,13},{10,... | collective-permute-start | bytes 18440 | tf_op jit(solution)/shard_map/ppermute | solution.py:304
  20.1 1.9 collective-permute-start.12
  22.0 2.5 collective-permute-start.11
  30.8 2.2 constant_dynamic-slice_fusion.18
  38.8 2.4 collective-permute-done.3
  47.9 5.8 %collective-permute-done.9 = bf16[2,128,768]{2,1,0:T(8,128)(2,1)} collective-permute-done((bf16[2,128,768]{2,1,0:T(8,128)(2,1)}, bf16[2,128,768]{2,1,0:T(8,128)(2,1)}, u32[]{:S(2)}, u32[]{:S(2)}) %collective-permute-start.9) | collective-permute-done | bytes 393248 | tf_op jit(solution)/shard_map/ppermute | solution.py:407
  55.1 11.5 %collective-permute-done.8 = bf16[2,128,768]{2,1,0:T(8,128)(2,1)} collective-permute-done((bf16[2,128,768]{2,1,0:T(8,128)(2,1)S(1)}, bf16[2,128,768]{2,1,0:T(8,128)(2,1)}, u32[]{:S(2)}, u32[]{:S(2)}) %collective-permute-start.8) | collective-permute-done | bytes 393248 | tf_op jit(solution)/shard_map/ppermute | solution.py:407
  66.6 2.0 fusion.3
  69.5 1.9 add_convert_fusion.2
  71.5 4.5 %collective-permute-done.15 = bf16[2,2,24,2304]{3,2,1,0:T(8,128)(2,1)S(1)} collective-permute-done((bf16[2,2,24,2304]{3,2,1,0:T(8,128)(2,1)S(1)}, bf16[2,2,24,2304]{3,2,1,0:T(8,128)(2,1)S(1)}, u32[]{:S(2)}, u32[]{:S(2)}) %collective-permute-start.15) | collective-permute-done | bytes 442400 | tf_op jit(solution)/shard_map/ppermute | solution.py:306
  76.0 16.2 %collective-permute-done.13 = bf16[2,2,24,2304]{3,2,1,0:T(8,128)(2,1)S(1)} collective-permute-done((bf16[2,2,24,2304]{3,2,1,0:T(8,128)(2,1)S(1)}, bf16[2,2,24,2304]{3,2,1,0:T(8,128)(2,1)S(1)}, u32[]{:S(2)}, u32[]{:S(2)}) %collective-permute-start.13) | collective-permute-done | bytes 442400 | tf_op jit(solution)/shard_map/ppermute | solution.py:306
  92.6 1.7 collective-permute-start.16
  98.8 5.4 %add_convert_fusion = bf16[1024,2304]{1,0:T(8,128)(2,1)} fusion(bf16[1024,768]{1,0:T(8,128)(2,1)S(1)} %bitcast.304, bf16[768,2304]{1,0:T(8,128)(2,1)S(1)} %bitcast.310, f32[2304]{0:T(1024)S(1)} %pad_maximum_fusion.16), kind=kOutput, calls=%fused_computation | convolution fusion | flops 3628597248 | bytes 9839616 | tf_op jit(solution)/shard_map/dot_general | solution.py:484
  104.8 1.9 collective-permute-start.18
  108.9 18.1 %attend_forward.1 = (bf16[4,2,128,768]{3,2,1,0:T(8,128)(2,1)}, f32[2,6,2,512]{3,2,1,0:T(2,128)}) custom-call(bf16[4,2,128,2304]{3,2,1,0:T(8,128)(2,1)} %bitcast.280, bf16[4,2,128,2304]{3,2,1,0:T(8,128)(2,1)} %bitcast.281, bf16[4,2,128,2304]{3,2,1,0:T(8,128)(2,1)} %bitcast.282), custom_call_target="tpu_custom_call" | custom-call | tf_op jit(solution)/shard_map/attend_forward/pallas_call | solution.py:83
  126.9 2.6 copy.105
  131.1 3.2 fusion.76
  138.6 2.5 pad_maximum_fusion.w_ref.w_up_ref
  141.1 19.6 %feed_up.1 = (bf16[1024,3072]{1,0:T(8,128)(2,1)}, f32[1024,3072]{1,0:T(8,128)}, bf16[3072,768]{1,0:T(8,128)(2,1)}) custom-call(bf16[1024,768]{1,0:T(8,128)(2,1)} %add_convert_fusion.1.second_ref, bf16[768,3072]{1,0:T(8,128)(2,1)} %pad_maximum_fusion.w_ref.w_up_ref, f32[1,3072]{1,0:T(1,128)} %reshape.766.bias_ref, bf16[1024,768]{1,0:T(8,128)(2,1)} %bitcast.292), custom_call_target="tpu_custom_call" | custom-call | tf_op jit(solution)/shard_map/feed_up/pallas_call | solution.py:181
  160.7 23.0 %feed_back.1 = (bf16[768,3072]{1,0:T(8,128)(2,1)}, f32[1,3072]{1,0:T(1,128)}, f32[1024,768]{1,0:T(8,128)}) custom-call(bf16[1024,768]{1,0:T(8,128)(2,1)} %add_convert_fusion.1.second_ref, bf16[1024,768]{1,0:T(8,128)(2,1)} %bitcast.293, bf16[768,3072]{1,0:T(8,128)(2,1)} %pad_maximum_fusion.w_ref.w_up_ref, bf16[32,216,768]{2,1,0:T(8,128)(2,1)} %bitcast.290, ...), custom_call_target="tpu_custom_call" | custom-call | tf_op jit(solution)/shard_map/feed_back/pallas_call | solution.py:246
  183.7 4.2 %constant_dynamic-slice_fusion.17 = (bf16[2,1,2,2,2,24,3072]{6,5,4,3,2,1,0:T(8,128)(2,1)}, bf16[2,1,2,2,2,24,3072]{6,5,4,3,2,1,0:T(8,128)(2,1)S(1)}) fusion(bf16[2,2,2,2,2,24,3072]{6,5,4,3,2,1,0:T(8,128)(2,1)} %bitcast.309, s32[]{:T(128)S(6)} %select_n.700, s32[]{:T(128)S(6)} %select_n.701), kind=kLoop, calls=%fused_computation.203 | loop fusion | bytes 9437192 | tf_op jit(solution)/shard_map/jit(dynamic_index_in_dim)/dynamic_slice | solution.py:324
  192.2 1.9 fusion.75
  200.4 2.2 bitcast_select_fusion.q_ref.k_ref.v_ref
  207.1 10.0 %feed_final.1 = bf16[1024,768]{1,0:T(8,128)(2,1)} custom-call(bf16[1024,3072]{1,0:T(8,128)(2,1)} %get-tuple-element.68.active_ref, bf16[32,216,768]{2,1,0:T(8,128)(2,1)} %bitcast.291, f32[1024,768]{1,0:T(8,128)} %copy-done, f32[1,768]{1,0:T(1,128)} %get-tuple-element.266.bias_ref), custom_call_target="tpu_custom_call" | custom-call | tf_op jit(solution)/shard_map/feed_final/pallas_call | solution.py:209
  217.1 2.6 convolution_convert_fusion
  221.7 2.6 convert_add_fusion
  226.7 1.9 collective-permute-start.22
  232.0 15.1 %attend_backward.2 = bf16[4,2,128,1152]{3,2,1,0:T(8,128)(2,1)} custom-call(bf16[4,2,128,2304]{3,2,1,0:T(8,128)(2,1)} %bitcast.283, bf16[4,2,128,2304]{3,2,1,0:T(8,128)(2,1)} %bitcast.284, bf16[4,2,128,2304]{3,2,1,0:T(8,128)(2,1)} %bitcast.285, bf16[4,2,128,768]{3,2,1,0:T(8,128)(2,1)} %bitcast.301, f32[2,6,2,512]{3,2,1,0:T(2,128)} %get-tuple-element.77.log_ref), custom_call_target="tpu_custom_call" | custom-call | tf_op jit(solution)/shard_map/attend_backward/pallas_call | solution.py:103
  247.1 4.1 %fusion.80 = f32[768,1152,1,1]{1,0,3,2:T(8,128)S(1)} fusion(bf16[4,2,128,768]{3,2,1,0:T(8,128)(2,1)S(1)} %copy-done.19, bf16[4,2,128,1152]{3,2,1,0:T(8,128)(2,1)} %attend_backward.2), kind=kOutput, calls=%fused_computation.276 | convolution fusion | flops 1811939328 | bytes 7471104 | tf_op jit(solution)/shard_map/dot_general | solution.py:25
  251.7 15.4 %collective-permute-done.23 = bf16[2,2,24,3840]{3,2,1,0:T(8,128)(2,1)} collective-permute-done((bf16[2,2,24,3840]{3,2,1,0:T(8,128)(2,1)}, bf16[2,2,24,3840]{3,2,1,0:T(8,128)(2,1)}, u32[]{:S(2)}, u32[]{:S(2)}) %collective-permute-start.23) | collective-permute-done | bytes 737312 | tf_op jit(solution)/shard_map/ppermute | solution.py:306
  268.2 2.0 fusion.8
  274.6 15.2 %attend_backward.3 = bf16[4,2,128,1152]{3,2,1,0:T(8,128)(2,1)} custom-call(bf16[4,2,128,2304]{3,2,1,0:T(8,128)(2,1)} %bitcast.286, bf16[4,2,128,2304]{3,2,1,0:T(8,128)(2,1)} %bitcast.287, bf16[4,2,128,2304]{3,2,1,0:T(8,128)(2,1)} %bitcast.288, bf16[4,2,128,768]{3,2,1,0:T(8,128)(2,1)} %bitcast.302, f32[2,6,2,512]{3,2,1,0:T(2,128)} %get-tuple-element.77.log_ref), custom_call_target="tpu_custom_call" | custom-call | tf_op jit(solution)/shard_map/attend_backward/pallas_call | solution.py:103
  289.9 2.8 copy.109
  292.7 3.6 fusion.81
  303.4 8.4 %feed_first.1 = f32[1024,768]{1,0:T(8,128)} custom-call(bf16[1024,1152]{1,0:T(8,128)(2,1)} %bitcast.294, bf16[1024,1152]{1,0:T(8,128)(2,1)} %bitcast.296, bf16[768,2304]{1,0:T(8,128)(2,1)} %bitcast_select_fusion.q_ref.k_ref.v_ref, bf16[768,2304]{1,0:T(8,128)(2,1)} %bitcast_select_fusion.q_ref.k_ref.v_ref, bf16[768,2304]{1,0:T(8,128)(2,1)} %bitcast_select_fusion.q_ref.k_ref.v_ref), custom_call_target="tpu_custom_call" | custom-call | tf_op jit(solution)/shard_map/feed_first/pallas_call | solution.py:128
  311.9 2.4 collective-permute-start.34
  314.2 1.9 bitcast_add_fusion
  317.1 1.8 multiply_reduce_fusion.1
  318.9 1.7 fusion.74
  324.2 2.7 collective-permute-start.47
  327.1 1.9 collective-permute-start.48
  329.7 1.9 copy.113
  336.2 4.3 %collective-permute-start.38 = (bf16[2,2,24,1152]{3,2,1,0:T(8,128)(2,1)}, bf16[2,2,24,1152]{3,2,1,0:T(8,128)(2,1)S(1)}, u32[]{:S(2)}, u32[]{:S(2)}) collective-permute-start(bf16[2,2,24,1152]{3,2,1,0:T(8,128)(2,1)} %get-tuple-element.224), channel_id=1, source_target_pairs={{0,17},{1,16},{2,19},{3,18},{4,21},{5,20},{6,23},{7,22},{16,1},{17... | collective-permute-start | bytes 663560 | tf_op jit(solution)/shard_map/ppermute | solution.py:306
  344.4 2.0 fusion.20
  353.3 9.9 %collective-permute-done.42 = f32[2,2,24,128]{3,2,1,0:T(8,128)S(1)} collective-permute-done((f32[2,2,24,128]{3,2,1,0:T(8,128)S(1)}, f32[2,2,24,128]{3,2,1,0:T(8,128)S(1)}, u32[]{:S(2)}, u32[]{:S(2)}) %collective-permute-start.42) | collective-permute-done | bytes 49184 | tf_op jit(solution)/shard_map/ppermute | solution.py:306
  365.3 3.5 collective-permute-start.43
  370.1 2.1 collective-permute-done.45
  372.2 3.6 collective-permute-done.43
  (364 shorter events, 113.2 us)
Async XLA Ops:
  7.2 123.9 %all-gather.3.cloned.1.call-start = ((), (), s32[]{:S(2)}) async-start(), calls=%async_computation.2 | async-start | bytes 10948608 | tf_op jit(solution)/shard_map/all_gather | solution.py:454
  12.8 372.0 %reduce-scatter.2.cloned.1.call-start = ((), (), s32[]{:S(2)}) async-start(), calls=%async_computation.1 | async-start | bytes 4866048 | tf_op jit(solution)/shard_map/reduce_scatter | solution.py:499
  14.3 18.7 %collective-permute-start.2 = (bf16[24,128]{0,1:T(8,128)(2,1)S(1)}, bf16[24,128]{0,1:T(8,128)(2,1)S(1)}, u32[]{:S(2)}, u32[]{:S(2)}) collective-permute-start(bf16[24,128]{0,1:T(8,128)(2,1)S(1)} %fusion.59), channel_id=1, source_target_pairs={{0,4},{1,5},{2,6},{3,7},{4,0},{5,1},{6,2},{7,3},{8,12},{9,13},{10,... | collective-permute-start | bytes 18440 | tf_op jit(solution)/shard_map/ppermute | solution.py:304
  18.5 14.7 %collective-permute-start.1 = (bf16[24,128]{0,1:T(8,128)(2,1)S(1)}, bf16[24,128]{0,1:T(8,128)(2,1)S(1)}, u32[]{:S(2)}, u32[]{:S(2)}) collective-permute-start(bf16[24,128]{0,1:T(8,128)(2,1)S(1)} %fusion.59), channel_id=1, source_target_pairs={{0,2},{1,3},{2,0},{3,1},{4,6},{5,7},{6,4},{7,5},{8,10},{9,11},{10,... | collective-permute-start | bytes 18440 | tf_op jit(solution)/shard_map/ppermute | solution.py:304
  20.1 13.2 %collective-permute-start = (bf16[24,128]{0,1:T(8,128)(2,1)S(1)}, bf16[24,128]{0,1:T(8,128)(2,1)S(1)}, u32[]{:S(2)}, u32[]{:S(2)}) collective-permute-start(bf16[24,128]{0,1:T(8,128)(2,1)S(1)} %fusion.59), channel_id=1, source_target_pairs={{0,6},{1,7},{2,4},{3,5},{4,2},{5,3},{6,0},{7,1},{8,14},{9,15},{10,... | collective-permute-start | bytes 18440 | tf_op jit(solution)/shard_map/ppermute | solution.py:304
  20.1 22.0 %collective-permute-start.12 = (bf16[24,2304]{1,0:T(8,128)(2,1)}, bf16[24,2304]{1,0:T(8,128)(2,1)S(1)}, u32[]{:S(2)}, u32[]{:S(2)}) collective-permute-start(bf16[24,2304]{1,0:T(8,128)(2,1)} %param.24), channel_id=1, source_target_pairs={{0,4},{1,5},{2,6},{3,7},{4,0},{5,1},{6,2},{7,3},{8,12},{9,13},{10,... | collective-permute-start | bytes 331784 | tf_op jit(solution)/shard_map/ppermute | solution.py:304
  22.0 20.2 %collective-permute-start.11 = (bf16[24,2304]{1,0:T(8,128)(2,1)}, bf16[24,2304]{1,0:T(8,128)(2,1)S(1)}, u32[]{:S(2)}, u32[]{:S(2)}) collective-permute-start(bf16[24,2304]{1,0:T(8,128)(2,1)} %param.24), channel_id=1, source_target_pairs={{0,2},{1,3},{2,0},{3,1},{4,6},{5,7},{6,4},{7,5},{8,10},{9,11},{10,... | collective-permute-start | bytes 331784 | tf_op jit(solution)/shard_map/ppermute | solution.py:304
  36.5 4.7 %collective-permute-start.3 = (bf16[2,2,24,128]{3,2,1,0:T(8,128)(2,1)S(1)}, bf16[2,2,24,128]{3,2,1,0:T(8,128)(2,1)S(1)}, u32[]{:S(2)}, u32[]{:S(2)}) collective-permute-start(bf16[2,2,24,128]{3,2,1,0:T(8,128)(2,1)S(1)} %select_select_fusion.3), channel_id=1, source_target_pairs={{0,17},{1,16},{2,19},{3,18},{4,21},{5,20},{6,23},{7,22},{16,1},{17... | collective-permute-start | bytes 73736 | tf_op jit(solution)/shard_map/ppermute | solution.py:306
  37.4 6.5 %collective-permute-start.10 = (bf16[24,2304]{1,0:T(8,128)(2,1)S(1)}, bf16[24,2304]{1,0:T(8,128)(2,1)S(1)}, u32[]{:S(2)}, u32[]{:S(2)}) collective-permute-start(bf16[24,2304]{1,0:T(8,128)(2,1)S(1)} %copy-done.36), channel_id=1, source_target_pairs={{0,6},{1,7},{2,4},{3,5},{4,2},{5,3},{6,0},{7,1},{8,14},{9,15},{10,... | collective-permute-start | bytes 331784 | tf_op jit(solution)/shard_map/ppermute | solution.py:304
  38.8 14.9 %collective-permute-start.9 = (bf16[2,128,768]{2,1,0:T(8,128)(2,1)}, bf16[2,128,768]{2,1,0:T(8,128)(2,1)}, u32[]{:S(2)}, u32[]{:S(2)}) collective-permute-start(bf16[2,128,768]{2,1,0:T(8,128)(2,1)} %get-tuple-element.251), channel_id=1, source_target_pairs={{0,24},{8,16},{16,8},{24,0},{1,25},{9,17},{17,9},{25,1},{2,26},{10... | collective-permute-start | bytes 1179656 | tf_op jit(solution)/shard_map/ppermute | solution.py:407
  41.2 25.4 %collective-permute-start.8 = (bf16[2,128,768]{2,1,0:T(8,128)(2,1)S(1)}, bf16[2,128,768]{2,1,0:T(8,128)(2,1)}, u32[]{:S(2)}, u32[]{:S(2)}) collective-permute-start(bf16[2,128,768]{2,1,0:T(8,128)(2,1)S(1)} %get-tuple-element.252), channel_id=1, source_target_pairs={{0,16},{8,24},{16,0},{24,8},{1,17},{9,25},{17,1},{25,9},{2,18},{10... | collective-permute-start | bytes 1179656 | tf_op jit(solution)/shard_map/ppermute | solution.py:407
  42.1 24.6 %collective-permute-start.7 = (bf16[2,128,768]{2,1,0:T(8,128)(2,1)S(1)}, bf16[2,128,768]{2,1,0:T(8,128)(2,1)}, u32[]{:S(2)}, u32[]{:S(2)}) collective-permute-start(bf16[2,128,768]{2,1,0:T(8,128)(2,1)S(1)} %get-tuple-element.253), channel_id=1, source_target_pairs={{0,8},{8,0},{16,24},{24,16},{1,9},{9,1},{17,25},{25,17},{2,10},{10... | collective-permute-start | bytes 1179656 | tf_op jit(solution)/shard_map/ppermute | solution.py:407
  44.1 31.9 %collective-permute-start.15 = (bf16[2,2,24,2304]{3,2,1,0:T(8,128)(2,1)S(1)}, bf16[2,2,24,2304]{3,2,1,0:T(8,128)(2,1)S(1)}, u32[]{:S(2)}, u32[]{:S(2)}) collective-permute-start(bf16[2,2,24,2304]{3,2,1,0:T(8,128)(2,1)S(1)} %select_select_fusion.1), channel_id=1, source_target_pairs={{0,16},{1,17},{2,18},{3,19},{4,20},{5,21},{6,22},{7,23},{16,0},{17... | collective-permute-start | bytes 1327112 | tf_op jit(solution)/shard_map/ppermute | solution.py:306
  45.6 30.4 %collective-permute-start.14 = (bf16[2,2,24,2304]{3,2,1,0:T(8,128)(2,1)S(1)}, bf16[2,2,24,2304]{3,2,1,0:T(8,128)(2,1)S(1)}, u32[]{:S(2)}, u32[]{:S(2)}) collective-permute-start(bf16[2,2,24,2304]{3,2,1,0:T(8,128)(2,1)S(1)} %select_select_fusion.1), channel_id=1, source_target_pairs={{0,1},{1,0},{2,3},{3,2},{4,5},{5,4},{6,7},{7,6},{16,17},{17,16},{1... | collective-permute-start | bytes 1327112 | tf_op jit(solution)/shard_map/ppermute | solution.py:306
  53.7 38.5 %collective-permute-start.13 = (bf16[2,2,24,2304]{3,2,1,0:T(8,128)(2,1)S(1)}, bf16[2,2,24,2304]{3,2,1,0:T(8,128)(2,1)S(1)}, u32[]{:S(2)}, u32[]{:S(2)}) collective-permute-start(bf16[2,2,24,2304]{3,2,1,0:T(8,128)(2,1)S(1)} %select_select_fusion.1), channel_id=1, source_target_pairs={{0,17},{1,16},{2,19},{3,18},{4,21},{5,20},{6,23},{7,22},{16,1},{17... | collective-permute-start | bytes 1327112 | tf_op jit(solution)/shard_map/ppermute | solution.py:306
  92.6 5.0 %collective-permute-start.16 = (bf16[2,2,2,2,24,2304]{5,4,3,2,1,0:T(8,128)(2,1)S(1)}, bf16[2,2,2,2,24,2304]{5,4,3,2,1,0:T(8,128)(2,1)S(1)}, u32[]{:S(2)}, u32[]{:S(2)}) collective-permute-start(bf16[2,2,2,2,24,2304]{5,4,3,2,1,0:T(8,128)(2,1)S(1)} %select_select_fusion), channel_id=1, source_target_pairs={{0,8},{8,0},{1,9},{9,1},{2,10},{10,2},{3,11},{11,3},{4,12},{12,4},... | collective-permute-start | bytes 5308424 | tf_op jit(solution)/shard_map/ppermute | solution.py:304
  104.4 25.2 %collective-permute-start.17 = (bf16[2,128,768]{2,1,0:T(8,128)(2,1)S(1)}, bf16[2,128,768]{2,1,0:T(8,128)(2,1)S(1)}, u32[]{:S(2)}, u32[]{:S(2)}) collective-permute-start(bf16[2,128,768]{2,1,0:T(8,128)(2,1)S(1)} %get-tuple-element.248), channel_id=1, source_target_pairs={{0,8},{8,0},{16,24},{24,16},{1,9},{9,1},{17,25},{25,17},{2,10},{10... | collective-permute-start | bytes 1179656 | tf_op jit(solution)/shard_map/ppermute | solution.py:407
  104.8 24.7 %collective-permute-start.18 = (bf16[2,128,768]{2,1,0:T(8,128)(2,1)S(1)}, bf16[2,128,768]{2,1,0:T(8,128)(2,1)S(1)}, u32[]{:S(2)}, u32[]{:S(2)}) collective-permute-start(bf16[2,128,768]{2,1,0:T(8,128)(2,1)S(1)} %get-tuple-element.247), channel_id=1, source_target_pairs={{0,16},{8,24},{16,0},{24,8},{1,17},{9,25},{17,1},{25,9},{2,18},{10... | collective-permute-start | bytes 1179656 | tf_op jit(solution)/shard_map/ppermute | solution.py:407
  106.7 22.9 %collective-permute-start.19 = (bf16[2,128,768]{2,1,0:T(8,128)(2,1)S(1)}, bf16[2,128,768]{2,1,0:T(8,128)(2,1)S(1)}, u32[]{:S(2)}, u32[]{:S(2)}) collective-permute-start(bf16[2,128,768]{2,1,0:T(8,128)(2,1)S(1)} %get-tuple-element.246), channel_id=1, source_target_pairs={{0,24},{8,16},{16,8},{24,0},{1,25},{9,17},{17,9},{25,1},{2,26},{10... | collective-permute-start | bytes 1179656 | tf_op jit(solution)/shard_map/ppermute | solution.py:407
  189.5 31.8 %collective-permute-start.20 = (bf16[2,2,2,2,24,3072]{5,4,2,1,3,0:T(8,128)(2,1)}, bf16[2,2,2,2,24,3072]{5,4,2,1,3,0:T(8,128)(2,1)}, u32[]{:S(2)}, u32[]{:S(2)}) collective-permute-start(bf16[2,2,2,2,24,3072]{5,4,2,1,3,0:T(8,128)(2,1)} %bitcast.279), channel_id=1, source_target_pairs={{0,8},{8,0},{1,9},{9,1},{2,10},{10,2},{3,11},{11,3},{4,12},{12,4},... | collective-permute-start | bytes 7077896 | tf_op jit(solution)/shard_map/ppermute | solution.py:304
  199.6 20.2 %collective-permute-start.21 = (bf16[2,2,2,2,24,768]{5,4,3,2,1,0:T(8,128)(2,1)S(1)}, bf16[2,2,2,2,24,768]{5,4,3,2,1,0:T(8,128)(2,1)}, u32[]{:S(2)}, u32[]{:S(2)}) collective-permute-start(bf16[2,2,2,2,24,768]{5,4,3,2,1,0:T(8,128)(2,1)S(1)} %fusion.11), channel_id=1, source_target_pairs={{0,8},{8,0},{1,9},{9,1},{2,10},{10,2},{3,11},{11,3},{4,12},{12,4},... | collective-permute-start | bytes 1769480 | tf_op jit(solution)/shard_map/ppermute | solution.py:304
  226.7 25.0 %collective-permute-start.22 = (bf16[2,2,24,3840]{3,2,1,0:T(8,128)(2,1)}, bf16[2,2,24,3840]{3,2,1,0:T(8,128)(2,1)S(1)}, u32[]{:S(2)}, u32[]{:S(2)}) collective-permute-start(bf16[2,2,24,3840]{3,2,1,0:T(8,128)(2,1)} %pad_maximum_fusion.7), channel_id=1, source_target_pairs={{0,16},{1,17},{2,18},{3,19},{4,20},{5,21},{6,22},{7,23},{16,0},{17... | collective-permute-start | bytes 2211848 | tf_op jit(solution)/shard_map/ppermute | solution.py:306
  229.5 37.6 %collective-permute-start.23 = (bf16[2,2,24,3840]{3,2,1,0:T(8,128)(2,1)}, bf16[2,2,24,3840]{3,2,1,0:T(8,128)(2,1)}, u32[]{:S(2)}, u32[]{:S(2)}) collective-permute-start(bf16[2,2,24,3840]{3,2,1,0:T(8,128)(2,1)} %pad_maximum_fusion.8), channel_id=1, source_target_pairs={{0,1},{1,0},{2,3},{3,2},{4,5},{5,4},{6,7},{7,6},{16,17},{17,16},{1... | collective-permute-start | bytes 2211848 | tf_op jit(solution)/shard_map/ppermute | solution.py:306
  231.1 36.0 %collective-permute-start.24 = (bf16[2,2,24,3840]{3,2,1,0:T(8,128)(2,1)}, bf16[2,2,24,3840]{3,2,1,0:T(8,128)(2,1)}, u32[]{:S(2)}, u32[]{:S(2)}) collective-permute-start(bf16[2,2,24,3840]{3,2,1,0:T(8,128)(2,1)} %pad_maximum_fusion.9), channel_id=1, source_target_pairs={{0,17},{1,16},{2,19},{3,18},{4,21},{5,20},{6,23},{7,22},{16,1},{17... | collective-permute-start | bytes 2211848 | tf_op jit(solution)/shard_map/ppermute | solution.py:306
  251.3 21.1 %collective-permute-start.28 = (bf16[2,2,2,2,24,1152]{5,4,2,1,3,0:T(8,128)(2,1)S(1)}, bf16[2,2,2,2,24,1152]{5,4,2,1,3,0:T(8,128)(2,1)S(1)}, u32[]{:S(2)}, u32[]{:S(2)}) collective-permute-start(bf16[2,2,2,2,24,1152]{5,4,2,1,3,0:T(8,128)(2,1)S(1)} %fusion.9), channel_id=1, source_target_pairs={{0,8},{8,0},{1,9},{9,1},{2,10},{10,2},{3,11},{11,3},{4,12},{12,4},... | collective-permute-start | bytes 2654216 | tf_op jit(solution)/shard_map/ppermute | solution.py:304
  297.4 14.5 %collective-permute-start.29 = (bf16[2,2,2,2,24,1152]{5,4,2,1,3,0:T(8,128)(2,1)}, bf16[2,2,2,2,24,1152]{5,4,2,1,3,0:T(8,128)(2,1)}, u32[]{:S(2)}, u32[]{:S(2)}) collective-permute-start(bf16[2,2,2,2,24,1152]{5,4,2,1,3,0:T(8,128)(2,1)} %fusion.10), channel_id=1, source_target_pairs={{0,8},{8,0},{1,9},{9,1},{2,10},{10,2},{3,11},{11,3},{4,12},{12,4},... | collective-permute-start | bytes 2654216 | tf_op jit(solution)/shard_map/ppermute | solution.py:304
  300.0 22.9 %collective-permute-start.25 = (bf16[2,128,768]{2,1,0:T(8,128)(2,1)}, bf16[2,128,768]{2,1,0:T(8,128)(2,1)}, u32[]{:S(2)}, u32[]{:S(2)}) collective-permute-start(bf16[2,128,768]{2,1,0:T(8,128)(2,1)} %bitcast.69), channel_id=1, source_target_pairs={{0,8},{8,0},{16,24},{24,16},{1,9},{9,1},{17,25},{25,17},{2,10},{10... | collective-permute-start | bytes 1179656 | tf_op jit(solution)/shard_map/ppermute | solution.py:407
  300.1 24.2 %collective-permute-start.26 = (bf16[2,128,768]{2,1,0:T(8,128)(2,1)}, bf16[2,128,768]{2,1,0:T(8,128)(2,1)}, u32[]{:S(2)}, u32[]{:S(2)}) collective-permute-start(bf16[2,128,768]{2,1,0:T(8,128)(2,1)} %bitcast.70), channel_id=1, source_target_pairs={{0,16},{8,24},{16,0},{24,8},{1,17},{9,25},{17,1},{25,9},{2,18},{10... | collective-permute-start | bytes 1179656 | tf_op jit(solution)/shard_map/ppermute | solution.py:407
  301.2 23.0 %collective-permute-start.27 = (bf16[2,128,768]{2,1,0:T(8,128)(2,1)}, bf16[2,128,768]{2,1,0:T(8,128)(2,1)}, u32[]{:S(2)}, u32[]{:S(2)}) collective-permute-start(bf16[2,128,768]{2,1,0:T(8,128)(2,1)} %bitcast.71), channel_id=1, source_target_pairs={{0,24},{8,16},{16,8},{24,0},{1,25},{9,17},{17,9},{25,1},{2,26},{10... | collective-permute-start | bytes 1179656 | tf_op jit(solution)/shard_map/ppermute | solution.py:407
  301.9 25.1 %collective-permute-start.33 = (bf16[2,2,24,1152]{3,2,1,0:T(8,128)(2,1)}, bf16[2,2,24,1152]{3,2,1,0:T(8,128)(2,1)}, u32[]{:S(2)}, u32[]{:S(2)}) collective-permute-start(bf16[2,2,24,1152]{3,2,1,0:T(8,128)(2,1)} %get-tuple-element.229), channel_id=1, source_target_pairs={{0,16},{1,17},{2,18},{3,19},{4,20},{5,21},{6,22},{7,23},{16,0},{17... | collective-permute-start | bytes 663560 | tf_op jit(solution)/shard_map/ppermute | solution.py:306
  311.9 19.8 %collective-permute-start.34 = (bf16[2,2,24,1152]{3,2,1,0:T(8,128)(2,1)}, bf16[2,2,24,1152]{3,2,1,0:T(8,128)(2,1)}, u32[]{:S(2)}, u32[]{:S(2)}) collective-permute-start(bf16[2,2,24,1152]{3,2,1,0:T(8,128)(2,1)} %get-tuple-element.228), channel_id=1, source_target_pairs={{0,1},{1,0},{2,3},{3,2},{4,5},{5,4},{6,7},{7,6},{16,17},{17,16},{1... | collective-permute-start | bytes 663560 | tf_op jit(solution)/shard_map/ppermute | solution.py:306
  322.9 10.3 %collective-permute-start.35 = (bf16[2,2,24,1152]{3,2,1,0:T(8,128)(2,1)}, bf16[2,2,24,1152]{3,2,1,0:T(8,128)(2,1)}, u32[]{:S(2)}, u32[]{:S(2)}) collective-permute-start(bf16[2,2,24,1152]{3,2,1,0:T(8,128)(2,1)} %get-tuple-element.227), channel_id=1, source_target_pairs={{0,17},{1,16},{2,19},{3,18},{4,21},{5,20},{6,23},{7,22},{16,1},{17... | collective-permute-start | bytes 663560 | tf_op jit(solution)/shard_map/ppermute | solution.py:306
  324.2 12.0 %collective-permute-start.46 = (bf16[24,3840]{1,0:T(8,128)(2,1)}, bf16[24,3840]{1,0:T(8,128)(2,1)}, u32[]{:S(2)}, u32[]{:S(2)}) collective-permute-start(bf16[24,3840]{1,0:T(8,128)(2,1)} %pad_maximum_fusion.10), channel_id=1, source_target_pairs={{0,4},{1,5},{2,6},{3,7},{4,0},{5,1},{6,2},{7,3},{8,12},{9,13},{10,... | collective-permute-start | bytes 552968 | tf_op jit(solution)/shard_map/ppermute | solution.py:304
  324.2 16.4 %collective-permute-start.47 = (bf16[24,3840]{1,0:T(8,128)(2,1)}, bf16[24,3840]{1,0:T(8,128)(2,1)}, u32[]{:S(2)}, u32[]{:S(2)}) collective-permute-start(bf16[24,3840]{1,0:T(8,128)(2,1)} %pad_maximum_fusion.11), channel_id=1, source_target_pairs={{0,2},{1,3},{2,0},{3,1},{4,6},{5,7},{6,4},{7,5},{8,10},{9,11},{10,... | collective-permute-start | bytes 552968 | tf_op jit(solution)/shard_map/ppermute | solution.py:304
  327.1 13.5 %collective-permute-start.48 = (bf16[24,3840]{1,0:T(8,128)(2,1)}, bf16[24,3840]{1,0:T(8,128)(2,1)}, u32[]{:S(2)}, u32[]{:S(2)}) collective-permute-start(bf16[24,3840]{1,0:T(8,128)(2,1)} %pad_maximum_fusion.12), channel_id=1, source_target_pairs={{0,6},{1,7},{2,4},{3,5},{4,2},{5,3},{6,0},{7,1},{8,14},{9,15},{10,... | collective-permute-start | bytes 552968 | tf_op jit(solution)/shard_map/ppermute | solution.py:304
  331.6 17.9 %collective-permute-start.36 = (bf16[2,2,24,1152]{3,2,1,0:T(8,128)(2,1)}, bf16[2,2,24,1152]{3,2,1,0:T(8,128)(2,1)S(1)}, u32[]{:S(2)}, u32[]{:S(2)}) collective-permute-start(bf16[2,2,24,1152]{3,2,1,0:T(8,128)(2,1)} %get-tuple-element.226), channel_id=1, source_target_pairs={{0,16},{1,17},{2,18},{3,19},{4,20},{5,21},{6,22},{7,23},{16,0},{17... | collective-permute-start | bytes 663560 | tf_op jit(solution)/shard_map/ppermute | solution.py:306
  333.2 17.1 %collective-permute-start.37 = (bf16[2,2,24,1152]{3,2,1,0:T(8,128)(2,1)}, bf16[2,2,24,1152]{3,2,1,0:T(8,128)(2,1)S(1)}, u32[]{:S(2)}, u32[]{:S(2)}) collective-permute-start(bf16[2,2,24,1152]{3,2,1,0:T(8,128)(2,1)} %get-tuple-element.225), channel_id=1, source_target_pairs={{0,1},{1,0},{2,3},{3,2},{4,5},{5,4},{6,7},{7,6},{16,17},{17,16},{1... | collective-permute-start | bytes 663560 | tf_op jit(solution)/shard_map/ppermute | solution.py:306
  336.2 15.3 %collective-permute-start.38 = (bf16[2,2,24,1152]{3,2,1,0:T(8,128)(2,1)}, bf16[2,2,24,1152]{3,2,1,0:T(8,128)(2,1)S(1)}, u32[]{:S(2)}, u32[]{:S(2)}) collective-permute-start(bf16[2,2,24,1152]{3,2,1,0:T(8,128)(2,1)} %get-tuple-element.224), channel_id=1, source_target_pairs={{0,17},{1,16},{2,19},{3,18},{4,21},{5,20},{6,23},{7,22},{16,1},{17... | collective-permute-start | bytes 663560 | tf_op jit(solution)/shard_map/ppermute | solution.py:306
  340.6 41.4 %collective-permute-start.32 = (bf16[2,128,768]{2,1,0:T(8,128)(2,1)}, bf16[2,128,768]{2,1,0:T(8,128)(2,1)}, u32[]{:S(2)}, u32[]{:S(2)}) collective-permute-start(bf16[2,128,768]{2,1,0:T(8,128)(2,1)} %bitcast.329), channel_id=1, source_target_pairs={{0,24},{8,16},{16,8},{24,0},{1,25},{9,17},{17,9},{25,1},{2,26},{10... | collective-permute-start | bytes 1179656 | tf_op jit(solution)/shard_map/ppermute | solution.py:407
  340.6 7.3 %collective-permute-start.39 = (f32[2,2,2,2,24,128]{5,4,3,2,1,0:T(8,128)S(1)}, f32[2,2,2,2,24,128]{5,4,3,2,1,0:T(8,128)S(1)}, u32[]{:S(2)}, u32[]{:S(2)}) collective-permute-start(f32[2,2,2,2,24,128]{5,4,3,2,1,0:T(8,128)S(1)} %dynamic-slice_bitcast_fusion.7), channel_id=1, source_target_pairs={{0,8},{8,0},{1,9},{9,1},{2,10},{10,2},{3,11},{11,3},{4,12},{12,4},... | collective-permute-start | bytes 589832 | tf_op jit(solution)/shard_map/ppermute | solution.py:304
  347.9 34.1 %collective-permute-start.31 = (bf16[2,128,768]{2,1,0:T(8,128)(2,1)}, bf16[2,128,768]{2,1,0:T(8,128)(2,1)}, u32[]{:S(2)}, u32[]{:S(2)}) collective-permute-start(bf16[2,128,768]{2,1,0:T(8,128)(2,1)} %bitcast.98), channel_id=1, source_target_pairs={{0,16},{8,24},{16,0},{24,8},{1,17},{9,25},{17,1},{25,9},{2,18},{10... | collective-permute-start | bytes 1179656 | tf_op jit(solution)/shard_map/ppermute | solution.py:407
  349.6 13.6 %collective-permute-start.42 = (f32[2,2,24,128]{3,2,1,0:T(8,128)S(1)}, f32[2,2,24,128]{3,2,1,0:T(8,128)S(1)}, u32[]{:S(2)}, u32[]{:S(2)}) collective-permute-start(f32[2,2,24,128]{3,2,1,0:T(8,128)S(1)} %get-tuple-element.273), channel_id=1, source_target_pairs={{0,17},{1,16},{2,19},{3,18},{4,21},{5,20},{6,23},{7,22},{16,1},{17... | collective-permute-start | bytes 147464 | tf_op jit(solution)/shard_map/ppermute | solution.py:306
  350.3 12.9 %collective-permute-start.41 = (f32[2,2,24,128]{3,2,1,0:T(8,128)S(1)}, f32[2,2,24,128]{3,2,1,0:T(8,128)S(1)}, u32[]{:S(2)}, u32[]{:S(2)}) collective-permute-start(f32[2,2,24,128]{3,2,1,0:T(8,128)S(1)} %get-tuple-element.274), channel_id=1, source_target_pairs={{0,1},{1,0},{2,3},{3,2},{4,5},{5,4},{6,7},{7,6},{16,17},{17,16},{1... | collective-permute-start | bytes 147464 | tf_op jit(solution)/shard_map/ppermute | solution.py:306
  351.5 12.6 %collective-permute-start.40 = (f32[2,2,24,128]{3,2,1,0:T(8,128)S(1)}, f32[2,2,24,128]{3,2,1,0:T(8,128)S(1)}, u32[]{:S(2)}, u32[]{:S(2)}) collective-permute-start(f32[2,2,24,128]{3,2,1,0:T(8,128)S(1)} %get-tuple-element.272), channel_id=1, source_target_pairs={{0,16},{1,17},{2,18},{3,19},{4,20},{5,21},{6,22},{7,23},{16,0},{17... | collective-permute-start | bytes 147464 | tf_op jit(solution)/shard_map/ppermute | solution.py:306
  364.2 8.0 %collective-permute-start.45 = (bf16[24,2432]{1,0:T(8,128)(2,1)S(1)}, bf16[24,2432]{1,0:T(8,128)(2,1)S(1)}, u32[]{:S(2)}, u32[]{:S(2)}) collective-permute-start(bf16[24,2432]{1,0:T(8,128)(2,1)S(1)} %pad_maximum_fusion.15), channel_id=1, source_target_pairs={{0,6},{1,7},{2,4},{3,5},{4,2},{5,3},{6,0},{7,1},{8,14},{9,15},{10,... | collective-permute-start | bytes 350216 | tf_op jit(solution)/shard_map/ppermute | solution.py:304
  365.1 7.1 %collective-permute-start.44 = (bf16[24,2432]{1,0:T(8,128)(2,1)S(1)}, bf16[24,2432]{1,0:T(8,128)(2,1)S(1)}, u32[]{:S(2)}, u32[]{:S(2)}) collective-permute-start(bf16[24,2432]{1,0:T(8,128)(2,1)S(1)} %pad_maximum_fusion.14), channel_id=1, source_target_pairs={{0,2},{1,3},{2,0},{3,1},{4,6},{5,7},{6,4},{7,5},{8,10},{9,11},{10,... | collective-permute-start | bytes 350216 | tf_op jit(solution)/shard_map/ppermute | solution.py:304
  365.3 10.5 %collective-permute-start.43 = (bf16[24,2432]{1,0:T(8,128)(2,1)S(1)}, bf16[24,2432]{1,0:T(8,128)(2,1)S(1)}, u32[]{:S(2)}, u32[]{:S(2)}) collective-permute-start(bf16[24,2432]{1,0:T(8,128)(2,1)S(1)} %pad_maximum_fusion.13), channel_id=1, source_target_pairs={{0,4},{1,5},{2,6},{3,7},{4,0},{5,1},{6,2},{7,3},{8,12},{9,13},{10,... | collective-permute-start | bytes 350216 | tf_op jit(solution)/shard_map/ppermute | solution.py:304
  372.2 9.8 %collective-permute-start.30 = (bf16[2,128,768]{2,1,0:T(8,128)(2,1)S(1)}, bf16[2,128,768]{2,1,0:T(8,128)(2,1)S(1)}, u32[]{:S(2)}, u32[]{:S(2)}) collective-permute-start(bf16[2,128,768]{2,1,0:T(8,128)(2,1)S(1)} %bitcast.328), channel_id=1, source_target_pairs={{0,8},{8,0},{16,24},{24,16},{1,9},{9,1},{17,25},{25,17},{2,10},{10... | collective-permute-start | bytes 1179656 | tf_op jit(solution)/shard_map/ppermute | solution.py:407
  (64 other events, 567.2 us)
Sparse Core Ops, SparseCore 0:
  13.0 106.5 all-gather.2
  207.2 111.0 reduce-scatter.1
